TPU v7x, 512 devices: a whole 4x4x16 slice. The times are simulated.
512 devices in a mesh: bx: 16 (over z), by: 32 (over x, y, core).
Axes of the slice: x: 4, y: 4, z: 16, core: 2. Of those that a mesh axis runs over, the one named last changes fastest.
Arguments:
- rhs: float32 [32, 64, 256, 384], P('bx', 'by'), may hold values from -6 to 6
- perm1: int32 [32, 64, 256], P('bx', 'by'), may hold values from 0 to 255, each once within a row
- interp1: bfloat16 [32, 64, 160, 96], P('bx', 'by'), may hold values from -0.5 to 0.5
- pivinv1: bfloat16 [32, 64, 160, 160], P('bx', 'by'), may hold values from -0.5 to 0.5
- couple1: bfloat16 [32, 64, 8, 96, 160], P('bx', 'by'), may hold values from -0.15625 to 0.15625
- perm2: int32 [16, 32, 384], P('bx', 'by'), may hold values from 0 to 383, each once within a row
- interp2: bfloat16 [16, 32, 256, 128], P('bx', 'by'), may hold values from -0.375 to 0.375
- pivinv2: bfloat16 [16, 32, 256, 256], P('bx', 'by'), may hold values from -0.375 to 0.375
- couple2: bfloat16 [16, 32, 8, 128, 256], P('bx', 'by'), may hold values from -0.125 to 0.125
Outputs:
- red1: bfloat16 [32, 64, 160, 384], P('bx', 'by')
- red2: bfloat16 [16, 32, 256, 384], P('bx', 'by')
- skel2: float32 [16, 32, 128, 384], P('bx', 'by')
Inputs may be any that keep to these rules, and one draw needn't show every extreme that they name: Each row of perm1 holds every point index once. Each row of perm2 holds every point index once.
All inputs are finite; a program needn't handle non-finite values.
Results may differ from a plain program's by a relative error of at most 0.013.
Values may be sent and summed in bfloat16 or wider, within the bound.
No kernel may reach another device: no remote copies, remote signals or barrier semaphores. Data moves between devices by JAX's collectives and lax.ppermute only.
A program may use at most 64 MiB of HBM per device.

v0:
```python
import functools

import jax
import jax.numpy as jnp
from jax import lax
from jax.experimental import pallas as pl
from jax.experimental.pallas import tpu as pltpu
from jax.sharding import PartitionSpec as P


S1, R1, P1 = 96, 160, 256
S2, R2, P2 = 128, 256, 384
K = 384
OFFSETS = [(-1, -1), (-1, 0), (-1, 1), (0, -1), (0, 1), (1, -1), (1, 0), (1, 1)]
BOXES = [(0, 0), (0, 1), (1, 0), (1, 1)]
F32, BF16 = jnp.float32, jnp.bfloat16
LEAF_S, LEAF_R, LEAF_Z = ((S1, K), F32), ((R1, K), F32), ((R1, K), BF16)
LEAF_W, LEAF_M = ((5, R1, S1), BF16), ((2 * S1, K), BF16)
PAR_S, PAR_R, PAR_Z, PAR_M = ((S2, K), F32), ((R2, K), F32), ((R2, K), BF16), ((S2, K), BF16)


UP_TERMS = [((1, 0), (6, 7), (0, 1)), ((1, 1), (5, 6, 7), (0, 1, 2))]
DOWN_TERMS = [((0, 0), (1, 2), (0, 1)), ((0, 1), (0, 1, 2), (0, 1, 2))]

PACKS = {
    (1, 1): (6, 2, (0, 1)),
    (1, -1): (5, 1, (1,)),
    (1, 0): (5, 3, (0, 1, 2)),
    (-1, 1): (1, 2, (0, 1)),
    (-1, -1): (0, 1, (1,)),
    (-1, 0): (0, 3, (0, 1, 2)),
}
CORNERS = [(-1, -1), (-1, 1), (1, -1), (1, 1)]
ENDS = [(-1, 0), (1, 0)]


def dot(a, b):
    return lax.dot_general(a, b, (((1,), (0,)), ((), ())), preferred_element_type=F32)


def dot_t(a, b):
    return lax.dot_general(a, b, (((0,), (0,)), ((), ())), preferred_element_type=F32)


def source(box, k):
    row, col = box[0] + OFFSETS[k][0], box[1] + OFFSETS[k][1]
    return (row % 2) * 2 + col % 2, (row // 2, col // 2)


def reordered(x, perm, rows):
    pick = (lax.broadcasted_iota(jnp.int32, (rows, rows), 0) == perm).astype(F32).astype(BF16)
    high = x.astype(BF16)
    low = (x - high.astype(F32)).astype(BF16)
    return dot_t(pick, high) + dot_t(pick, low)


SMEM, VMEM, ANY, HBM = (pl.BlockSpec(memory_space=s) for s in (pltpu.SMEM, pltpu.VMEM, pl.ANY, pltpu.HBM))


def call(body, ins, outs, specs=(), scratch=()):
    specs = list(specs) + [VMEM] * (len(ins) - len(specs))
    return pl.pallas_call(
        body,
        out_shape=[jax.ShapeDtypeStruct(s, d) for s, d in outs],
        in_specs=specs,
        out_specs=[VMEM] * len(outs),
        scratch_shapes=list(scratch),
        compiler_params=pltpu.CompilerParams(vmem_limit_bytes=20 * 1024 * 1024),
        cost_estimate=pl.CostEstimate(flops=300_000_000, bytes_accessed=2_000_000, transcendentals=0),
    )(*ins)


def pairs(dx, dy, colours):
    nx, ny = lax.axis_size("bx"), lax.axis_size("by")
    out = []
    for i in range(nx):
        for j in range(ny):
            if (i % 2) * 2 + j % 2 in colours and 0 <= i + dx < nx and 0 <= j + dy < ny:
                out.append((i * ny + j, (i + dx) * ny + j + dy))
    return out


def shift(x, to, colours=(0, 1, 2, 3)):
    return lax.ppermute(x, ("bx", "by"), pairs(*to, colours))


def after(x, value):
    return lax.optimization_barrier((x, value))


def first_body(rhs, perm, interp, piv, couple, top, z_out, skel_out, up_out, down_out, *rest):
    packs, (x, p, t, v, sems) = rest[:6], rest[6:]
    jobs = [(rhs.at[0, 0], x), (perm, p), (interp.at[0, 0], t), (piv.at[0, 0], v)]
    for terms, out in ((UP_TERMS, up_out), (DOWN_TERMS, down_out)):
        at = 0
        for (i, j), ks, _ in terms:
            jobs.append((couple.at[i, j, pl.ds(ks[0], len(ks))], out.at[pl.ds(at, len(ks))]))
            at += len(ks)
    for (k, n, _), out in zip(PACKS.values(), packs):
        jobs.append((top.at[0, 0, pl.ds(k, n)], out))
    copies = [pltpu.make_async_copy(a, b, sems.at[n]) for n, (a, b) in enumerate(jobs)]
    for c in copies:
        c.start()
    for c in copies[:4]:
        c.wait()
    leaf = reordered(x[...], p[0, 0:1, :], P1)
    skel = leaf[:S1]
    diff = leaf[S1:] - dot(t[...], skel.astype(BF16))
    z_out[...] = dot(v[...], diff.astype(BF16)).astype(BF16)
    skel_out[...] = skel
    for c in copies[4:]:
        c.wait()


def spread_body(rhs, perm, interp, couple, z, skel0, s0, s1, s2, s3, r1, r2, r3):
    zc = z[...]
    s0[...] = skel0[...] - dot_t(interp[0, 0], zc)
    for n, (s, r) in ((1, (s1, r1)), (2, (s2, r2)), (3, (s3, r3))):
        i, j = BOXES[n]
        leaf = reordered(rhs[i, j], perm[i, j : j + 1, :], P1)
        r[...] = leaf[S1:]
        acc = leaf[:S1]
        for k in range(8):
            if source((i, j), k) == (0, (0, 0)):
                acc = acc - dot_t(couple[i, j, k], zc)
        s[...] = acc


def solve_body(n_ties, box, ks, part, terms, *rest):
    interp, piv, couple, skel, red, *rest = rest[n_ties:]
    zs, rest = rest[: len(ks)], rest[len(ks) :]
    i, j = box
    acc = skel[...]
    if part is not None:
        acc = acc - rest[0][part * S1 : (part + 1) * S1].astype(F32)
        rest = rest[1:]
    for k, z in zip(ks, zs):
        acc = acc - dot_t(couple[i, j, k], z[...])
    diff = red[...] - dot(interp[i, j], acc.astype(BF16))
    z = dot(piv[i, j], diff.astype(BF16)).astype(BF16)
    if terms is None:
        z_out, skel_out = rest
    else:
        left, right, mats, z_out, skel_out, sum_out = rest
        values, at = (left[...], z, right[...]), 0
        for n, (_, ks, which) in enumerate(terms):
            total = None
            for w in which:
                term = dot_t(mats[at], values[w])
                total = term if total is None else total + term
                at += 1
            sum_out[n * S1 : (n + 1) * S1] = total.astype(BF16)
    z_out[...] = z
    skel_out[...] = acc


def update_body(own, jobs, n_z, part, interp, couple, *refs):
    zs, skels, rest = refs[:n_z], refs[n_z : n_z + 4], refs[n_z + 4 :]
    if part is not None:
        arrived, rest = rest[0], rest[1:]
    for n in range(4):
        i, j = BOXES[n]
        acc = skels[n][...]
        if n == own:
            acc = acc - dot_t(interp[i, j], zs[0][...])
        if part == n:
            acc = acc - arrived[S1 : 2 * S1].astype(F32)
        for k, at in jobs[n]:
            acc = acc - dot_t(couple[i, j, k], zs[at][...])
        rest[n][...] = acc


def jobs_of(order, drop=()):
    jobs = [[], [], [], []]
    for n in range(4):
        for k in range(8):
            where = source(BOXES[n], k)
            if where in order and (n, where) not in drop:
                jobs[n].append((k, order.index(where)))
    return jobs


def work(rhs, perm1, interp1, pivinv1, couple1, perm2, interp2, pivinv2, couple2):
    couple1 = couple1.swapaxes(3, 4)
    have = {}
    here = (0, 0)

    def solve(colour, keys, skels, reds, arrived=None, part=None, terms=None, extra=(), ties=()):
        box = BOXES[colour]
        ks, zs = [], []
        for k in range(8):
            if source(box, k) in keys:
                ks.append(k)
                zs.append(have[source(box, k)])
        ins = [interp1, pivinv1, couple1, skels[colour], reds[colour], *zs]
        if arrived is not None:
            ins.append(arrived)
        outs = [LEAF_Z, LEAF_S] + ([LEAF_M] if terms else [])
        body = functools.partial(solve_body, len(ties), box, ks, part, terms)
        out = call(body, [*ties, *ins, *extra], outs, specs=[ANY] * len(ties))
        have[(colour, here)] = out[0]
        skels = list(skels)
        skels[colour] = out[1]
        return out[0], skels, out[2:]

    def update(own, keys, skels, drop=(), arrived=None, part=None):
        order = [(own, here), *keys]
        ins = [interp1, couple1, *[have[key] for key in order], *skels] + ([arrived] if arrived is not None else [])
        body = functools.partial(update_body, own, jobs_of(order, drop), len(order), part)
        return call(body, ins, [LEAF_S] * 4)

    dma = pltpu.SemaphoreType.DMA((4 + 4 + 6,))
    z00, skel0, up_pack, down_pack, *packs = call(
        first_body,
        [pltpu.with_memory_space_constraint(x, pltpu.HBM) for x in (rhs, perm1, interp1, pivinv1, couple1, couple2)],
        [LEAF_Z, LEAF_S, LEAF_W, LEAF_W] + [((n, S2, R2), BF16) for _, n, _ in PACKS.values()],
        specs=[HBM] * 6,
        scratch=[
            pltpu.VMEM((P1, K), F32),
            pltpu.VMEM((2, 2, P1), jnp.int32),
            pltpu.VMEM((R1, S1), BF16),
            pltpu.VMEM((R1, R1), BF16),
            dma,
        ],
    )
    packs = dict(zip(PACKS, packs))
    have[(0, here)] = z00
    have[(0, (0, 1))] = shift(z00, (0, -1))
    up_mats = shift(up_pack, (1, 0))
    down_mats = shift(down_pack, (-1, 0))
    s0, s1, s2, s3, r1, r2, r3 = call(
        spread_body, [rhs, perm1, interp1, couple1, z00, skel0], [LEAF_S] * 4 + [LEAF_R] * 3
    )
    reds = [None, r1, r2, r3]
    z01, skels, (up_sum,) = solve(
        1, {(0, (0, 1))}, [s0, s1, s2, s3], reds, terms=UP_TERMS, extra=(z00, have[(0, (0, 1))], up_mats), ties=(down_mats,)
    )
    from_below = shift(up_sum, (-1, 0))
    have[(1, (1, -1))] = shift(z01, (-1, 1))
    have[(1, (0, -1))] = shift(z01, (0, 1))
    mats = {}

    def fetch(dx, value):
        (ready, value) = after([packs[to] for to in PACKS if to[0] == dx], value)
        for to, pack in zip([to for to in PACKS if to[0] == dx], ready):
            mats[(-to[0], -to[1])] = shift(pack, to, (1, 3) if to[1] == 0 else (0, 2))
        return value, [mats[(-to[0], -to[1])] for to in PACKS if to[0] == dx]

    z01, fetched = fetch(1, z01)
    have[(1, here)] = z01
    skels = update(1, [(0, (0, 1))], skels, drop=[(1, (0, (0, 1)))])
    z10, skels, _ = solve(2, {(1, (0, -1)), (1, (1, -1))}, skels, reds, arrived=from_below, part=0, ties=fetched)
    have[(2, (0, 1))] = shift(z10, (0, -1))
    z10, fetched = fetch(-1, z10)
    have[(2, here)] = z10
    skels = update(2, [(1, (0, -1))], skels, drop=[(2, (1, (0, -1)))], arrived=from_below, part=3)
    z11, skels, (down_sum,) = solve(
        3, {(2, (0, 1))}, skels, reds, terms=DOWN_TERMS, extra=(z10, have[(2, (0, 1))], down_mats), ties=fetched
    )
    from_above = shift(down_sum, (1, 0))
    have[(3, (-1, -1))] = shift(z11, (1, 1))
    have[(3, (0, -1))] = shift(z11, (0, 1))
    skels = update(3, [(2, (0, 1))], skels, drop=[(3, (2, (0, 1)))])
    red1 = jnp.stack([z00, z01, z10, z11]).reshape(2, 2, R1, K)

    colour = ((lax.axis_index("bx") % 2) * 2 + lax.axis_index("by") % 2).astype(jnp.int32).reshape(1)
    last = [(3, (0, -1)), (3, (-1, -1))]
    last_jobs = jobs_of(last)

    def solve_parent(interp, piv, skel, red):
        diff = red - dot(interp[0, 0], skel.astype(BF16))
        return dot(piv[0, 0], diff.astype(BF16)).astype(BF16)

    def join_body(me, perm, interp, piv, couple, za, zb, arrived, ca, cb, cc, cd, skel_out, red_out, z_out):
        zs = [za, zb]
        parts = []
        for n, c in enumerate((ca, cb, cc, cd)):
            acc = c[...]
            if n < 2:
                acc = acc - arrived[n * S1 : (n + 1) * S1].astype(F32)
            for k, at in last_jobs[n]:
                acc = acc - dot_t(couple[BOXES[n][0], BOXES[n][1], k], zs[at][...])
            parts.append(acc)
        parent = reordered(jnp.concatenate(parts, axis=0), perm[0], P2)
        skel_out[...] = parent[:S2]
        red_out[...] = parent[S2:]

        @pl.when(me[0] == 0)
        def _():
            z_out[...] = solve_parent(interp, piv, parent[:S2], parent[S2:])

    skel, red, z0 = call(
        join_body,
        [colour, perm2, interp2, pivinv2, couple1, *[have[key] for key in last], from_above, *skels],
        [PAR_S, PAR_R, PAR_Z],
        specs=[SMEM],
    )

    def sides(z, c):
        return shift(z, (0, 1), (c,)), shift(z, (0, -1), (c,))

    def odd_body(c, me, interp, piv, couple, skel, red, zl, zr, *rest):
        if c == 3:
            arrived, rest = rest[:2], rest[2:]
        ws, (z_out, skel_out), sums = rest[:6], rest[6:8], rest[8:]

        @pl.when(me[0] != c)
        def _():
            skel_out[...] = skel[...]

        @pl.when(me[0] == c)
        def _():
            acc = skel[...]
            if c == 3:
                acc = acc - arrived[0][...].astype(F32) - arrived[1][...].astype(F32)
            acc = acc - (dot(couple[0, 0, 3], zl[...]) + dot(couple[0, 0, 4], zr[...]))
            skel_out[...] = acc
            z = solve_parent(interp, piv, acc, red[...])
            z_out[...] = z
            values = (zl[...], z, zr[...])
            for (_, _, which), w, out in zip(PACKS.values(), ws, sums):
                total = None
                for n, v in enumerate(which):
                    term = dot(w[n], values[v])
                    total = term if total is None else total + term
                out[...] = total.astype(BF16)

    def odd(c, skel, zl, zr, arrived=()):
        ws = [mats[(-dx, -dy)] for dx, dy in PACKS]
        z, skel, *sums = call(
            functools.partial(odd_body, c),
            [colour, interp2, pivinv2, couple2, skel, red, zl, zr, *arrived, *ws],
            [PAR_Z, PAR_S] + [PAR_M] * 6,
            specs=[SMEM],
        )
        got = {}
        for way in CORNERS + ENDS:
            got[way] = shift(sums[list(PACKS).index((-way[0], -way[1]))], way, (c,))
        return z, skel, got

    def even_body(me, interp, piv, skel, red, a, b, c, d, z_out, skel_out):
        @pl.when(me[0] != 2)
        def _():
            skel_out[...] = skel[...]

        @pl.when(me[0] == 2)
        def _():
            acc = skel[...] - (a[...].astype(F32) + b[...].astype(F32) + c[...].astype(F32) + d[...].astype(F32))
            skel_out[...] = acc
            z_out[...] = solve_parent(interp, piv, acc, red[...])

    zl, zr = sides(z0, 0)
    z1, skel, got1 = odd(1, skel, zl, zr)
    side1 = sides(z1, 1)
    z2, skel = call(
        even_body, [colour, interp2, pivinv2, skel, red, *[got1[way] for way in CORNERS]], [PAR_Z, PAR_S], specs=[SMEM]
    )
    zl, zr = sides(z2, 2)
    z3, skel, got3 = odd(3, skel, zl, zr, [got1[way] for way in ENDS])
    side3 = sides(z3, 3)

    def early_body(me, interp, couple, skel, z0, z1, z2, z3, xl, xr, skel_out, z_out):
        for c, own in enumerate((z0, z1, z2, z3)):

            @pl.when(me[0] == c)
            def _():
                zc = own[...]
                z_out[...] = zc
                acc = skel[...] - dot_t(interp[0, 0], zc)
                if c == 0:
                    acc = acc - (dot(couple[0, 0, 3], xl[...]) + dot(couple[0, 0, 4], xr[...]))
                skel_out[...] = acc

    skel, red2 = call(
        early_body, [colour, interp2, couple2, skel, z0, z1, z2, z3, *side1], [PAR_S, PAR_Z], specs=[SMEM]
    )

    def late_body(me, couple, skel, a, b, c, d, e, f, xl, xr, skel_out):
        @pl.when(me[0] == 0)
        def _():
            skel_out[...] = skel[...] - (
                a[...].astype(F32) + b[...].astype(F32) + c[...].astype(F32) + d[...].astype(F32)
            )

        @pl.when(me[0] == 1)
        def _():
            skel_out[...] = skel[...] - (e[...].astype(F32) + f[...].astype(F32))

        @pl.when(me[0] == 2)
        def _():
            skel_out[...] = skel[...] - (dot(couple[0, 0, 3], xl[...]) + dot(couple[0, 0, 4], xr[...]))

        @pl.when(me[0] == 3)
        def _():
            skel_out[...] = skel[...]

    (skel2,) = call(
        late_body, [colour, couple2, skel, *[got3[way] for way in CORNERS + ENDS], *side3], [PAR_S], specs=[SMEM]
    )
    return (red1, red2[None, None], skel2[None, None])


def solution(mesh):
    in_specs = (
        P("bx", "by", None, None),
        P("bx", "by", None),
        P("bx", "by", None, None),
        P("bx", "by", None, None),
        P("bx", "by", None, None, None),
        P("bx", "by", None),
        P("bx", "by", None, None),
        P("bx", "by", None, None),
        P("bx", "by", None, None, None),
    )
    out_specs = (P("bx", "by", None, None), P("bx", "by", None, None), P("bx", "by", None, None))
    return jax.shard_map(work, mesh=mesh, in_specs=in_specs, out_specs=out_specs, check_vma=False)
```

profile of v0, /device:TPU:83, one launch (start us, length us, event | category | flops | bytes accessed | tf_op | source)
XLA Modules:
  0.0 114.7 jit_solution(14780391541041467556)
XLA Ops:
  0.7 2.0 %shard_map.112 = (bf16[160,384]{1,0:T(8,128)(2,1)S(1)}, f32[96,384]{1,0:T(8,128)S(1)}, bf16[5,160,96]{2,1,0:T(8,128)(2,1)S(1)}, bf16[5,160,96]{2,1,0:T(8,128)(2,...) custom-call(f32[2,2,256,384]{3,2,1,0:T(8,128)} %rhs.3, ...), custom_call_target="tpu_custom_call" | custom-call | flops 300000000 | bytes 2000000 | tf_op jit(solution)/shard_map/pallas_call | solution.py:62
  2.6 1.9 %collective-permute-start = (bf16[5,160,96]{2,1,0:T(8,128)(2,1)S(1)}, bf16[5,160,96]{2,1,0:T(8,128)(2,1)S(1)}, u32[]{:S(2)}, u32[]{:S(2)}) collective-permute-start(bf16[5,160,96]{2,1,0:T(8,128)(2,1)S(1)} %get-tuple-element.75), channel_id=1, source_target_pairs={{32,0},{33,1},{34,2},{35,3},{36,4},{37,5},{38,6},{39,7},{40,8},{41... | collective-permute-start | bytes 460808 | tf_op jit(solution)/shard_map/ppermute | solution.py:84
  4.6 3.5 %collective-permute-start.2 = (bf16[5,160,96]{2,1,0:T(8,128)(2,1)S(1)}, bf16[5,160,96]{2,1,0:T(8,128)(2,1)S(1)}, u32[]{:S(2)}, u32[]{:S(2)}) collective-permute-start(bf16[5,160,96]{2,1,0:T(8,128)(2,1)S(1)} %get-tuple-element.79), channel_id=1, source_target_pairs={{0,32},{1,33},{2,34},{3,35},{4,36},{5,37},{6,38},{7,39},{8,40},{9,... | collective-permute-start | bytes 460808 | tf_op jit(solution)/shard_map/ppermute | solution.py:84
  8.1 3.0 %collective-permute-start.1 = (bf16[160,384]{1,0:T(8,128)(2,1)S(1)}, bf16[160,384]{1,0:T(8,128)(2,1)S(1)}, u32[]{:S(2)}, u32[]{:S(2)}) collective-permute-start(bf16[160,384]{1,0:T(8,128)(2,1)S(1)} %get-tuple-element.71.z.rest_7_), channel_id=1, source_target_pairs={{1,0},{2,1},{3,2},{4,3},{5,4},{6,5},{7,6},{8,7},{9,8},{10,9},{11,1... | collective-permute-start | bytes 368648 | tf_op jit(solution)/shard_map/ppermute | solution.py:84
  11.9 2.6 %collective-permute-done.1.rest_6_.rest_8_.refs_1_ = bf16[160,384]{1,0:T(8,128)(2,1)S(1)} collective-permute-done((bf16[160,384]{1,0:T(8,128)(2,1)S(1)}, bf16[160,384]{1,0:T(8,128)(2,1)S(1)}, u32[]{:S(2)}, u32[]{:S(2)}) %collective-permute-start.1) | collective-permute-done | bytes 122912 | tf_op jit(solution)/shard_map/ppermute | solution.py:84
  15.3 4.8 %collective-permute-start.5 = (bf16[3,128,256]{2,1,0:T(8,128)(2,1)S(1)}, bf16[3,128,256]{2,1,0:T(8,128)(2,1)S(1)}, u32[]{:S(2)}, u32[]{:S(2)}) collective-permute-start(bf16[3,128,256]{2,1,0:T(8,128)(2,1)S(1)} %get-tuple-element.87), channel_id=1, source_target_pairs={{1,33},{3,35},{5,37},{7,39},{9,41},{11,43},{13,45},{15,47},{17,49}... | collective-permute-start | bytes 589832 | tf_op jit(solution)/shard_map/ppermute | solution.py:84
  20.1 1.3 %collective-permute-start.4 = (bf16[1,128,256]{2,1,0:T(8,128)(2,1)S(1)}, bf16[1,128,256]{2,1,0:T(8,128)(2,1)S(1)}, u32[]{:S(2)}, u32[]{:S(2)}) collective-permute-start(bf16[1,128,256]{2,1,0:T(8,128)(2,1)S(1)} %get-tuple-element.86), channel_id=1, source_target_pairs={{2,33},{4,35},{6,37},{8,39},{10,41},{12,43},{14,45},{16,47},{18,49... | collective-permute-start | bytes 196616 | tf_op jit(solution)/shard_map/ppermute | solution.py:84
  21.4 1.9 %collective-permute-start.8 = (bf16[192,384]{1,0:T(8,128)(2,1)S(1)}, bf16[192,384]{1,0:T(8,128)(2,1)S(1)}, u32[]{:S(2)}, u32[]{:S(2)}) collective-permute-start(bf16[192,384]{1,0:T(8,128)(2,1)S(1)} %get-tuple-element.94), channel_id=1, source_target_pairs={{32,0},{33,1},{34,2},{35,3},{36,4},{37,5},{38,6},{39,7},{40,8},{41... | collective-permute-start | bytes 442376 | tf_op jit(solution)/shard_map/ppermute | solution.py:84
  23.3 1.3 %collective-permute-start.3 = (bf16[2,128,256]{2,1,0:T(8,128)(2,1)S(1)}, bf16[2,128,256]{2,1,0:T(8,128)(2,1)S(1)}, u32[]{:S(2)}, u32[]{:S(2)}) collective-permute-start(bf16[2,128,256]{2,1,0:T(8,128)(2,1)S(1)} %get-tuple-element.85), channel_id=1, source_target_pairs={{0,33},{2,35},{4,37},{6,39},{8,41},{10,43},{12,45},{14,47},{16,49}... | collective-permute-start | bytes 393224 | tf_op jit(solution)/shard_map/ppermute | solution.py:84
  24.6 6.9 %collective-permute-start.7 = (bf16[160,384]{1,0:T(8,128)(2,1)S(1)}, bf16[160,384]{1,0:T(8,128)(2,1)S(1)}, u32[]{:S(2)}, u32[]{:S(2)}) collective-permute-start(bf16[160,384]{1,0:T(8,128)(2,1)S(1)} %get-tuple-element.81.refs_0_), channel_id=1, source_target_pairs={{32,1},{33,2},{34,3},{35,4},{36,5},{37,6},{38,7},{39,8},{40,9},{41... | collective-permute-start | bytes 368648 | tf_op jit(solution)/shard_map/ppermute | solution.py:84
  31.6 2.4 %collective-permute-start.6 = (bf16[160,384]{1,0:T(8,128)(2,1)S(1)}, bf16[160,384]{1,0:T(8,128)(2,1)S(1)}, u32[]{:S(2)}, u32[]{:S(2)}) collective-permute-start(bf16[160,384]{1,0:T(8,128)(2,1)S(1)} %get-tuple-element.81.refs_0_), channel_id=1, source_target_pairs={{0,1},{1,2},{2,3},{3,4},{4,5},{5,6},{6,7},{7,8},{8,9},{9,10},{10,1... | collective-permute-start | bytes 368648 | tf_op jit(solution)/shard_map/ppermute | solution.py:84
  37.1 1.9 %collective-permute-start.11 = (bf16[3,128,256]{2,1,0:T(8,128)(2,1)S(1)}, bf16[3,128,256]{2,1,0:T(8,128)(2,1)S(1)}, u32[]{:S(2)}, u32[]{:S(2)}) collective-permute-start(bf16[3,128,256]{2,1,0:T(8,128)(2,1)S(1)} %get-tuple-element.99), channel_id=1, source_target_pairs={{33,1},{35,3},{37,5},{39,7},{41,9},{43,11},{45,13},{47,15},{49,17}... | collective-permute-start | bytes 589832 | tf_op jit(solution)/shard_map/ppermute | solution.py:84
  39.0 1.3 %collective-permute-start.9 = (bf16[2,128,256]{2,1,0:T(8,128)(2,1)S(1)}, bf16[2,128,256]{2,1,0:T(8,128)(2,1)S(1)}, u32[]{:S(2)}, u32[]{:S(2)}) collective-permute-start(bf16[2,128,256]{2,1,0:T(8,128)(2,1)S(1)} %get-tuple-element.97), channel_id=1, source_target_pairs={{32,1},{34,3},{36,5},{38,7},{40,9},{42,11},{44,13},{46,15},{48,17}... | collective-permute-start | bytes 393224 | tf_op jit(solution)/shard_map/ppermute | solution.py:84
  40.3 2.3 %collective-permute-start.12 = (bf16[160,384]{1,0:T(8,128)(2,1)S(1)}, bf16[160,384]{1,0:T(8,128)(2,1)S(1)}, u32[]{:S(2)}, u32[]{:S(2)}) collective-permute-start(bf16[160,384]{1,0:T(8,128)(2,1)S(1)} %get-tuple-element.96.refs_0_.rest_9_), channel_id=1, source_target_pairs={{1,0},{2,1},{3,2},{4,3},{5,4},{6,5},{7,6},{8,7},{9,8},{10,9},{11,1... | collective-permute-start | bytes 368648 | tf_op jit(solution)/shard_map/ppermute | solution.py:84
  42.6 1.3 %collective-permute-start.10 = (bf16[1,128,256]{2,1,0:T(8,128)(2,1)S(1)}, bf16[1,128,256]{2,1,0:T(8,128)(2,1)S(1)}, u32[]{:S(2)}, u32[]{:S(2)}) collective-permute-start(bf16[1,128,256]{2,1,0:T(8,128)(2,1)S(1)} %get-tuple-element.98), channel_id=1, source_target_pairs={{34,1},{36,3},{38,5},{40,7},{42,9},{44,11},{46,13},{48,15},{50,17}... | collective-permute-start | bytes 196616 | tf_op jit(solution)/shard_map/ppermute | solution.py:84
  44.2 6.2 %collective-permute-done.10.rest_1_.rest_4_.rest_6_ = bf16[1,128,256]{2,1,0:T(8,128)(2,1)S(1)} collective-permute-done((bf16[1,128,256]{2,1,0:T(8,128)(2,1)S(1)}, bf16[1,128,256]{2,1,0:T(8,128)(2,1)S(1)}, u32[]{:S(2)}, u32[]{:S(2)}) %collective-permute-start.10) | collective-permute-done | bytes 65568 | tf_op jit(solution)/shard_map/ppermute | solution.py:84
  50.5 1.5 %shard_map.118 = (bf16[160,384]{1,0:T(8,128)(2,1)S(1)}, f32[96,384]{1,0:T(8,128)S(1)}, bf16[192,384]{1,0:T(8,128)(2,1)}) custom-call(bf16[2,128,256]{2,1,0:T(8,128)(2,1)S(1)} %collective-permute-done.9.rest_0_.rest_3_.rest_5_, bf16[1,128,256]{2,1,0:T(8,128)(2,1)S(1)} %collective-permute-done.10.rest_1_.rest_4_.rest_6_, ...), custom_call_target="tpu_custom_call" | custom-call | flops 300000000 | bytes 2000000 | tf_op jit(solution)/shard_map/pallas_call | solution.py:62
  52.6 5.9 %collective-permute-start.15 = (bf16[192,384]{1,0:T(8,128)(2,1)}, bf16[192,384]{1,0:T(8,128)(2,1)}, u32[]{:S(2)}, u32[]{:S(2)}) collective-permute-start(bf16[192,384]{1,0:T(8,128)(2,1)} %get-tuple-element.107), channel_id=1, source_target_pairs={{0,32},{1,33},{2,34},{3,35},{4,36},{5,37},{6,38},{7,39},{8,40},{9,... | collective-permute-start | bytes 442376 | tf_op jit(solution)/shard_map/ppermute | solution.py:84
  58.6 2.2 %collective-permute-start.14 = (bf16[160,384]{1,0:T(8,128)(2,1)S(1)}, bf16[160,384]{1,0:T(8,128)(2,1)}, u32[]{:S(2)}, u32[]{:S(2)}) collective-permute-start(bf16[160,384]{1,0:T(8,128)(2,1)S(1)} %get-tuple-element.106.refs_0_), channel_id=1, source_target_pairs={{0,33},{1,34},{2,35},{3,36},{4,37},{5,38},{6,39},{7,40},{8,41},{9,... | collective-permute-start | bytes 368648 | tf_op jit(solution)/shard_map/ppermute | solution.py:84
  60.7 7.7 %collective-permute-start.13 = (bf16[160,384]{1,0:T(8,128)(2,1)S(1)}, bf16[160,384]{1,0:T(8,128)(2,1)}, u32[]{:S(2)}, u32[]{:S(2)}) collective-permute-start(bf16[160,384]{1,0:T(8,128)(2,1)S(1)} %get-tuple-element.106.refs_0_), channel_id=1, source_target_pairs={{0,1},{1,2},{2,3},{3,4},{4,5},{5,6},{6,7},{7,8},{8,9},{9,10},{10,1... | collective-permute-start | bytes 368648 | tf_op jit(solution)/shard_map/ppermute | solution.py:84
  70.3 1.8 %shard_map.120 = (f32[128,384]{1,0:T(8,128)S(1)}, f32[256,384]{1,0:T(8,128)S(1)}, bf16[256,384]{1,0:T(8,128)(2,1)S(1)}) custom-call(s32[1]{0:T(128)} %bitcast.6.me, s32[1,1,384]{2,1,0:T(1,128)S(1)} %copy-done.10, bf16[1,1,256,128]{3,2,1,0:T(8,128)(2,1)S(1)} %copy-done.6, bf16[1,1,256,256]{3,2,1,0:T(8,128)(2,1)S(1)} %copy-done.5, ...), custom_call_target="tpu_custom_call" | custom-call | flops 300000000 | bytes 2000000 | tf_op jit(solution)/shard_map/pallas_call | solution.py:62
  74.7 5.0 %collective-permute-done.17.zr = bf16[256,384]{1,0:T(8,128)(2,1)S(1)} collective-permute-done((bf16[256,384]{1,0:T(8,128)(2,1)S(1)}, bf16[256,384]{1,0:T(8,128)(2,1)S(1)}, u32[]{:S(2)}, u32[]{:S(2)}) %collective-permute-start.17) | collective-permute-done | bytes 196640 | tf_op jit(solution)/shard_map/ppermute | solution.py:84
  80.9 1.3 %collective-permute-start.18 = (bf16[128,384]{1,0:T(8,128)(2,1)S(1)}, bf16[128,384]{1,0:T(8,128)(2,1)S(1)}, u32[]{:S(2)}, u32[]{:S(2)}) collective-permute-start(bf16[128,384]{1,0:T(8,128)(2,1)S(1)} %get-tuple-element.120), channel_id=1, source_target_pairs={{65,32},{67,34},{69,36},{71,38},{73,40},{75,42},{77,44},{79,46},{8... | collective-permute-start | bytes 294920 | tf_op jit(solution)/shard_map/ppermute | solution.py:84
  82.2 1.3 %collective-permute-start.19 = (bf16[128,384]{1,0:T(8,128)(2,1)S(1)}, bf16[128,384]{1,0:T(8,128)(2,1)S(1)}, u32[]{:S(2)}, u32[]{:S(2)}) collective-permute-start(bf16[128,384]{1,0:T(8,128)(2,1)S(1)} %get-tuple-element.121), channel_id=1, source_target_pairs={{65,34},{67,36},{69,38},{71,40},{73,42},{75,44},{77,46},{79,48},{8... | collective-permute-start | bytes 294920 | tf_op jit(solution)/shard_map/ppermute | solution.py:84
  83.5 1.3 %collective-permute-start.20 = (bf16[128,384]{1,0:T(8,128)(2,1)S(1)}, bf16[128,384]{1,0:T(8,128)(2,1)S(1)}, u32[]{:S(2)}, u32[]{:S(2)}) collective-permute-start(bf16[128,384]{1,0:T(8,128)(2,1)S(1)} %get-tuple-element.122), channel_id=1, source_target_pairs={{1,32},{3,34},{5,36},{7,38},{9,40},{11,42},{13,44},{15,46},{17,48}... | collective-permute-start | bytes 294920 | tf_op jit(solution)/shard_map/ppermute | solution.py:84
  84.8 1.3 %collective-permute-start.21 = (bf16[128,384]{1,0:T(8,128)(2,1)S(1)}, bf16[128,384]{1,0:T(8,128)(2,1)S(1)}, u32[]{:S(2)}, u32[]{:S(2)}) collective-permute-start(bf16[128,384]{1,0:T(8,128)(2,1)S(1)} %get-tuple-element.123), channel_id=1, source_target_pairs={{1,34},{3,36},{5,38},{7,40},{9,42},{11,44},{13,46},{15,48},{17,50}... | collective-permute-start | bytes 294920 | tf_op jit(solution)/shard_map/ppermute | solution.py:84
  86.1 1.3 %collective-permute-start.24 = (bf16[128,384]{1,0:T(8,128)(2,1)S(1)}, bf16[128,384]{1,0:T(8,128)(2,1)S(1)}, u32[]{:S(2)}, u32[]{:S(2)}) collective-permute-start(bf16[128,384]{1,0:T(8,128)(2,1)S(1)} %get-tuple-element.126), channel_id=1, source_target_pairs={{65,33},{67,35},{69,37},{71,39},{73,41},{75,43},{77,45},{79,47},{8... | collective-permute-start | bytes 294920 | tf_op jit(solution)/shard_map/ppermute | solution.py:84
  89.1 1.3 %collective-permute-start.27 = (bf16[256,384]{1,0:T(8,128)(2,1)S(1)}, bf16[256,384]{1,0:T(8,128)(2,1)S(1)}, u32[]{:S(2)}, u32[]{:S(2)}) collective-permute-start(bf16[256,384]{1,0:T(8,128)(2,1)S(1)} %get-tuple-element.129.z1), channel_id=1, source_target_pairs={{1,0},{3,2},{5,4},{7,6},{9,8},{11,10},{13,12},{15,14},{17,16},{19,... | collective-permute-start | bytes 589832 | tf_op jit(solution)/shard_map/ppermute | solution.py:84
  90.4 1.3 %collective-permute-start.26 = (bf16[256,384]{1,0:T(8,128)(2,1)S(1)}, bf16[256,384]{1,0:T(8,128)(2,1)S(1)}, u32[]{:S(2)}, u32[]{:S(2)}) collective-permute-start(bf16[256,384]{1,0:T(8,128)(2,1)S(1)} %get-tuple-element.129.z1), channel_id=1, source_target_pairs={{1,2},{3,4},{5,6},{7,8},{9,10},{11,12},{13,14},{15,16},{17,18},{19... | collective-permute-start | bytes 589832 | tf_op jit(solution)/shard_map/ppermute | solution.py:84
  91.7 1.7 %collective-permute-start.25 = (bf16[128,384]{1,0:T(8,128)(2,1)S(1)}, bf16[128,384]{1,0:T(8,128)(2,1)S(1)}, u32[]{:S(2)}, u32[]{:S(2)}) collective-permute-start(bf16[128,384]{1,0:T(8,128)(2,1)S(1)} %get-tuple-element.127), channel_id=1, source_target_pairs={{1,33},{3,35},{5,37},{7,39},{9,41},{11,43},{13,45},{15,47},{17,49}... | collective-permute-start | bytes 294920 | tf_op jit(solution)/shard_map/ppermute | solution.py:84
  93.4 1.6 %collective-permute-done.25.rest_1_ = bf16[128,384]{1,0:T(8,128)(2,1)S(1)} collective-permute-done((bf16[128,384]{1,0:T(8,128)(2,1)S(1)}, bf16[128,384]{1,0:T(8,128)(2,1)S(1)}, u32[]{:S(2)}, u32[]{:S(2)}) %collective-permute-start.25) | collective-permute-done | bytes 98336 | tf_op jit(solution)/shard_map/ppermute | solution.py:84
  103.5 10.4 %collective-permute-done.32.e = bf16[128,384]{1,0:T(8,128)(2,1)S(1)} collective-permute-done((bf16[128,384]{1,0:T(8,128)(2,1)S(1)}, bf16[128,384]{1,0:T(8,128)(2,1)S(1)}, u32[]{:S(2)}, u32[]{:S(2)}) %collective-permute-start.32) | collective-permute-done | bytes 98336 | tf_op jit(solution)/shard_map/ppermute | solution.py:84
  (77 shorter events, 22.0 us)
Async XLA Ops:
  2.6 11.9 %collective-permute-start = (bf16[5,160,96]{2,1,0:T(8,128)(2,1)S(1)}, bf16[5,160,96]{2,1,0:T(8,128)(2,1)S(1)}, u32[]{:S(2)}, u32[]{:S(2)}) collective-permute-start(bf16[5,160,96]{2,1,0:T(8,128)(2,1)S(1)} %get-tuple-element.75), channel_id=1, source_target_pairs={{32,0},{33,1},{34,2},{35,3},{36,4},{37,5},{38,6},{39,7},{40,8},{41... | collective-permute-start | bytes 460808 | tf_op jit(solution)/shard_map/ppermute | solution.py:84
  4.6 10.0 %collective-permute-start.2 = (bf16[5,160,96]{2,1,0:T(8,128)(2,1)S(1)}, bf16[5,160,96]{2,1,0:T(8,128)(2,1)S(1)}, u32[]{:S(2)}, u32[]{:S(2)}) collective-permute-start(bf16[5,160,96]{2,1,0:T(8,128)(2,1)S(1)} %get-tuple-element.79), channel_id=1, source_target_pairs={{0,32},{1,33},{2,34},{3,35},{4,36},{5,37},{6,38},{7,39},{8,40},{9,... | collective-permute-start | bytes 460808 | tf_op jit(solution)/shard_map/ppermute | solution.py:84
  8.1 6.4 %collective-permute-start.1 = (bf16[160,384]{1,0:T(8,128)(2,1)S(1)}, bf16[160,384]{1,0:T(8,128)(2,1)S(1)}, u32[]{:S(2)}, u32[]{:S(2)}) collective-permute-start(bf16[160,384]{1,0:T(8,128)(2,1)S(1)} %get-tuple-element.71.z.rest_7_), channel_id=1, source_target_pairs={{1,0},{2,1},{3,2},{4,3},{5,4},{6,5},{7,6},{8,7},{9,8},{10,9},{11,1... | collective-permute-start | bytes 368648 | tf_op jit(solution)/shard_map/ppermute | solution.py:84
  15.3 21.1 %collective-permute-start.5 = (bf16[3,128,256]{2,1,0:T(8,128)(2,1)S(1)}, bf16[3,128,256]{2,1,0:T(8,128)(2,1)S(1)}, u32[]{:S(2)}, u32[]{:S(2)}) collective-permute-start(bf16[3,128,256]{2,1,0:T(8,128)(2,1)S(1)} %get-tuple-element.87), channel_id=1, source_target_pairs={{1,33},{3,35},{5,37},{7,39},{9,41},{11,43},{13,45},{15,47},{17,49}... | collective-permute-start | bytes 589832 | tf_op jit(solution)/shard_map/ppermute | solution.py:84
  20.1 11.4 %collective-permute-start.4 = (bf16[1,128,256]{2,1,0:T(8,128)(2,1)S(1)}, bf16[1,128,256]{2,1,0:T(8,128)(2,1)S(1)}, u32[]{:S(2)}, u32[]{:S(2)}) collective-permute-start(bf16[1,128,256]{2,1,0:T(8,128)(2,1)S(1)} %get-tuple-element.86), channel_id=1, source_target_pairs={{2,33},{4,35},{6,37},{8,39},{10,41},{12,43},{14,45},{16,47},{18,49... | collective-permute-start | bytes 196616 | tf_op jit(solution)/shard_map/ppermute | solution.py:84
  21.4 15.1 %collective-permute-start.8 = (bf16[192,384]{1,0:T(8,128)(2,1)S(1)}, bf16[192,384]{1,0:T(8,128)(2,1)S(1)}, u32[]{:S(2)}, u32[]{:S(2)}) collective-permute-start(bf16[192,384]{1,0:T(8,128)(2,1)S(1)} %get-tuple-element.94), channel_id=1, source_target_pairs={{32,0},{33,1},{34,2},{35,3},{36,4},{37,5},{38,6},{39,7},{40,8},{41... | collective-permute-start | bytes 442376 | tf_op jit(solution)/shard_map/ppermute | solution.py:84
  23.3 13.1 %collective-permute-start.3 = (bf16[2,128,256]{2,1,0:T(8,128)(2,1)S(1)}, bf16[2,128,256]{2,1,0:T(8,128)(2,1)S(1)}, u32[]{:S(2)}, u32[]{:S(2)}) collective-permute-start(bf16[2,128,256]{2,1,0:T(8,128)(2,1)S(1)} %get-tuple-element.85), channel_id=1, source_target_pairs={{0,33},{2,35},{4,37},{6,39},{8,41},{10,43},{12,45},{14,47},{16,49}... | collective-permute-start | bytes 393224 | tf_op jit(solution)/shard_map/ppermute | solution.py:84
  24.6 10.7 %collective-permute-start.7 = (bf16[160,384]{1,0:T(8,128)(2,1)S(1)}, bf16[160,384]{1,0:T(8,128)(2,1)S(1)}, u32[]{:S(2)}, u32[]{:S(2)}) collective-permute-start(bf16[160,384]{1,0:T(8,128)(2,1)S(1)} %get-tuple-element.81.refs_0_), channel_id=1, source_target_pairs={{32,1},{33,2},{34,3},{35,4},{36,5},{37,6},{38,7},{39,8},{40,9},{41... | collective-permute-start | bytes 368648 | tf_op jit(solution)/shard_map/ppermute | solution.py:84
  31.6 4.9 %collective-permute-start.6 = (bf16[160,384]{1,0:T(8,128)(2,1)S(1)}, bf16[160,384]{1,0:T(8,128)(2,1)S(1)}, u32[]{:S(2)}, u32[]{:S(2)}) collective-permute-start(bf16[160,384]{1,0:T(8,128)(2,1)S(1)} %get-tuple-element.81.refs_0_), channel_id=1, source_target_pairs={{0,1},{1,2},{2,3},{3,4},{4,5},{5,6},{6,7},{7,8},{8,9},{9,10},{10,1... | collective-permute-start | bytes 368648 | tf_op jit(solution)/shard_map/ppermute | solution.py:84
  37.1 13.4 %collective-permute-start.11 = (bf16[3,128,256]{2,1,0:T(8,128)(2,1)S(1)}, bf16[3,128,256]{2,1,0:T(8,128)(2,1)S(1)}, u32[]{:S(2)}, u32[]{:S(2)}) collective-permute-start(bf16[3,128,256]{2,1,0:T(8,128)(2,1)S(1)} %get-tuple-element.99), channel_id=1, source_target_pairs={{33,1},{35,3},{37,5},{39,7},{41,9},{43,11},{45,13},{47,15},{49,17}... | collective-permute-start | bytes 589832 | tf_op jit(solution)/shard_map/ppermute | solution.py:84
  39.0 11.5 %collective-permute-start.9 = (bf16[2,128,256]{2,1,0:T(8,128)(2,1)S(1)}, bf16[2,128,256]{2,1,0:T(8,128)(2,1)S(1)}, u32[]{:S(2)}, u32[]{:S(2)}) collective-permute-start(bf16[2,128,256]{2,1,0:T(8,128)(2,1)S(1)} %get-tuple-element.97), channel_id=1, source_target_pairs={{32,1},{34,3},{36,5},{38,7},{40,9},{42,11},{44,13},{46,15},{48,17}... | collective-permute-start | bytes 393224 | tf_op jit(solution)/shard_map/ppermute | solution.py:84
  40.3 10.2 %collective-permute-start.12 = (bf16[160,384]{1,0:T(8,128)(2,1)S(1)}, bf16[160,384]{1,0:T(8,128)(2,1)S(1)}, u32[]{:S(2)}, u32[]{:S(2)}) collective-permute-start(bf16[160,384]{1,0:T(8,128)(2,1)S(1)} %get-tuple-element.96.refs_0_.rest_9_), channel_id=1, source_target_pairs={{1,0},{2,1},{3,2},{4,3},{5,4},{6,5},{7,6},{8,7},{9,8},{10,9},{11,1... | collective-permute-start | bytes 368648 | tf_op jit(solution)/shard_map/ppermute | solution.py:84
  42.6 7.9 %collective-permute-start.10 = (bf16[1,128,256]{2,1,0:T(8,128)(2,1)S(1)}, bf16[1,128,256]{2,1,0:T(8,128)(2,1)S(1)}, u32[]{:S(2)}, u32[]{:S(2)}) collective-permute-start(bf16[1,128,256]{2,1,0:T(8,128)(2,1)S(1)} %get-tuple-element.98), channel_id=1, source_target_pairs={{34,1},{36,3},{38,5},{40,7},{42,9},{44,11},{46,13},{48,15},{50,17}... | collective-permute-start | bytes 196616 | tf_op jit(solution)/shard_map/ppermute | solution.py:84
  52.6 17.7 %collective-permute-start.15 = (bf16[192,384]{1,0:T(8,128)(2,1)}, bf16[192,384]{1,0:T(8,128)(2,1)}, u32[]{:S(2)}, u32[]{:S(2)}) collective-permute-start(bf16[192,384]{1,0:T(8,128)(2,1)} %get-tuple-element.107), channel_id=1, source_target_pairs={{0,32},{1,33},{2,34},{3,35},{4,36},{5,37},{6,38},{7,39},{8,40},{9,... | collective-permute-start | bytes 442376 | tf_op jit(solution)/shard_map/ppermute | solution.py:84
  58.6 11.1 %collective-permute-start.14 = (bf16[160,384]{1,0:T(8,128)(2,1)S(1)}, bf16[160,384]{1,0:T(8,128)(2,1)}, u32[]{:S(2)}, u32[]{:S(2)}) collective-permute-start(bf16[160,384]{1,0:T(8,128)(2,1)S(1)} %get-tuple-element.106.refs_0_), channel_id=1, source_target_pairs={{0,33},{1,34},{2,35},{3,36},{4,37},{5,38},{6,39},{7,40},{8,41},{9,... | collective-permute-start | bytes 368648 | tf_op jit(solution)/shard_map/ppermute | solution.py:84
  60.7 9.6 %collective-permute-start.13 = (bf16[160,384]{1,0:T(8,128)(2,1)S(1)}, bf16[160,384]{1,0:T(8,128)(2,1)}, u32[]{:S(2)}, u32[]{:S(2)}) collective-permute-start(bf16[160,384]{1,0:T(8,128)(2,1)S(1)} %get-tuple-element.106.refs_0_), channel_id=1, source_target_pairs={{0,1},{1,2},{2,3},{3,4},{4,5},{5,6},{6,7},{7,8},{8,9},{9,10},{10,1... | collective-permute-start | bytes 368648 | tf_op jit(solution)/shard_map/ppermute | solution.py:84
  72.1 7.6 %collective-permute-start.17 = (bf16[256,384]{1,0:T(8,128)(2,1)S(1)}, bf16[256,384]{1,0:T(8,128)(2,1)S(1)}, u32[]{:S(2)}, u32[]{:S(2)}) collective-permute-start(bf16[256,384]{1,0:T(8,128)(2,1)S(1)} %get-tuple-element.118.z0), channel_id=1, source_target_pairs={{2,1},{4,3},{6,5},{8,7},{10,9},{12,11},{14,13},{16,15},{18,17},{20... | collective-permute-start | bytes 589832 | tf_op jit(solution)/shard_map/ppermute | solution.py:84
  73.4 6.3 %collective-permute-start.16 = (bf16[256,384]{1,0:T(8,128)(2,1)S(1)}, bf16[256,384]{1,0:T(8,128)(2,1)S(1)}, u32[]{:S(2)}, u32[]{:S(2)}) collective-permute-start(bf16[256,384]{1,0:T(8,128)(2,1)S(1)} %get-tuple-element.118.z0), channel_id=1, source_target_pairs={{0,1},{2,3},{4,5},{6,7},{8,9},{10,11},{12,13},{14,15},{16,17},{18,... | collective-permute-start | bytes 589832 | tf_op jit(solution)/shard_map/ppermute | solution.py:84
  80.9 6.5 %collective-permute-start.18 = (bf16[128,384]{1,0:T(8,128)(2,1)S(1)}, bf16[128,384]{1,0:T(8,128)(2,1)S(1)}, u32[]{:S(2)}, u32[]{:S(2)}) collective-permute-start(bf16[128,384]{1,0:T(8,128)(2,1)S(1)} %get-tuple-element.120), channel_id=1, source_target_pairs={{65,32},{67,34},{69,36},{71,38},{73,40},{75,42},{77,44},{79,46},{8... | collective-permute-start | bytes 294920 | tf_op jit(solution)/shard_map/ppermute | solution.py:84
  82.2 5.2 %collective-permute-start.19 = (bf16[128,384]{1,0:T(8,128)(2,1)S(1)}, bf16[128,384]{1,0:T(8,128)(2,1)S(1)}, u32[]{:S(2)}, u32[]{:S(2)}) collective-permute-start(bf16[128,384]{1,0:T(8,128)(2,1)S(1)} %get-tuple-element.121), channel_id=1, source_target_pairs={{65,34},{67,36},{69,38},{71,40},{73,42},{75,44},{77,46},{79,48},{8... | collective-permute-start | bytes 294920 | tf_op jit(solution)/shard_map/ppermute | solution.py:84
  83.5 3.9 %collective-permute-start.20 = (bf16[128,384]{1,0:T(8,128)(2,1)S(1)}, bf16[128,384]{1,0:T(8,128)(2,1)S(1)}, u32[]{:S(2)}, u32[]{:S(2)}) collective-permute-start(bf16[128,384]{1,0:T(8,128)(2,1)S(1)} %get-tuple-element.122), channel_id=1, source_target_pairs={{1,32},{3,34},{5,36},{7,38},{9,40},{11,42},{13,44},{15,46},{17,48}... | collective-permute-start | bytes 294920 | tf_op jit(solution)/shard_map/ppermute | solution.py:84
  86.1 5.6 %collective-permute-start.24 = (bf16[128,384]{1,0:T(8,128)(2,1)S(1)}, bf16[128,384]{1,0:T(8,128)(2,1)S(1)}, u32[]{:S(2)}, u32[]{:S(2)}) collective-permute-start(bf16[128,384]{1,0:T(8,128)(2,1)S(1)} %get-tuple-element.126), channel_id=1, source_target_pairs={{65,33},{67,35},{69,37},{71,39},{73,41},{75,43},{77,45},{79,47},{8... | collective-permute-start | bytes 294920 | tf_op jit(solution)/shard_map/ppermute | solution.py:84
  87.7 7.3 %collective-permute-start.23 = (bf16[256,384]{1,0:T(8,128)(2,1)S(1)}, bf16[256,384]{1,0:T(8,128)(2,1)S(1)}, u32[]{:S(2)}, u32[]{:S(2)}) collective-permute-start(bf16[256,384]{1,0:T(8,128)(2,1)S(1)} %get-tuple-element.125.z2), channel_id=1, source_target_pairs={{34,33},{36,35},{38,37},{40,39},{42,41},{44,43},{46,45},{48,47},{5... | collective-permute-start | bytes 589832 | tf_op jit(solution)/shard_map/ppermute | solution.py:84
  88.4 6.6 %collective-permute-start.22 = (bf16[256,384]{1,0:T(8,128)(2,1)S(1)}, bf16[256,384]{1,0:T(8,128)(2,1)S(1)}, u32[]{:S(2)}, u32[]{:S(2)}) collective-permute-start(bf16[256,384]{1,0:T(8,128)(2,1)S(1)} %get-tuple-element.125.z2), channel_id=1, source_target_pairs={{32,33},{34,35},{36,37},{38,39},{40,41},{42,43},{44,45},{46,47},{4... | collective-permute-start | bytes 589832 | tf_op jit(solution)/shard_map/ppermute | solution.py:84
  89.1 8.0 %collective-permute-start.27 = (bf16[256,384]{1,0:T(8,128)(2,1)S(1)}, bf16[256,384]{1,0:T(8,128)(2,1)S(1)}, u32[]{:S(2)}, u32[]{:S(2)}) collective-permute-start(bf16[256,384]{1,0:T(8,128)(2,1)S(1)} %get-tuple-element.129.z1), channel_id=1, source_target_pairs={{1,0},{3,2},{5,4},{7,6},{9,8},{11,10},{13,12},{15,14},{17,16},{19,... | collective-permute-start | bytes 589832 | tf_op jit(solution)/shard_map/ppermute | solution.py:84
  90.4 7.4 %collective-permute-start.26 = (bf16[256,384]{1,0:T(8,128)(2,1)S(1)}, bf16[256,384]{1,0:T(8,128)(2,1)S(1)}, u32[]{:S(2)}, u32[]{:S(2)}) collective-permute-start(bf16[256,384]{1,0:T(8,128)(2,1)S(1)} %get-tuple-element.129.z1), channel_id=1, source_target_pairs={{1,2},{3,4},{5,6},{7,8},{9,10},{11,12},{13,14},{15,16},{17,18},{19... | collective-permute-start | bytes 589832 | tf_op jit(solution)/shard_map/ppermute | solution.py:84
  96.4 4.1 %collective-permute-start.30 = (bf16[128,384]{1,0:T(8,128)(2,1)S(1)}, bf16[128,384]{1,0:T(8,128)(2,1)S(1)}, u32[]{:S(2)}, u32[]{:S(2)}) collective-permute-start(bf16[128,384]{1,0:T(8,128)(2,1)S(1)} %get-tuple-element.135), channel_id=1, source_target_pairs={{33,64},{35,66},{37,68},{39,70},{41,72},{43,74},{45,76},{47,78},{4... | collective-permute-start | bytes 294920 | tf_op jit(solution)/shard_map/ppermute | solution.py:84
  97.1 16.9 %collective-permute-start.35 = (bf16[256,384]{1,0:T(8,128)(2,1)S(1)}, bf16[256,384]{1,0:T(8,128)(2,1)S(1)}, u32[]{:S(2)}, u32[]{:S(2)}) collective-permute-start(bf16[256,384]{1,0:T(8,128)(2,1)S(1)} %get-tuple-element.130.z3), channel_id=1, source_target_pairs={{33,32},{35,34},{37,36},{39,38},{41,40},{43,42},{45,44},{47,46},{4... | collective-permute-start | bytes 589832 | tf_op jit(solution)/shard_map/ppermute | solution.py:84
  97.8 16.2 %collective-permute-start.34 = (bf16[256,384]{1,0:T(8,128)(2,1)S(1)}, bf16[256,384]{1,0:T(8,128)(2,1)S(1)}, u32[]{:S(2)}, u32[]{:S(2)}) collective-permute-start(bf16[256,384]{1,0:T(8,128)(2,1)S(1)} %get-tuple-element.130.z3), channel_id=1, source_target_pairs={{33,34},{35,36},{37,38},{39,40},{41,42},{43,44},{45,46},{47,48},{4... | collective-permute-start | bytes 589832 | tf_op jit(solution)/shard_map/ppermute | solution.py:84
  98.5 5.1 %collective-permute-start.31 = (bf16[128,384]{1,0:T(8,128)(2,1)S(1)}, bf16[128,384]{1,0:T(8,128)(2,1)S(1)}, u32[]{:S(2)}, u32[]{:S(2)}) collective-permute-start(bf16[128,384]{1,0:T(8,128)(2,1)S(1)} %get-tuple-element.136), channel_id=1, source_target_pairs={{33,66},{35,68},{37,70},{39,72},{41,74},{43,76},{45,78},{47,80},{4... | collective-permute-start | bytes 294920 | tf_op jit(solution)/shard_map/ppermute | solution.py:84
  99.1 14.8 %collective-permute-start.32 = (bf16[128,384]{1,0:T(8,128)(2,1)S(1)}, bf16[128,384]{1,0:T(8,128)(2,1)S(1)}, u32[]{:S(2)}, u32[]{:S(2)}) collective-permute-start(bf16[128,384]{1,0:T(8,128)(2,1)S(1)} %get-tuple-element.137), channel_id=1, source_target_pairs={{33,1},{35,3},{37,5},{39,7},{41,9},{43,11},{45,13},{47,15},{49,17}... | collective-permute-start | bytes 294920 | tf_op jit(solution)/shard_map/ppermute | solution.py:84
  100.5 13.5 %collective-permute-start.33 = (bf16[128,384]{1,0:T(8,128)(2,1)S(1)}, bf16[128,384]{1,0:T(8,128)(2,1)S(1)}, u32[]{:S(2)}, u32[]{:S(2)}) collective-permute-start(bf16[128,384]{1,0:T(8,128)(2,1)S(1)} %get-tuple-element.138), channel_id=1, source_target_pairs={{33,65},{35,67},{37,69},{39,71},{41,73},{43,75},{45,77},{47,79},{4... | collective-permute-start | bytes 294920 | tf_op jit(solution)/shard_map/ppermute | solution.py:84
  (15 other events, 125.0 us)
where the time goes:
time: 116 us; the launch traced here: 115 us
  starting transfers between devices  70.8 us (61%)
  waiting for transfers between devices  29 us (25%)
  Pallas kernels  11.2 us (10%)
  local copies, waits for them, and re-layouts  1.61 us (1%)
  between operations  1.23 us (1%)
    ppermute x36, starting transfers between devices, shift(): return lax.ppermute(x, ('bx', 'by'), pairs(*to, colours))  70.8 us
    ppermute x36, waiting for transfers between devices, shift(): return lax.ppermute(x, ('bx', 'by'), pairs(*to, colours))  29 us
    pallas_call x14, Pallas kernels, call(): pl.pallas_call(body, out_shape=[jax.ShapeDtypeStruct(s, d) for s, d in ou...  11.2 us
  transfers between devices with their start and end apart: 36, of which 9 were waited for; matrix products, arithmetic and copies ran while one was open for 1% of the time, Pallas kernels for 2%

commit v1 on v0

v1 whole, which is shorter than its diff:
```python
import functools

import jax
import jax.numpy as jnp
from jax import lax
from jax.experimental import pallas as pl
from jax.experimental.pallas import tpu as pltpu
from jax.sharding import PartitionSpec as P


S1, R1, P1 = 96, 160, 256
S2, R2, P2 = 128, 256, 384
K = 384
OFFSETS = [(-1, -1), (-1, 0), (-1, 1), (0, -1), (0, 1), (1, -1), (1, 0), (1, 1)]
BOXES = [(0, 0), (0, 1), (1, 0), (1, 1)]
F32, BF16 = jnp.float32, jnp.bfloat16
LEAF_S, LEAF_R, LEAF_Z = ((4, S1, K), F32), ((3, R1, K), F32), ((R1, K), BF16)
LEAF_W, LEAF_M = ((5, R1, S1), BF16), ((2 * S1, K), BF16)
PAR_W = ((3, S2, R2), BF16)
PAR_S, PAR_R, PAR_Z, PAR_M = ((S2, K), F32), ((R2, K), F32), ((R2, K), BF16), ((S2, K), BF16)


UP_TERMS = [((1, 0), (6, 7)), ((1, 1), (5, 6, 7))]
DOWN_TERMS = [((0, 0), (1, 2)), ((0, 1), (0, 1, 2))]


def dot(a, b):
    return lax.dot_general(a, b, (((1,), (0,)), ((), ())), preferred_element_type=F32)


def dot_t(a, b):
    return lax.dot_general(a, b, (((0,), (0,)), ((), ())), preferred_element_type=F32)


def source(box, k):
    row, col = box[0] + OFFSETS[k][0], box[1] + OFFSETS[k][1]
    return (row % 2) * 2 + col % 2, (row // 2, col // 2)


def reordered(x, perm, rows):
    pick = (lax.broadcasted_iota(jnp.int32, (rows, rows), 0) == perm).astype(F32).astype(BF16)
    high = x.astype(BF16)
    low = (x - high.astype(F32)).astype(BF16)
    return dot_t(pick, high) + dot_t(pick, low)


SMEM, VMEM, HBM = (pl.BlockSpec(memory_space=s) for s in (pltpu.SMEM, pltpu.VMEM, pltpu.HBM))


def call(body, ins, outs, specs=(), scratch=(), alias=None):
    specs = list(specs) + [VMEM] * (len(ins) - len(specs))
    return pl.pallas_call(
        body,
        out_shape=[jax.ShapeDtypeStruct(s, d) for s, d in outs],
        in_specs=specs,
        out_specs=[VMEM] * len(outs),
        scratch_shapes=list(scratch),
        input_output_aliases=alias or {},
        compiler_params=pltpu.CompilerParams(vmem_limit_bytes=20 * 1024 * 1024),
        cost_estimate=pl.CostEstimate(flops=300_000_000, bytes_accessed=2_000_000, transcendentals=0),
    )(*ins)


def pairs(dx, dy, colours):
    nx, ny = lax.axis_size("bx"), lax.axis_size("by")
    out = []
    for i in range(nx):
        for j in range(ny):
            if (i % 2) * 2 + j % 2 in colours and 0 <= i + dx < nx and 0 <= j + dy < ny:
                out.append((i * ny + j, (i + dx) * ny + j + dy))
    return out


def shift(x, to, colours=(0, 1, 2, 3)):
    return lax.ppermute(x, ("bx", "by"), pairs(*to, colours))


def after(x, value):
    return lax.optimization_barrier((x, value))


def first_body(rhs, perm, interp, piv, couple, top, z_out, skel_out, up_out, down_out, below_out, above_out, *rest):
    x, p, t, v, sems = rest
    jobs = [(rhs.at[0, 0], x), (perm, p), (interp.at[0, 0], t), (piv.at[0, 0], v)]
    for terms, out in ((UP_TERMS, up_out), (DOWN_TERMS, down_out)):
        at = 0
        for (i, j), ks in terms:
            jobs.append((couple.at[i, j, pl.ds(ks[0], len(ks))], out.at[pl.ds(at, len(ks))]))
            at += len(ks)
    jobs.append((top.at[0, 0, pl.ds(5, 3)], below_out))
    jobs.append((top.at[0, 0, pl.ds(0, 3)], above_out))
    copies = [pltpu.make_async_copy(a, b, sems.at[n]) for n, (a, b) in enumerate(jobs)]
    for c in copies:
        c.start()
    for c in copies[:4]:
        c.wait()
    leaf = reordered(x[...], p[0, 0:1, :], P1)
    skel = leaf[:S1]
    diff = leaf[S1:] - dot(t[...], skel.astype(BF16))
    z_out[...] = dot(v[...], diff.astype(BF16)).astype(BF16)
    skel_out[...] = skel
    for c in copies[4:]:
        c.wait()


def spread_body(rhs, perm, interp, couple, z, skel0, skels, reds):
    zc = z[...]
    skels[0] = skel0[...] - dot_t(interp[0, 0], zc)
    for n in (1, 2, 3):
        i, j = BOXES[n]
        leaf = reordered(rhs[i, j], perm[i, j : j + 1, :], P1)
        reds[n - 1] = leaf[S1:]
        acc = leaf[:S1]
        for k in range(8):
            if source((i, j), k) == (0, (0, 0)):
                acc = acc - dot_t(couple[i, j, k], zc)
        skels[n] = acc


def solve_body(colour, ks, part, interp, piv, couple, skels, reds, *rest):
    zs, (*arrived, z_out, out) = rest[: len(ks)], rest[len(ks) :]
    i, j = BOXES[colour]
    acc = skels[colour]
    if part is not None:
        acc = acc - arrived[0][part * S1 : (part + 1) * S1].astype(F32)
    for k, z in zip(ks, zs):
        acc = acc - dot_t(couple[i, j, k], z[...])
    diff = reds[colour - 1] - dot(interp[i, j], acc.astype(BF16))
    z_out[...] = dot(piv[i, j], diff.astype(BF16)).astype(BF16)
    out[...] = skels[...]
    out[colour] = acc


def sum_body(terms, left, own, right, mats, out):
    values, at = (left[...], own[...], right[...]), 0
    for n, (_, ks) in enumerate(terms):
        total = None
        for w in range(len(ks)):
            term = dot_t(mats[at], values[w])
            total = term if total is None else total + term
            at += 1
        out[n * S1 : (n + 1) * S1] = total.astype(BF16)


def update_body(own, jobs, n_z, part, interp, couple, *refs):
    zs, (skels, *arrived, out) = refs[:n_z], refs[n_z:]
    for n in range(4):
        i, j = BOXES[n]
        acc = skels[n]
        if n == own:
            acc = acc - dot_t(interp[i, j], zs[0][...])
        if part == n:
            acc = acc - arrived[0][S1 : 2 * S1].astype(F32)
        for k, at in jobs[n]:
            acc = acc - dot_t(couple[i, j, k], zs[at][...])
        out[n] = acc


def pick_body(perm, pick_out):
    hit = (lax.broadcasted_iota(jnp.int32, (P2, P2), 0) == perm[0]).astype(F32)
    pick_out[...] = hit.T.astype(BF16)


def jobs_of(order, drop=()):
    jobs = [[], [], [], []]
    for n in range(4):
        for k in range(8):
            where = source(BOXES[n], k)
            if where in order and (n, where) not in drop:
                jobs[n].append((k, order.index(where)))
    return jobs


def work(rhs, perm1, interp1, pivinv1, couple1, perm2, interp2, pivinv2, couple2):
    couple1 = couple1.swapaxes(3, 4)
    have = {}
    here = (0, 0)

    def solve(colour, keys, skels, reds, arrived=None, part=None):
        box = BOXES[colour]
        ks, zs = [], []
        for k in range(8):
            if source(box, k) in keys:
                ks.append(k)
                zs.append(have[source(box, k)])
        ins = [interp1, pivinv1, couple1, skels, reds, *zs] + ([arrived] if arrived is not None else [])
        body = functools.partial(solve_body, colour, ks, part)
        z, skels = call(body, ins, [LEAF_Z, LEAF_S])
        have[(colour, here)] = z
        return z, skels

    def total(terms, left, own, right, mats):
        return call(functools.partial(sum_body, terms), [left, own, right, mats], [LEAF_M])[0]

    def update(own, keys, skels, drop=(), arrived=None, part=None):
        order = [(own, here), *keys]
        ins = [interp1, couple1, *[have[key] for key in order], skels] + ([arrived] if arrived is not None else [])
        body = functools.partial(update_body, own, jobs_of(order, drop), len(order), part)
        return call(body, ins, [LEAF_S])[0]

    z00, skel0, up_pack, down_pack, below_pack, above_pack = call(
        first_body,
        [pltpu.with_memory_space_constraint(x, pltpu.HBM) for x in (rhs, perm1, interp1, pivinv1, couple1, couple2)],
        [LEAF_Z, ((S1, K), F32), LEAF_W, LEAF_W, PAR_W, PAR_W],
        specs=[HBM] * 6,
        scratch=[
            pltpu.VMEM((P1, K), F32),
            pltpu.VMEM((2, 2, P1), jnp.int32),
            pltpu.VMEM((R1, S1), BF16),
            pltpu.VMEM((R1, R1), BF16),
            pltpu.SemaphoreType.DMA((4 + 4 + 2,)),
        ],
    )
    have[(0, here)] = z00
    z00r = have[(0, (0, 1))] = shift(z00, (0, -1))
    up_mats = shift(up_pack, (1, 0))
    skels, reds = call(spread_body, [rhs, perm1, interp1, couple1, z00, skel0], [LEAF_S, LEAF_R])
    z01, skels = solve(1, {(0, (0, 1))}, skels, reds)
    have[(1, (1, -1))] = shift(z01, (-1, 1))
    from_below = shift(total(UP_TERMS, z00, z01, z00r, up_mats), (-1, 0))
    have[(1, (0, -1))] = shift(z01, (0, 1))
    below_pack, z01 = after(below_pack, z01)
    have[(1, here)] = z01
    above_mats = shift(below_pack, (1, 0))
    skels = update(1, [(0, (0, 1))], skels, drop=[(1, (0, (0, 1)))])
    z10, skels = solve(2, {(1, (0, -1)), (1, (1, -1))}, skels, reds, arrived=from_below, part=0)
    z10r = have[(2, (0, 1))] = shift(z10, (0, -1))
    down_pack, z10 = after(down_pack, z10)
    have[(2, here)] = z10
    down_mats = shift(down_pack, (-1, 0))
    skels = update(2, [(1, (0, -1))], skels, drop=[(2, (1, (0, -1)))], arrived=from_below, part=3)
    z11, skels = solve(3, {(2, (0, 1))}, skels, reds)
    have[(3, (-1, -1))] = shift(z11, (1, 1))
    from_above = shift(total(DOWN_TERMS, z10, z11, z10r, down_mats), (1, 0))
    have[(3, (0, -1))] = shift(z11, (0, 1))
    above_pack, z11 = after(above_pack, z11)
    have[(3, here)] = z11
    below_mats = shift(above_pack, (-1, 0))
    skels = update(3, [(2, (0, 1))], skels, drop=[(3, (2, (0, 1)))])
    (pick,) = call(pick_body, [perm2], [((P2, P2), BF16)])
    red1 = jnp.stack([z00, z01, z10, z11]).reshape(2, 2, R1, K)

    colour = ((lax.axis_index("bx") % 2) * 2 + lax.axis_index("by") % 2).astype(jnp.int32).reshape(1)
    last = [(3, (0, -1)), (3, (-1, -1))]
    last_jobs = jobs_of(last)

    def solve_parent(interp, piv, skel, red):
        diff = red - dot(interp[0, 0], skel.astype(BF16))
        return dot(piv[0, 0], diff.astype(BF16)).astype(BF16)

    def join_body(me, pick, interp, piv, couple, za, zb, arrived, children, skel_out, red_out, z_out):
        zs = [za, zb]
        parts = []
        for n in range(4):
            acc = children[n]
            if n < 2:
                acc = acc - arrived[n * S1 : (n + 1) * S1].astype(F32)
            for k, at in last_jobs[n]:
                acc = acc - dot_t(couple[BOXES[n][0], BOXES[n][1], k], zs[at][...])
            parts.append(acc)
        x = jnp.concatenate(parts, axis=0)
        high = x.astype(BF16)
        low = (x - high.astype(F32)).astype(BF16)
        parent = dot(pick[...], high) + dot(pick[...], low)
        skel_out[...] = parent[:S2]
        red_out[...] = parent[S2:]

        @pl.when(me[0] == 0)
        def _():
            z_out[...] = solve_parent(interp, piv, parent[:S2], parent[S2:])

    skel, red, z0 = call(
        join_body,
        [colour, pick, interp2, pivinv2, couple1, *[have[key] for key in last], from_above, skels],
        [PAR_S, PAR_R, PAR_Z],
        specs=[SMEM],
    )

    def sides(z, c):
        return shift(z, (0, 1), (c,)), shift(z, (0, -1), (c,))

    def ends(sums, row):
        colours = (2 * row, 2 * row + 1)
        return shift(sums[0], (-1, 0), colours), shift(sums[1], (1, 0), colours)

    def parent_body(c, me, interp, piv, couple, skel, red, *rest):
        *got, z_out, skel_out = rest

        @pl.when(me[0] != c)
        def _():
            skel_out[...] = skel[...]

        @pl.when(me[0] == c)
        def _():
            acc = skel[...]
            if c % 2:
                acc = acc - (dot(couple[0, 0, 3], got[0][...]) + dot(couple[0, 0, 4], got[1][...]))
            if c >= 2:
                acc = acc - (got[-2][...].astype(F32) + got[-1][...].astype(F32))
            skel_out[...] = acc
            z_out[...] = solve_parent(interp, piv, acc, red[...])

    def parent(c, skel, got):
        return call(
            functools.partial(parent_body, c),
            [colour, interp2, pivinv2, couple2, skel, red, *got],
            [PAR_Z, PAR_S],
            specs=[SMEM],
        )

    def row_body(row, me, above, below, el, er, ol, orr, ze, zo, up_out, down_out):
        for c, (a, own, b) in ((2 * row, (ol, ze, orr)), (2 * row + 1, (el, zo, er))):

            @pl.when(me[0] == c)
            def _():
                for w, out in ((above, up_out), (below, down_out)):
                    total = dot(w[0], a[...]) + dot(w[1], own[...]) + dot(w[2], b[...])
                    out[...] = total.astype(BF16)

    def row(n, even, odd, z_even, z_odd):
        return call(
            functools.partial(row_body, n),
            [colour, above_mats, below_mats, *even, *odd, z_even, z_odd],
            [PAR_M, PAR_M],
            specs=[SMEM],
        )

    side0 = sides(z0, 0)
    z1, skel = parent(1, skel, side0)
    side1 = sides(z1, 1)
    end0 = ends(row(0, side0, side1, z0, z1), 0)
    z2, skel = parent(2, skel, end0)
    side2 = sides(z2, 2)
    z3, skel = parent(3, skel, (*side2, *end0))
    side3 = sides(z3, 3)
    end1 = ends(row(1, side2, side3, z2, z3), 1)

    def early_body(me, interp, couple, skel, z0, z1, z2, z3, al, ar, bl, br, skel_out, z_out):
        for c, own in enumerate((z0, z1, z2, z3)):

            @pl.when(me[0] == c)
            def _():
                zc = own[...]
                z_out[...] = zc
                acc = skel[...] - dot_t(interp[0, 0], zc)
                if c % 2 == 0:
                    xl, xr = ((al, ar), (bl, br))[c // 2]
                    acc = acc - (dot(couple[0, 0, 3], xl[...]) + dot(couple[0, 0, 4], xr[...]))
                skel_out[...] = acc

    skel, red2 = call(
        early_body, [colour, interp2, couple2, skel, z0, z1, z2, z3, *side1, *side3], [PAR_S, PAR_Z], specs=[SMEM]
    )

    def late_body(me, skel, a, b, skel_out):
        @pl.when(me[0] < 2)
        def _():
            skel_out[...] = skel[...] - (a[...].astype(F32) + b[...].astype(F32))

        @pl.when(me[0] >= 2)
        def _():
            skel_out[...] = skel[...]

    (skel2,) = call(late_body, [colour, skel, *end1], [PAR_S], specs=[SMEM])
    return (red1, red2[None, None], skel2[None, None])


def solution(mesh):
    in_specs = (
        P("bx", "by", None, None),
        P("bx", "by", None),
        P("bx", "by", None, None),
        P("bx", "by", None, None),
        P("bx", "by", None, None, None),
        P("bx", "by", None),
        P("bx", "by", None, None),
        P("bx", "by", None, None),
        P("bx", "by", None, None, None),
    )
    out_specs = (P("bx", "by", None, None), P("bx", "by", None, None), P("bx", "by", None, None))
    return jax.shard_map(work, mesh=mesh, in_specs=in_specs, out_specs=out_specs, check_vma=False)
```

time: 116 us -> 107 us (0.922)
  the two profiles are of different devices: /device:TPU:83 before, /device:TPU:70 now
where the time goes in v1:
time: 107 us; the launch traced here: 106 us
  starting transfers between devices  47.4 us (44%)
  waiting for transfers between devices  46.8 us (44%)
  Pallas kernels  10.1 us (9%)
  between operations  1.14 us (1%)
    ppermute x24, starting transfers between devices, shift(): return lax.ppermute(x, ('bx', 'by'), pairs(*to, colours))  47.4 us
    ppermute x24, waiting for transfers between devices, shift(): return lax.ppermute(x, ('bx', 'by'), pairs(*to, colours))  46.8 us
    pallas_call x19, Pallas kernels, call(): pl.pallas_call(body, out_shape=[jax.ShapeDtypeStruct(s, d) for s, d in ou...  10.1 us
  transfers between devices with their start and end apart: 24, of which 12 were waited for; matrix products, arithmetic and copies ran while one was open for 1% of the time, Pallas kernels for 4%

profile of v1, /device:TPU:70, one launch (start us, length us, event | category | flops | bytes accessed | tf_op | source)
XLA Modules:
  0.0 106.5 jit_solution(17147050020593593497)
XLA Ops:
  0.7 1.9 %shard_map.112 = (bf16[160,384]{1,0:T(8,128)(2,1)S(1)}, f32[96,384]{1,0:T(8,128)S(1)}, bf16[5,160,96]{2,1,0:T(8,128)(2,1)S(1)}, bf16[5,160,96]{2,1,0:T(8,128)(2,...) custom-call(f32[2,2,256,384]{3,2,1,0:T(8,128)} %rhs.3, s32[2,2,256]{2,1,0:T(2,128)} %perm.4, ...), custom_call_target="tpu_custom_call" | custom-call | flops 300000000 | bytes 2000000 | tf_op jit(solution)/shard_map/pallas_call | solution.py:52
  2.6 3.8 %collective-permute-start.3 = (bf16[5,160,96]{2,1,0:T(8,128)(2,1)S(1)}, bf16[5,160,96]{2,1,0:T(8,128)(2,1)S(1)}, u32[]{:S(2)}, u32[]{:S(2)}) collective-permute-start(bf16[5,160,96]{2,1,0:T(8,128)(2,1)S(1)} %get-tuple-element.47), channel_id=1, source_target_pairs={{0,32},{1,33},{2,34},{3,35},{4,36},{5,37},{6,38},{7,39},{8,40},{9,... | collective-permute-start | bytes 460808 | tf_op jit(solution)/shard_map/ppermute | solution.py:75
  6.4 4.3 %collective-permute-start = (bf16[160,384]{1,0:T(8,128)(2,1)S(1)}, bf16[160,384]{1,0:T(8,128)(2,1)S(1)}, u32[]{:S(2)}, u32[]{:S(2)}) collective-permute-start(bf16[160,384]{1,0:T(8,128)(2,1)S(1)} %get-tuple-element.38.z.left), channel_id=1, source_target_pairs={{1,0},{2,1},{3,2},{4,3},{5,4},{6,5},{7,6},{8,7},{9,8},{10,9},{11,1... | collective-permute-start | bytes 368648 | tf_op jit(solution)/shard_map/ppermute | solution.py:75
  11.6 1.6 %collective-permute-done.rest_0_.refs_1_.right = bf16[160,384]{1,0:T(8,128)(2,1)S(1)} collective-permute-done((bf16[160,384]{1,0:T(8,128)(2,1)S(1)}, bf16[160,384]{1,0:T(8,128)(2,1)S(1)}, u32[]{:S(2)}, u32[]{:S(2)}) %collective-permute-start) | collective-permute-done | bytes 122912 | tf_op jit(solution)/shard_map/ppermute | solution.py:75
  14.1 2.0 %collective-permute-start.4 = (bf16[192,384]{1,0:T(8,128)(2,1)S(1)}, bf16[192,384]{1,0:T(8,128)(2,1)S(1)}, u32[]{:S(2)}, u32[]{:S(2)}) collective-permute-start(bf16[192,384]{1,0:T(8,128)(2,1)S(1)} %shard_map.116), channel_id=1, source_target_pairs={{32,0},{33,1},{34,2},{35,3},{36,4},{37,5},{38,6},{39,7},{40,8},{41... | collective-permute-start | bytes 442376 | tf_op jit(solution)/shard_map/ppermute | solution.py:75
  16.1 1.9 %collective-permute-start.1 = (bf16[160,384]{1,0:T(8,128)(2,1)S(1)}, bf16[160,384]{1,0:T(8,128)(2,1)S(1)}, u32[]{:S(2)}, u32[]{:S(2)}) collective-permute-start(bf16[160,384]{1,0:T(8,128)(2,1)S(1)} %get-tuple-element.44.refs_0_.own), channel_id=1, source_target_pairs={{0,1},{1,2},{2,3},{3,4},{4,5},{5,6},{6,7},{7,8},{8,9},{9,10},{10,1... | collective-permute-start | bytes 368648 | tf_op jit(solution)/shard_map/ppermute | solution.py:75
  18.1 1.9 %collective-permute-start.2 = (bf16[160,384]{1,0:T(8,128)(2,1)S(1)}, bf16[160,384]{1,0:T(8,128)(2,1)S(1)}, u32[]{:S(2)}, u32[]{:S(2)}) collective-permute-start(bf16[160,384]{1,0:T(8,128)(2,1)S(1)} %get-tuple-element.44.refs_0_.own), channel_id=1, source_target_pairs={{32,1},{33,2},{34,3},{35,4},{36,5},{37,6},{38,7},{39,8},{40,9},{41... | collective-permute-start | bytes 368648 | tf_op jit(solution)/shard_map/ppermute | solution.py:75
  20.3 4.1 %collective-permute-done.1.rest_0_.refs_1_ = bf16[160,384]{1,0:T(8,128)(2,1)S(1)} collective-permute-done((bf16[160,384]{1,0:T(8,128)(2,1)S(1)}, bf16[160,384]{1,0:T(8,128)(2,1)S(1)}, u32[]{:S(2)}, u32[]{:S(2)}) %collective-permute-start.1) | collective-permute-done | bytes 122912 | tf_op jit(solution)/shard_map/ppermute | solution.py:75
  24.5 5.1 %collective-permute-done.2.rest_1_ = bf16[160,384]{1,0:T(8,128)(2,1)S(1)} collective-permute-done((bf16[160,384]{1,0:T(8,128)(2,1)S(1)}, bf16[160,384]{1,0:T(8,128)(2,1)S(1)}, u32[]{:S(2)}, u32[]{:S(2)}) %collective-permute-start.2) | collective-permute-done | bytes 122912 | tf_op jit(solution)/shard_map/ppermute | solution.py:75
  30.2 1.9 %collective-permute-start.8 = (bf16[5,160,96]{2,1,0:T(8,128)(2,1)S(1)}, bf16[5,160,96]{2,1,0:T(8,128)(2,1)S(1)}, u32[]{:S(2)}, u32[]{:S(2)}) collective-permute-start(bf16[5,160,96]{2,1,0:T(8,128)(2,1)S(1)} %get-tuple-element.54), channel_id=1, source_target_pairs={{32,0},{33,1},{34,2},{35,3},{36,4},{37,5},{38,6},{39,7},{40,8},{41... | collective-permute-start | bytes 460808 | tf_op jit(solution)/shard_map/ppermute | solution.py:75
  32.1 2.6 %collective-permute-start.5 = (bf16[160,384]{1,0:T(8,128)(2,1)S(1)}, bf16[160,384]{1,0:T(8,128)(2,1)S(1)}, u32[]{:S(2)}, u32[]{:S(2)}) collective-permute-start(bf16[160,384]{1,0:T(8,128)(2,1)S(1)} %get-tuple-element.49.refs_0_.left), channel_id=1, source_target_pairs={{1,0},{2,1},{3,2},{4,3},{5,4},{6,5},{7,6},{8,7},{9,8},{10,9},{11,1... | collective-permute-start | bytes 368648 | tf_op jit(solution)/shard_map/ppermute | solution.py:75
  35.0 2.1 %collective-permute-done.5.rest_0_.right.refs_1_ = bf16[160,384]{1,0:T(8,128)(2,1)S(1)} collective-permute-done((bf16[160,384]{1,0:T(8,128)(2,1)S(1)}, bf16[160,384]{1,0:T(8,128)(2,1)S(1)}, u32[]{:S(2)}, u32[]{:S(2)}) %collective-permute-start.5) | collective-permute-done | bytes 122912 | tf_op jit(solution)/shard_map/ppermute | solution.py:75
  37.7 1.4 %collective-permute-done.8.mats = bf16[5,160,96]{2,1,0:T(8,128)(2,1)S(1)} collective-permute-done((bf16[5,160,96]{2,1,0:T(8,128)(2,1)S(1)}, bf16[5,160,96]{2,1,0:T(8,128)(2,1)S(1)}, u32[]{:S(2)}, u32[]{:S(2)}) %collective-permute-start.8) | collective-permute-done | bytes 153632 | tf_op jit(solution)/shard_map/ppermute | solution.py:75
  40.1 5.1 %collective-permute-start.9 = (bf16[192,384]{1,0:T(8,128)(2,1)}, bf16[192,384]{1,0:T(8,128)(2,1)S(1)}, u32[]{:S(2)}, u32[]{:S(2)}) collective-permute-start(bf16[192,384]{1,0:T(8,128)(2,1)} %shard_map.121), channel_id=1, source_target_pairs={{0,32},{1,33},{2,34},{3,35},{4,36},{5,37},{6,38},{7,39},{8,40},{9,... | collective-permute-start | bytes 442376 | tf_op jit(solution)/shard_map/ppermute | solution.py:75
  45.2 1.9 %collective-permute-start.6 = (bf16[160,384]{1,0:T(8,128)(2,1)S(1)}, bf16[160,384]{1,0:T(8,128)(2,1)S(1)}, u32[]{:S(2)}, u32[]{:S(2)}) collective-permute-start(bf16[160,384]{1,0:T(8,128)(2,1)S(1)} %get-tuple-element.53.own.refs_0_), channel_id=1, source_target_pairs={{0,1},{1,2},{2,3},{3,4},{4,5},{5,6},{6,7},{7,8},{8,9},{9,10},{10,1... | collective-permute-start | bytes 368648 | tf_op jit(solution)/shard_map/ppermute | solution.py:75
  47.1 1.9 %collective-permute-start.7 = (bf16[160,384]{1,0:T(8,128)(2,1)S(1)}, bf16[160,384]{1,0:T(8,128)(2,1)S(1)}, u32[]{:S(2)}, u32[]{:S(2)}) collective-permute-start(bf16[160,384]{1,0:T(8,128)(2,1)S(1)} %get-tuple-element.53.own.refs_0_), channel_id=1, source_target_pairs={{0,33},{1,34},{2,35},{3,36},{4,37},{5,38},{6,39},{7,40},{8,41},{9,... | collective-permute-start | bytes 368648 | tf_op jit(solution)/shard_map/ppermute | solution.py:75
  49.6 3.9 %collective-permute-done.6.za = bf16[160,384]{1,0:T(8,128)(2,1)S(1)} collective-permute-done((bf16[160,384]{1,0:T(8,128)(2,1)S(1)}, bf16[160,384]{1,0:T(8,128)(2,1)S(1)}, u32[]{:S(2)}, u32[]{:S(2)}) %collective-permute-start.6) | collective-permute-done | bytes 122912 | tf_op jit(solution)/shard_map/ppermute | solution.py:75
  53.5 3.3 %collective-permute-done.7.zb = bf16[160,384]{1,0:T(8,128)(2,1)S(1)} collective-permute-done((bf16[160,384]{1,0:T(8,128)(2,1)S(1)}, bf16[160,384]{1,0:T(8,128)(2,1)S(1)}, u32[]{:S(2)}, u32[]{:S(2)}) %collective-permute-start.7) | collective-permute-done | bytes 122912 | tf_op jit(solution)/shard_map/ppermute | solution.py:75
  58.0 1.3 %collective-permute-start.10 = (bf16[256,384]{1,0:T(8,128)(2,1)S(1)}, bf16[256,384]{1,0:T(8,128)(2,1)S(1)}, u32[]{:S(2)}, u32[]{:S(2)}) collective-permute-start(bf16[256,384]{1,0:T(8,128)(2,1)S(1)} %get-tuple-element.58.ze.z0), channel_id=1, source_target_pairs={{0,1},{2,3},{4,5},{6,7},{8,9},{10,11},{12,13},{14,15},{16,17},{18,... | collective-permute-start | bytes 589832 | tf_op jit(solution)/shard_map/ppermute | solution.py:75
  59.3 2.3 %collective-permute-start.11 = (bf16[256,384]{1,0:T(8,128)(2,1)S(1)}, bf16[256,384]{1,0:T(8,128)(2,1)S(1)}, u32[]{:S(2)}, u32[]{:S(2)}) collective-permute-start(bf16[256,384]{1,0:T(8,128)(2,1)S(1)} %get-tuple-element.58.ze.z0), channel_id=1, source_target_pairs={{2,1},{4,3},{6,5},{8,7},{10,9},{12,11},{14,13},{16,15},{18,17},{20... | collective-permute-start | bytes 589832 | tf_op jit(solution)/shard_map/ppermute | solution.py:75
  61.6 1.9 %collective-permute-start.12 = (bf16[3,128,256]{2,1,0:T(8,128)(2,1)S(1)}, bf16[3,128,256]{2,1,0:T(8,128)(2,1)S(1)}, u32[]{:S(2)}, u32[]{:S(2)}) collective-permute-start(bf16[3,128,256]{2,1,0:T(8,128)(2,1)S(1)} %get-tuple-element.60), channel_id=1, source_target_pairs={{0,32},{1,33},{2,34},{3,35},{4,36},{5,37},{6,38},{7,39},{8,40},{9,... | collective-permute-start | bytes 589832 | tf_op jit(solution)/shard_map/ppermute | solution.py:75
  63.6 3.9 %collective-permute-start.13 = (bf16[3,128,256]{2,1,0:T(8,128)(2,1)S(1)}, bf16[3,128,256]{2,1,0:T(8,128)(2,1)S(1)}, u32[]{:S(2)}, u32[]{:S(2)}) collective-permute-start(bf16[3,128,256]{2,1,0:T(8,128)(2,1)S(1)} %get-tuple-element.61), channel_id=1, source_target_pairs={{32,0},{33,1},{34,2},{35,3},{36,4},{37,5},{38,6},{39,7},{40,8},{41... | collective-permute-start | bytes 589832 | tf_op jit(solution)/shard_map/ppermute | solution.py:75
  67.6 1.3 %collective-permute-start.14 = (bf16[256,384]{1,0:T(8,128)(2,1)S(1)}, bf16[256,384]{1,0:T(8,128)(2,1)S(1)}, u32[]{:S(2)}, u32[]{:S(2)}) collective-permute-start(bf16[256,384]{1,0:T(8,128)(2,1)S(1)} %get-tuple-element.62.zo.z1), channel_id=1, source_target_pairs={{1,2},{3,4},{5,6},{7,8},{9,10},{11,12},{13,14},{15,16},{17,18},{19... | collective-permute-start | bytes 589832 | tf_op jit(solution)/shard_map/ppermute | solution.py:75
  68.9 1.3 %collective-permute-start.15 = (bf16[256,384]{1,0:T(8,128)(2,1)S(1)}, bf16[256,384]{1,0:T(8,128)(2,1)S(1)}, u32[]{:S(2)}, u32[]{:S(2)}) collective-permute-start(bf16[256,384]{1,0:T(8,128)(2,1)S(1)} %get-tuple-element.62.zo.z1), channel_id=1, source_target_pairs={{1,0},{3,2},{5,4},{7,6},{9,8},{11,10},{13,12},{15,14},{17,16},{19,... | collective-permute-start | bytes 589832 | tf_op jit(solution)/shard_map/ppermute | solution.py:75
  70.2 2.9 %collective-permute-done.13.below = bf16[3,128,256]{2,1,0:T(8,128)(2,1)S(1)} collective-permute-done((bf16[3,128,256]{2,1,0:T(8,128)(2,1)S(1)}, bf16[3,128,256]{2,1,0:T(8,128)(2,1)S(1)}, u32[]{:S(2)}, u32[]{:S(2)}) %collective-permute-start.13) | collective-permute-done | bytes 196640 | tf_op jit(solution)/shard_map/ppermute | solution.py:75
  73.0 3.6 %collective-permute-done.14.ol.al = bf16[256,384]{1,0:T(8,128)(2,1)S(1)} collective-permute-done((bf16[256,384]{1,0:T(8,128)(2,1)S(1)}, bf16[256,384]{1,0:T(8,128)(2,1)S(1)}, u32[]{:S(2)}, u32[]{:S(2)}) %collective-permute-start.14) | collective-permute-done | bytes 196640 | tf_op jit(solution)/shard_map/ppermute | solution.py:75
  77.0 1.3 %collective-permute-start.16 = (bf16[128,384]{1,0:T(8,128)(2,1)S(1)}, bf16[128,384]{1,0:T(8,128)(2,1)S(1)}, u32[]{:S(2)}, u32[]{:S(2)}) collective-permute-start(bf16[128,384]{1,0:T(8,128)(2,1)S(1)} %get-tuple-element.63), channel_id=1, source_target_pairs={{64,32},{65,33},{66,34},{67,35},{68,36},{69,37},{70,38},{71,39},{7... | collective-permute-start | bytes 294920 | tf_op jit(solution)/shard_map/ppermute | solution.py:75
  78.3 1.3 %collective-permute-start.17 = (bf16[128,384]{1,0:T(8,128)(2,1)S(1)}, bf16[128,384]{1,0:T(8,128)(2,1)S(1)}, u32[]{:S(2)}, u32[]{:S(2)}) collective-permute-start(bf16[128,384]{1,0:T(8,128)(2,1)S(1)} %get-tuple-element.64), channel_id=1, source_target_pairs={{0,32},{1,33},{2,34},{3,35},{4,36},{5,37},{6,38},{7,39},{8,40},{9,... | collective-permute-start | bytes 294920 | tf_op jit(solution)/shard_map/ppermute | solution.py:75
  80.5 1.3 %collective-permute-done.17.rest_1_.rest_3_ = bf16[128,384]{1,0:T(8,128)(2,1)S(1)} collective-permute-done((bf16[128,384]{1,0:T(8,128)(2,1)S(1)}, bf16[128,384]{1,0:T(8,128)(2,1)S(1)}, u32[]{:S(2)}, u32[]{:S(2)}) %collective-permute-start.17) | collective-permute-done | bytes 98336 | tf_op jit(solution)/shard_map/ppermute | solution.py:75
  84.7 1.3 %collective-permute-start.22 = (bf16[128,384]{1,0:T(8,128)(2,1)S(1)}, bf16[128,384]{1,0:T(8,128)(2,1)S(1)}, u32[]{:S(2)}, u32[]{:S(2)}) collective-permute-start(bf16[128,384]{1,0:T(8,128)(2,1)S(1)} %get-tuple-element.71), channel_id=1, source_target_pairs={{32,0},{33,1},{34,2},{35,3},{36,4},{37,5},{38,6},{39,7},{40,8},{41... | collective-permute-start | bytes 294920 | tf_op jit(solution)/shard_map/ppermute | solution.py:75
  86.0 1.3 %collective-permute-start.23 = (bf16[128,384]{1,0:T(8,128)(2,1)S(1)}, bf16[128,384]{1,0:T(8,128)(2,1)S(1)}, u32[]{:S(2)}, u32[]{:S(2)}) collective-permute-start(bf16[128,384]{1,0:T(8,128)(2,1)S(1)} %get-tuple-element.72), channel_id=1, source_target_pairs={{32,64},{33,65},{34,66},{35,67},{36,68},{37,69},{38,70},{39,71},{4... | collective-permute-start | bytes 294920 | tf_op jit(solution)/shard_map/ppermute | solution.py:75
  89.1 16.6 %collective-permute-done.22.a = bf16[128,384]{1,0:T(8,128)(2,1)S(1)} collective-permute-done((bf16[128,384]{1,0:T(8,128)(2,1)S(1)}, bf16[128,384]{1,0:T(8,128)(2,1)S(1)}, u32[]{:S(2)}, u32[]{:S(2)}) %collective-permute-start.22) | collective-permute-done | bytes 98336 | tf_op jit(solution)/shard_map/ppermute | solution.py:75
  (54 shorter events, 12.7 us)
Async XLA Ops:
  0.6 10.2 %copy-start = (bf16[2,2,8,96,160]{3,4,2,1,0:T(8,128)(2,1)S(1)}, bf16[2,2,8,96,160]{3,4,2,1,0:T(8,128)(2,1)}, u32[]{:S(2)}) copy-start(bf16[2,2,8,96,160]{3,4,2,1,0:T(8,128)(2,1)} %param.13) | copy-start | bytes 2949124
  0.6 10.2 %copy-start.2 = (bf16[2,2,160,96]{3,2,1,0:T(8,128)(2,1)S(1)}, bf16[2,2,160,96]{3,2,1,0:T(8,128)(2,1)}, u32[]{:S(2)}) copy-start(bf16[2,2,160,96]{3,2,1,0:T(8,128)(2,1)} %interp.20) | copy-start | bytes 368644
  0.7 10.2 %copy-start.3 = (f32[2,2,256,384]{3,2,1,0:T(8,128)S(1)}, f32[2,2,256,384]{3,2,1,0:T(8,128)}, u32[]{:S(2)}) copy-start(f32[2,2,256,384]{3,2,1,0:T(8,128)} %rhs.3) | copy-start | bytes 4718596
  0.7 10.2 %copy-start.7 = (s32[2,2,256]{2,1,0:T(2,128)S(1)}, s32[2,2,256]{2,1,0:T(2,128)}, u32[]{:S(2)}) copy-start(s32[2,2,256]{2,1,0:T(2,128)} %perm.4) | copy-start | bytes 12292
  2.6 11.2 %collective-permute-start.3 = (bf16[5,160,96]{2,1,0:T(8,128)(2,1)S(1)}, bf16[5,160,96]{2,1,0:T(8,128)(2,1)S(1)}, u32[]{:S(2)}, u32[]{:S(2)}) collective-permute-start(bf16[5,160,96]{2,1,0:T(8,128)(2,1)S(1)} %get-tuple-element.47), channel_id=1, source_target_pairs={{0,32},{1,33},{2,34},{3,35},{4,36},{5,37},{6,38},{7,39},{8,40},{9,... | collective-permute-start | bytes 460808 | tf_op jit(solution)/shard_map/ppermute | solution.py:75
  6.4 6.8 %collective-permute-start = (bf16[160,384]{1,0:T(8,128)(2,1)S(1)}, bf16[160,384]{1,0:T(8,128)(2,1)S(1)}, u32[]{:S(2)}, u32[]{:S(2)}) collective-permute-start(bf16[160,384]{1,0:T(8,128)(2,1)S(1)} %get-tuple-element.38.z.left), channel_id=1, source_target_pairs={{1,0},{2,1},{3,2},{4,3},{5,4},{6,5},{7,6},{8,7},{9,8},{10,9},{11,1... | collective-permute-start | bytes 368648 | tf_op jit(solution)/shard_map/ppermute | solution.py:75
  14.1 15.5 %collective-permute-start.4 = (bf16[192,384]{1,0:T(8,128)(2,1)S(1)}, bf16[192,384]{1,0:T(8,128)(2,1)S(1)}, u32[]{:S(2)}, u32[]{:S(2)}) collective-permute-start(bf16[192,384]{1,0:T(8,128)(2,1)S(1)} %shard_map.116), channel_id=1, source_target_pairs={{32,0},{33,1},{34,2},{35,3},{36,4},{37,5},{38,6},{39,7},{40,8},{41... | collective-permute-start | bytes 442376 | tf_op jit(solution)/shard_map/ppermute | solution.py:75
  16.1 8.3 %collective-permute-start.1 = (bf16[160,384]{1,0:T(8,128)(2,1)S(1)}, bf16[160,384]{1,0:T(8,128)(2,1)S(1)}, u32[]{:S(2)}, u32[]{:S(2)}) collective-permute-start(bf16[160,384]{1,0:T(8,128)(2,1)S(1)} %get-tuple-element.44.refs_0_.own), channel_id=1, source_target_pairs={{0,1},{1,2},{2,3},{3,4},{4,5},{5,6},{6,7},{7,8},{8,9},{9,10},{10,1... | collective-permute-start | bytes 368648 | tf_op jit(solution)/shard_map/ppermute | solution.py:75
  18.1 11.5 %collective-permute-start.2 = (bf16[160,384]{1,0:T(8,128)(2,1)S(1)}, bf16[160,384]{1,0:T(8,128)(2,1)S(1)}, u32[]{:S(2)}, u32[]{:S(2)}) collective-permute-start(bf16[160,384]{1,0:T(8,128)(2,1)S(1)} %get-tuple-element.44.refs_0_.own), channel_id=1, source_target_pairs={{32,1},{33,2},{34,3},{35,4},{36,5},{37,6},{38,7},{39,8},{40,9},{41... | collective-permute-start | bytes 368648 | tf_op jit(solution)/shard_map/ppermute | solution.py:75
  30.2 8.9 %collective-permute-start.8 = (bf16[5,160,96]{2,1,0:T(8,128)(2,1)S(1)}, bf16[5,160,96]{2,1,0:T(8,128)(2,1)S(1)}, u32[]{:S(2)}, u32[]{:S(2)}) collective-permute-start(bf16[5,160,96]{2,1,0:T(8,128)(2,1)S(1)} %get-tuple-element.54), channel_id=1, source_target_pairs={{32,0},{33,1},{34,2},{35,3},{36,4},{37,5},{38,6},{39,7},{40,8},{41... | collective-permute-start | bytes 460808 | tf_op jit(solution)/shard_map/ppermute | solution.py:75
  32.1 5.0 %collective-permute-start.5 = (bf16[160,384]{1,0:T(8,128)(2,1)S(1)}, bf16[160,384]{1,0:T(8,128)(2,1)S(1)}, u32[]{:S(2)}, u32[]{:S(2)}) collective-permute-start(bf16[160,384]{1,0:T(8,128)(2,1)S(1)} %get-tuple-element.49.refs_0_.left), channel_id=1, source_target_pairs={{1,0},{2,1},{3,2},{4,3},{5,4},{6,5},{7,6},{8,7},{9,8},{10,9},{11,1... | collective-permute-start | bytes 368648 | tf_op jit(solution)/shard_map/ppermute | solution.py:75
  35.0 14.0 %copy-start.8 = (s32[1,1,384]{2,1,0:T(1,128)S(1)}, s32[1,1,384]{2,1,0:T(1,128)}, u32[]{:S(2)}) copy-start(s32[1,1,384]{2,1,0:T(1,128)} %perm.5) | copy-start | bytes 4612
  40.1 16.7 %collective-permute-start.9 = (bf16[192,384]{1,0:T(8,128)(2,1)}, bf16[192,384]{1,0:T(8,128)(2,1)S(1)}, u32[]{:S(2)}, u32[]{:S(2)}) collective-permute-start(bf16[192,384]{1,0:T(8,128)(2,1)} %shard_map.121), channel_id=1, source_target_pairs={{0,32},{1,33},{2,34},{3,35},{4,36},{5,37},{6,38},{7,39},{8,40},{9,... | collective-permute-start | bytes 442376 | tf_op jit(solution)/shard_map/ppermute | solution.py:75
  45.2 8.3 %collective-permute-start.6 = (bf16[160,384]{1,0:T(8,128)(2,1)S(1)}, bf16[160,384]{1,0:T(8,128)(2,1)S(1)}, u32[]{:S(2)}, u32[]{:S(2)}) collective-permute-start(bf16[160,384]{1,0:T(8,128)(2,1)S(1)} %get-tuple-element.53.own.refs_0_), channel_id=1, source_target_pairs={{0,1},{1,2},{2,3},{3,4},{4,5},{5,6},{6,7},{7,8},{8,9},{9,10},{10,1... | collective-permute-start | bytes 368648 | tf_op jit(solution)/shard_map/ppermute | solution.py:75
  47.1 9.7 %collective-permute-start.7 = (bf16[160,384]{1,0:T(8,128)(2,1)S(1)}, bf16[160,384]{1,0:T(8,128)(2,1)S(1)}, u32[]{:S(2)}, u32[]{:S(2)}) collective-permute-start(bf16[160,384]{1,0:T(8,128)(2,1)S(1)} %get-tuple-element.53.own.refs_0_), channel_id=1, source_target_pairs={{0,33},{1,34},{2,35},{3,36},{4,37},{5,38},{6,39},{7,40},{8,41},{9,... | collective-permute-start | bytes 368648 | tf_op jit(solution)/shard_map/ppermute | solution.py:75
  49.2 7.5 %copy-start.5 = (bf16[1,1,256,256]{3,2,1,0:T(8,128)(2,1)S(1)}, bf16[1,1,256,256]{3,2,1,0:T(8,128)(2,1)}, u32[]{:S(2)}) copy-start(bf16[1,1,256,256]{3,2,1,0:T(8,128)(2,1)} %piv.15) | copy-start | bytes 393220
  49.3 7.5 %copy-start.6 = (bf16[1,1,256,128]{3,2,1,0:T(8,128)(2,1)S(1)}, bf16[1,1,256,128]{3,2,1,0:T(8,128)(2,1)}, u32[]{:S(2)}) copy-start(bf16[1,1,256,128]{3,2,1,0:T(8,128)(2,1)} %interp.25) | copy-start | bytes 196612
  49.6 17.9 %copy-start.1 = (bf16[1,1,8,128,256]{4,3,2,1,0:T(8,128)(2,1)S(1)}, bf16[1,1,8,128,256]{4,3,2,1,0:T(8,128)(2,1)}, u32[]{:S(2)}) copy-start(bf16[1,1,8,128,256]{4,3,2,1,0:T(8,128)(2,1)} %couple.7) | copy-start | bytes 1572868
  58.0 9.5 %collective-permute-start.10 = (bf16[256,384]{1,0:T(8,128)(2,1)S(1)}, bf16[256,384]{1,0:T(8,128)(2,1)S(1)}, u32[]{:S(2)}, u32[]{:S(2)}) collective-permute-start(bf16[256,384]{1,0:T(8,128)(2,1)S(1)} %get-tuple-element.58.ze.z0), channel_id=1, source_target_pairs={{0,1},{2,3},{4,5},{6,7},{8,9},{10,11},{12,13},{14,15},{16,17},{18,... | collective-permute-start | bytes 589832 | tf_op jit(solution)/shard_map/ppermute | solution.py:75
  59.3 8.2 %collective-permute-start.11 = (bf16[256,384]{1,0:T(8,128)(2,1)S(1)}, bf16[256,384]{1,0:T(8,128)(2,1)S(1)}, u32[]{:S(2)}, u32[]{:S(2)}) collective-permute-start(bf16[256,384]{1,0:T(8,128)(2,1)S(1)} %get-tuple-element.58.ze.z0), channel_id=1, source_target_pairs={{2,1},{4,3},{6,5},{8,7},{10,9},{12,11},{14,13},{16,15},{18,17},{20... | collective-permute-start | bytes 589832 | tf_op jit(solution)/shard_map/ppermute | solution.py:75
  61.6 8.5 %collective-permute-start.12 = (bf16[3,128,256]{2,1,0:T(8,128)(2,1)S(1)}, bf16[3,128,256]{2,1,0:T(8,128)(2,1)S(1)}, u32[]{:S(2)}, u32[]{:S(2)}) collective-permute-start(bf16[3,128,256]{2,1,0:T(8,128)(2,1)S(1)} %get-tuple-element.60), channel_id=1, source_target_pairs={{0,32},{1,33},{2,34},{3,35},{4,36},{5,37},{6,38},{7,39},{8,40},{9,... | collective-permute-start | bytes 589832 | tf_op jit(solution)/shard_map/ppermute | solution.py:75
  63.6 9.5 %collective-permute-start.13 = (bf16[3,128,256]{2,1,0:T(8,128)(2,1)S(1)}, bf16[3,128,256]{2,1,0:T(8,128)(2,1)S(1)}, u32[]{:S(2)}, u32[]{:S(2)}) collective-permute-start(bf16[3,128,256]{2,1,0:T(8,128)(2,1)S(1)} %get-tuple-element.61), channel_id=1, source_target_pairs={{32,0},{33,1},{34,2},{35,3},{36,4},{37,5},{38,6},{39,7},{40,8},{41... | collective-permute-start | bytes 589832 | tf_op jit(solution)/shard_map/ppermute | solution.py:75
  67.6 9.1 %collective-permute-start.14 = (bf16[256,384]{1,0:T(8,128)(2,1)S(1)}, bf16[256,384]{1,0:T(8,128)(2,1)S(1)}, u32[]{:S(2)}, u32[]{:S(2)}) collective-permute-start(bf16[256,384]{1,0:T(8,128)(2,1)S(1)} %get-tuple-element.62.zo.z1), channel_id=1, source_target_pairs={{1,2},{3,4},{5,6},{7,8},{9,10},{11,12},{13,14},{15,16},{17,18},{19... | collective-permute-start | bytes 589832 | tf_op jit(solution)/shard_map/ppermute | solution.py:75
  68.9 7.8 %collective-permute-start.15 = (bf16[256,384]{1,0:T(8,128)(2,1)S(1)}, bf16[256,384]{1,0:T(8,128)(2,1)S(1)}, u32[]{:S(2)}, u32[]{:S(2)}) collective-permute-start(bf16[256,384]{1,0:T(8,128)(2,1)S(1)} %get-tuple-element.62.zo.z1), channel_id=1, source_target_pairs={{1,0},{3,2},{5,4},{7,6},{9,8},{11,10},{13,12},{15,14},{17,16},{19,... | collective-permute-start | bytes 589832 | tf_op jit(solution)/shard_map/ppermute | solution.py:75
  77.0 3.5 %collective-permute-start.16 = (bf16[128,384]{1,0:T(8,128)(2,1)S(1)}, bf16[128,384]{1,0:T(8,128)(2,1)S(1)}, u32[]{:S(2)}, u32[]{:S(2)}) collective-permute-start(bf16[128,384]{1,0:T(8,128)(2,1)S(1)} %get-tuple-element.63), channel_id=1, source_target_pairs={{64,32},{65,33},{66,34},{67,35},{68,36},{69,37},{70,38},{71,39},{7... | collective-permute-start | bytes 294920 | tf_op jit(solution)/shard_map/ppermute | solution.py:75
  78.3 3.5 %collective-permute-start.17 = (bf16[128,384]{1,0:T(8,128)(2,1)S(1)}, bf16[128,384]{1,0:T(8,128)(2,1)S(1)}, u32[]{:S(2)}, u32[]{:S(2)}) collective-permute-start(bf16[128,384]{1,0:T(8,128)(2,1)S(1)} %get-tuple-element.64), channel_id=1, source_target_pairs={{0,32},{1,33},{2,34},{3,35},{4,36},{5,37},{6,38},{7,39},{8,40},{9,... | collective-permute-start | bytes 294920 | tf_op jit(solution)/shard_map/ppermute | solution.py:75
  81.9 1.4 %collective-permute-start.18 = (bf16[256,384]{1,0:T(8,128)(2,1)S(1)}, bf16[256,384]{1,0:T(8,128)(2,1)S(1)}, u32[]{:S(2)}, u32[]{:S(2)}) collective-permute-start(bf16[256,384]{1,0:T(8,128)(2,1)S(1)} %get-tuple-element.66.z2.ze), channel_id=1, source_target_pairs={{32,33},{34,35},{36,37},{38,39},{40,41},{42,43},{44,45},{46,47},{4... | collective-permute-start | bytes 589832 | tf_op jit(solution)/shard_map/ppermute | solution.py:75
  82.5 0.7 collective-permute-start.19
  83.3 1.4 %collective-permute-start.20 = (bf16[256,384]{1,0:T(8,128)(2,1)S(1)}, bf16[256,384]{1,0:T(8,128)(2,1)S(1)}, u32[]{:S(2)}, u32[]{:S(2)}) collective-permute-start(bf16[256,384]{1,0:T(8,128)(2,1)S(1)} %get-tuple-element.68.z3.zo), channel_id=1, source_target_pairs={{33,34},{35,36},{37,38},{39,40},{41,42},{43,44},{45,46},{47,48},{4... | collective-permute-start | bytes 589832 | tf_op jit(solution)/shard_map/ppermute | solution.py:75
  84.0 0.7 collective-permute-start.21
  84.7 21.1 %collective-permute-start.22 = (bf16[128,384]{1,0:T(8,128)(2,1)S(1)}, bf16[128,384]{1,0:T(8,128)(2,1)S(1)}, u32[]{:S(2)}, u32[]{:S(2)}) collective-permute-start(bf16[128,384]{1,0:T(8,128)(2,1)S(1)} %get-tuple-element.71), channel_id=1, source_target_pairs={{32,0},{33,1},{34,2},{35,3},{36,4},{37,5},{38,6},{39,7},{40,8},{41... | collective-permute-start | bytes 294920 | tf_op jit(solution)/shard_map/ppermute | solution.py:75
  86.0 19.8 %collective-permute-start.23 = (bf16[128,384]{1,0:T(8,128)(2,1)S(1)}, bf16[128,384]{1,0:T(8,128)(2,1)S(1)}, u32[]{:S(2)}, u32[]{:S(2)}) collective-permute-start(bf16[128,384]{1,0:T(8,128)(2,1)S(1)} %get-tuple-element.72), channel_id=1, source_target_pairs={{32,64},{33,65},{34,66},{35,67},{36,68},{37,69},{38,70},{39,71},{4... | collective-permute-start | bytes 294920 | tf_op jit(solution)/shard_map/ppermute | solution.py:75
  (1 other events, 2.4 us)

commit v2 on v1

--- a/solution.py
+++ b/solution.py
@@ -20,7 +20,6 @@
 PAR_S, PAR_R, PAR_Z, PAR_M = ((S2, K), F32), ((R2, K), F32), ((R2, K), BF16), ((S2, K), BF16)
 
 
-UP_TERMS = [((1, 0), (6, 7)), ((1, 1), (5, 6, 7))]
 DOWN_TERMS = [((0, 0), (1, 2)), ((0, 1), (0, 1, 2))]
 
 
@@ -44,7 +43,7 @@
     return dot_t(pick, high) + dot_t(pick, low)
 
 
-SMEM, VMEM, HBM = (pl.BlockSpec(memory_space=s) for s in (pltpu.SMEM, pltpu.VMEM, pltpu.HBM))
+SMEM, VMEM, ANY, HBM = (pl.BlockSpec(memory_space=s) for s in (pltpu.SMEM, pltpu.VMEM, pl.ANY, pltpu.HBM))
 
 
 def call(body, ins, outs, specs=(), scratch=(), alias=None):
@@ -79,27 +78,29 @@
     return lax.optimization_barrier((x, value))
 
 
-def first_body(rhs, perm, interp, piv, couple, top, z_out, skel_out, up_out, down_out, below_out, above_out, *rest):
-    x, p, t, v, sems = rest
+def first_body(rhs, perm, interp, piv, z_out, skel_out, x, p, t, v, sems):
     jobs = [(rhs.at[0, 0], x), (perm, p), (interp.at[0, 0], t), (piv.at[0, 0], v)]
-    for terms, out in ((UP_TERMS, up_out), (DOWN_TERMS, down_out)):
-        at = 0
-        for (i, j), ks in terms:
-            jobs.append((couple.at[i, j, pl.ds(ks[0], len(ks))], out.at[pl.ds(at, len(ks))]))
-            at += len(ks)
-    jobs.append((top.at[0, 0, pl.ds(5, 3)], below_out))
-    jobs.append((top.at[0, 0, pl.ds(0, 3)], above_out))
     copies = [pltpu.make_async_copy(a, b, sems.at[n]) for n, (a, b) in enumerate(jobs)]
     for c in copies:
         c.start()
-    for c in copies[:4]:
+    for c in copies:
         c.wait()
     leaf = reordered(x[...], p[0, 0:1, :], P1)
     skel = leaf[:S1]
     diff = leaf[S1:] - dot(t[...], skel.astype(BF16))
     z_out[...] = dot(v[...], diff.astype(BF16)).astype(BF16)
     skel_out[...] = skel
-    for c in copies[4:]:
+
+
+def pack_body(couple, top, tie, down_out, below_out, above_out, sems):
+    jobs, at = [(top.at[0, 0, pl.ds(5, 3)], below_out), (top.at[0, 0, pl.ds(0, 3)], above_out)], 0
+    for (i, j), ks in DOWN_TERMS:
+        jobs.append((couple.at[i, j, pl.ds(ks[0], len(ks))], down_out.at[pl.ds(at, len(ks))]))
+        at += len(ks)
+    copies = [pltpu.make_async_copy(a, b, sems.at[n]) for n, (a, b) in enumerate(jobs)]
+    for c in copies:
+        c.start()
+    for c in copies:
         c.wait()
 
 
@@ -117,12 +118,10 @@
         skels[n] = acc
 
 
-def solve_body(colour, ks, part, interp, piv, couple, skels, reds, *rest):
-    zs, (*arrived, z_out, out) = rest[: len(ks)], rest[len(ks) :]
+def solve_body(colour, ks, interp, piv, couple, skels, reds, *rest):
+    *zs, z_out, out = rest
     i, j = BOXES[colour]
     acc = skels[colour]
-    if part is not None:
-        acc = acc - arrived[0][part * S1 : (part + 1) * S1].astype(F32)
     for k, z in zip(ks, zs):
         acc = acc - dot_t(couple[i, j, k], z[...])
     diff = reds[colour - 1] - dot(interp[i, j], acc.astype(BF16))
@@ -142,15 +141,13 @@
         out[n * S1 : (n + 1) * S1] = total.astype(BF16)
 
 
-def update_body(own, jobs, n_z, part, interp, couple, *refs):
-    zs, (skels, *arrived, out) = refs[:n_z], refs[n_z:]
+def update_body(own, jobs, n_z, interp, couple, *refs):
+    zs, (skels, out) = refs[:n_z], refs[n_z:]
     for n in range(4):
         i, j = BOXES[n]
         acc = skels[n]
         if n == own:
             acc = acc - dot_t(interp[i, j], zs[0][...])
-        if part == n:
-            acc = acc - arrived[0][S1 : 2 * S1].astype(F32)
         for k, at in jobs[n]:
             acc = acc - dot_t(couple[i, j, k], zs[at][...])
         out[n] = acc
@@ -176,66 +173,65 @@
     have = {}
     here = (0, 0)
 
-    def solve(colour, keys, skels, reds, arrived=None, part=None):
+    def solve(colour, keys, skels, reds):
         box = BOXES[colour]
         ks, zs = [], []
         for k in range(8):
             if source(box, k) in keys:
                 ks.append(k)
                 zs.append(have[source(box, k)])
-        ins = [interp1, pivinv1, couple1, skels, reds, *zs] + ([arrived] if arrived is not None else [])
-        body = functools.partial(solve_body, colour, ks, part)
-        z, skels = call(body, ins, [LEAF_Z, LEAF_S])
+        body = functools.partial(solve_body, colour, ks)
+        z, skels = call(body, [interp1, pivinv1, couple1, skels, reds, *zs], [LEAF_Z, LEAF_S])
         have[(colour, here)] = z
         return z, skels
 
     def total(terms, left, own, right, mats):
         return call(functools.partial(sum_body, terms), [left, own, right, mats], [LEAF_M])[0]
 
-    def update(own, keys, skels, drop=(), arrived=None, part=None):
+    def update(own, keys, skels, drop=()):
         order = [(own, here), *keys]
-        ins = [interp1, couple1, *[have[key] for key in order], skels] + ([arrived] if arrived is not None else [])
-        body = functools.partial(update_body, own, jobs_of(order, drop), len(order), part)
-        return call(body, ins, [LEAF_S])[0]
-
-    z00, skel0, up_pack, down_pack, below_pack, above_pack = call(
+        body = functools.partial(update_body, own, jobs_of(order, drop), len(order))
+        return call(body, [interp1, couple1, *[have[key] for key in order], skels], [LEAF_S])[0]
+
+    z00, skel0 = call(
         first_body,
-        [pltpu.with_memory_space_constraint(x, pltpu.HBM) for x in (rhs, perm1, interp1, pivinv1, couple1, couple2)],
-        [LEAF_Z, ((S1, K), F32), LEAF_W, LEAF_W, PAR_W, PAR_W],
-        specs=[HBM] * 6,
+        [pltpu.with_memory_space_constraint(x, pltpu.HBM) for x in (rhs, perm1, interp1, pivinv1)],
+        [LEAF_Z, ((S1, K), F32)],
+        specs=[HBM] * 4,
         scratch=[
             pltpu.VMEM((P1, K), F32),
             pltpu.VMEM((2, 2, P1), jnp.int32),
             pltpu.VMEM((R1, S1), BF16),
             pltpu.VMEM((R1, R1), BF16),
-            pltpu.SemaphoreType.DMA((4 + 4 + 2,)),
+            pltpu.SemaphoreType.DMA((4,)),
         ],
     )
     have[(0, here)] = z00
-    z00r = have[(0, (0, 1))] = shift(z00, (0, -1))
-    up_mats = shift(up_pack, (1, 0))
+    have[(0, (0, 1))] = shift(z00, (0, -1))
+    have[(0, (1, 0))] = shift(z00, (-1, 0))
+    down_pack, below_pack, above_pack = call(
+        pack_body,
+        [*[pltpu.with_memory_space_constraint(x, pltpu.HBM) for x in (couple1, couple2)], z00],
+        [LEAF_W, PAR_W, PAR_W],
+        specs=[HBM, HBM, ANY],
+        scratch=[pltpu.SemaphoreType.DMA((4,))],
+    )
+    down_mats = shift(down_pack, (-1, 0))
     skels, reds = call(spread_body, [rhs, perm1, interp1, couple1, z00, skel0], [LEAF_S, LEAF_R])
     z01, skels = solve(1, {(0, (0, 1))}, skels, reds)
+    have[(1, (1, 0))] = shift(z01, (-1, 0))
     have[(1, (1, -1))] = shift(z01, (-1, 1))
-    from_below = shift(total(UP_TERMS, z00, z01, z00r, up_mats), (-1, 0))
     have[(1, (0, -1))] = shift(z01, (0, 1))
-    below_pack, z01 = after(below_pack, z01)
-    have[(1, here)] = z01
-    above_mats = shift(below_pack, (1, 0))
     skels = update(1, [(0, (0, 1))], skels, drop=[(1, (0, (0, 1)))])
-    z10, skels = solve(2, {(1, (0, -1)), (1, (1, -1))}, skels, reds, arrived=from_below, part=0)
+    below = [(1, (0, -1)), (1, (1, 0)), (0, (1, 0))]
+    z10, skels = solve(2, {*below, (1, (1, -1))}, skels, reds)
     z10r = have[(2, (0, 1))] = shift(z10, (0, -1))
-    down_pack, z10 = after(down_pack, z10)
-    have[(2, here)] = z10
-    down_mats = shift(down_pack, (-1, 0))
-    skels = update(2, [(1, (0, -1))], skels, drop=[(2, (1, (0, -1)))], arrived=from_below, part=3)
-    z11, skels = solve(3, {(2, (0, 1))}, skels, reds)
+    have[(0, (1, 1))] = shift(z00, (-1, -1))
+    skels = update(2, below, skels, drop=[(2, key) for key in below])
+    z11, skels = solve(3, {(2, (0, 1)), (0, (1, 1))}, skels, reds)
     have[(3, (-1, -1))] = shift(z11, (1, 1))
     from_above = shift(total(DOWN_TERMS, z10, z11, z10r, down_mats), (1, 0))
     have[(3, (0, -1))] = shift(z11, (0, 1))
-    above_pack, z11 = after(above_pack, z11)
-    have[(3, here)] = z11
-    below_mats = shift(above_pack, (-1, 0))
     skels = update(3, [(2, (0, 1))], skels, drop=[(3, (2, (0, 1)))])
     (pick,) = call(pick_body, [perm2], [((P2, P2), BF16)])
     red1 = jnp.stack([z00, z01, z10, z11]).reshape(2, 2, R1, K)
@@ -276,6 +272,9 @@
         specs=[SMEM],
     )
 
+    (below_pack, above_pack), z0 = after([below_pack, above_pack], z0)
+    above_mats, below_mats = shift(below_pack, (1, 0)), shift(above_pack, (-1, 0))
+
     def sides(z, c):
         return shift(z, (0, 1), (c,)), shift(z, (0, -1), (c,))
 

time: 107 us -> 106 us (level)
  the two profiles are of different devices: /device:TPU:70 before, /device:TPU:454 now
where the time goes in v2:
time: 106 us
  starting transfers between devices  54.4 us (51%)
  waiting for transfers between devices  36.4 us (34%)
  Pallas kernels  11 us (10%)
  local copies, waits for them, and re-layouts  1.68 us (2%)
  between operations  1.2 us (1%)
    ppermute x25, starting transfers between devices, shift(): return lax.ppermute(x, ('bx', 'by'), pairs(*to, colours))  54.4 us
    ppermute x25, waiting for transfers between devices, shift(): return lax.ppermute(x, ('bx', 'by'), pairs(*to, colours))  36.4 us
    pallas_call x19, Pallas kernels, call(): pl.pallas_call(body, out_shape=[jax.ShapeDtypeStruct(s, d) for s, d in ou...  11 us
  transfers between devices with their start and end apart: 25, of which 9 were waited for; matrix products, arithmetic and copies ran while one was open for 1% of the time, Pallas kernels for 6%

profile of v2, /device:TPU:454, one launch (start us, length us, event | category | flops | bytes accessed | tf_op | source)
XLA Modules:
  0.0 105.5 jit_solution(5138484557654190175)
XLA Ops:
  0.7 1.8 %shard_map.112 = (bf16[160,384]{1,0:T(8,128)(2,1)S(1)}, f32[96,384]{1,0:T(8,128)S(1)}) custom-call(f32[2,2,256,384]{3,2,1,0:T(8,128)} %rhs.3, s32[2,2,256]{2,1,0:T(2,128)} %perm.4, bf16[2,2,160,96]{3,2,1,0:T(8,128)(2,1)} %interp.20, bf16[2,2,160,160]{3,2,1,0:T(8,128)(2,1)} %piv.11), custom_call_target="tpu_custom_call" | custom-call | flops 300000000 | bytes 2000000 | tf_op jit(solution)/shard_map/pallas_call | solution.py:51
  2.5 4.6 %collective-permute-start = (bf16[160,384]{1,0:T(8,128)(2,1)S(1)}, bf16[160,384]{1,0:T(8,128)(2,1)S(1)}, u32[]{:S(2)}, u32[]{:S(2)}) collective-permute-start(bf16[160,384]{1,0:T(8,128)(2,1)S(1)} %get-tuple-element.34.z.tie), channel_id=1, source_target_pairs={{1,0},{2,1},{3,2},{4,3},{5,4},{6,5},{7,6},{8,7},{9,8},{10,9},{11,1... | collective-permute-start | bytes 368648 | tf_op jit(solution)/shard_map/ppermute | solution.py:74
  7.1 2.9 %collective-permute-start.3 = (bf16[160,384]{1,0:T(8,128)(2,1)S(1)}, bf16[160,384]{1,0:T(8,128)(2,1)S(1)}, u32[]{:S(2)}, u32[]{:S(2)}) collective-permute-start(bf16[160,384]{1,0:T(8,128)(2,1)S(1)} %get-tuple-element.34.z.tie), channel_id=1, source_target_pairs={{32,0},{33,1},{34,2},{35,3},{36,4},{37,5},{38,6},{39,7},{40,8},{41... | collective-permute-start | bytes 368648 | tf_op jit(solution)/shard_map/ppermute | solution.py:74
  10.1 1.4 %copy-done.4 = f32[2,2,256,384]{3,2,1,0:T(8,128)S(1)} copy-done((f32[2,2,256,384]{3,2,1,0:T(8,128)S(1)}, f32[2,2,256,384]{3,2,1,0:T(8,128)}, u32[]{:S(2)}) %copy-start.4) | copy-done | bytes 1572888
  13.0 2.1 %collective-permute-start.1 = (bf16[160,384]{1,0:T(8,128)(2,1)S(1)}, bf16[160,384]{1,0:T(8,128)(2,1)S(1)}, u32[]{:S(2)}, u32[]{:S(2)}) collective-permute-start(bf16[160,384]{1,0:T(8,128)(2,1)S(1)} %get-tuple-element.38.refs_0_), channel_id=1, source_target_pairs={{0,1},{1,2},{2,3},{3,4},{4,5},{5,6},{6,7},{7,8},{8,9},{9,10},{10,1... | collective-permute-start | bytes 368648 | tf_op jit(solution)/shard_map/ppermute | solution.py:74
  15.1 2.9 %collective-permute-start.4 = (bf16[160,384]{1,0:T(8,128)(2,1)S(1)}, bf16[160,384]{1,0:T(8,128)(2,1)S(1)}, u32[]{:S(2)}, u32[]{:S(2)}) collective-permute-start(bf16[160,384]{1,0:T(8,128)(2,1)S(1)} %get-tuple-element.38.refs_0_), channel_id=1, source_target_pairs={{32,0},{33,1},{34,2},{35,3},{36,4},{37,5},{38,6},{39,7},{40,8},{41... | collective-permute-start | bytes 368648 | tf_op jit(solution)/shard_map/ppermute | solution.py:74
  18.0 2.4 %collective-permute-start.2 = (bf16[160,384]{1,0:T(8,128)(2,1)S(1)}, bf16[160,384]{1,0:T(8,128)(2,1)S(1)}, u32[]{:S(2)}, u32[]{:S(2)}) collective-permute-start(bf16[160,384]{1,0:T(8,128)(2,1)S(1)} %get-tuple-element.38.refs_0_), channel_id=1, source_target_pairs={{32,1},{33,2},{34,3},{35,4},{36,5},{37,6},{38,7},{39,8},{40,9},{41... | collective-permute-start | bytes 368648 | tf_op jit(solution)/shard_map/ppermute | solution.py:74
  20.4 7.3 %collective-permute-start.6 = (bf16[160,384]{1,0:T(8,128)(2,1)S(1)}, bf16[160,384]{1,0:T(8,128)(2,1)S(1)}, u32[]{:S(2)}, u32[]{:S(2)}) collective-permute-start(bf16[160,384]{1,0:T(8,128)(2,1)S(1)} %get-tuple-element.34.z.tie), channel_id=1, source_target_pairs={{33,0},{34,1},{35,2},{36,3},{37,4},{38,5},{39,6},{40,7},{41,8},{42... | collective-permute-start | bytes 368648 | tf_op jit(solution)/shard_map/ppermute | solution.py:74
  27.8 1.2 %shard_map.120 = (bf16[5,160,96]{2,1,0:T(8,128)(2,1)S(1)}, bf16[3,128,256]{2,1,0:T(8,128)(2,1)S(1)}, bf16[3,128,256]{2,1,0:T(8,128)(2,1)S(1)}) custom-call(bf16[2,2,8,160,96]{4,3,2,1,0:T(8,128)(2,1)} %bitcast.9, bf16[1,1,8,128,256]{4,3,2,1,0:T(8,128)(2,1)} %couple.7, bf16[160,384]{1,0:T(8,128)(2,1)S(1)} %get-tuple-element.34.z.tie), custom_call_target="tpu_custom_call" | custom-call | flops 300000000 | bytes 2000000 | tf_op jit(solution)/shard_map/pallas_call | solution.py:51
  29.3 2.9 %collective-permute-start.9 = (bf16[5,160,96]{2,1,0:T(8,128)(2,1)S(1)}, bf16[5,160,96]{2,1,0:T(8,128)(2,1)S(1)}, u32[]{:S(2)}, u32[]{:S(2)}) collective-permute-start(bf16[5,160,96]{2,1,0:T(8,128)(2,1)S(1)} %get-tuple-element.43), channel_id=1, source_target_pairs={{32,0},{33,1},{34,2},{35,3},{36,4},{37,5},{38,6},{39,7},{40,8},{41... | collective-permute-start | bytes 460808 | tf_op jit(solution)/shard_map/ppermute | solution.py:74
  32.9 2.2 %collective-permute-start.5 = (bf16[160,384]{1,0:T(8,128)(2,1)S(1)}, bf16[160,384]{1,0:T(8,128)(2,1)S(1)}, u32[]{:S(2)}, u32[]{:S(2)}) collective-permute-start(bf16[160,384]{1,0:T(8,128)(2,1)S(1)} %get-tuple-element.40.refs_0_.left), channel_id=1, source_target_pairs={{1,0},{2,1},{3,2},{4,3},{5,4},{6,5},{7,6},{8,7},{9,8},{10,9},{11,1... | collective-permute-start | bytes 368648 | tf_op jit(solution)/shard_map/ppermute | solution.py:74
  35.5 2.0 %collective-permute-done.5.rest_0_.right.refs_1_ = bf16[160,384]{1,0:T(8,128)(2,1)S(1)} collective-permute-done((bf16[160,384]{1,0:T(8,128)(2,1)S(1)}, bf16[160,384]{1,0:T(8,128)(2,1)S(1)}, u32[]{:S(2)}, u32[]{:S(2)}) %collective-permute-start.5) | collective-permute-done | bytes 122912 | tf_op jit(solution)/shard_map/ppermute | solution.py:74
  39.1 2.9 %collective-permute-start.10 = (bf16[192,384]{1,0:T(8,128)(2,1)}, bf16[192,384]{1,0:T(8,128)(2,1)S(1)}, u32[]{:S(2)}, u32[]{:S(2)}) collective-permute-start(bf16[192,384]{1,0:T(8,128)(2,1)} %shard_map.121), channel_id=1, source_target_pairs={{0,32},{1,33},{2,34},{3,35},{4,36},{5,37},{6,38},{7,39},{8,40},{9,... | collective-permute-start | bytes 442376 | tf_op jit(solution)/shard_map/ppermute | solution.py:74
  42.0 1.9 %collective-permute-start.7 = (bf16[160,384]{1,0:T(8,128)(2,1)S(1)}, bf16[160,384]{1,0:T(8,128)(2,1)S(1)}, u32[]{:S(2)}, u32[]{:S(2)}) collective-permute-start(bf16[160,384]{1,0:T(8,128)(2,1)S(1)} %get-tuple-element.42.own.refs_0_), channel_id=1, source_target_pairs={{0,1},{1,2},{2,3},{3,4},{4,5},{5,6},{6,7},{7,8},{8,9},{9,10},{10,1... | collective-permute-start | bytes 368648 | tf_op jit(solution)/shard_map/ppermute | solution.py:74
  44.0 1.9 %collective-permute-start.8 = (bf16[160,384]{1,0:T(8,128)(2,1)S(1)}, bf16[160,384]{1,0:T(8,128)(2,1)S(1)}, u32[]{:S(2)}, u32[]{:S(2)}) collective-permute-start(bf16[160,384]{1,0:T(8,128)(2,1)S(1)} %get-tuple-element.42.own.refs_0_), channel_id=1, source_target_pairs={{0,33},{1,34},{2,35},{3,36},{4,37},{5,38},{6,39},{7,40},{8,41},{9,... | collective-permute-start | bytes 368648 | tf_op jit(solution)/shard_map/ppermute | solution.py:74
  46.5 3.9 %collective-permute-done.7.za = bf16[160,384]{1,0:T(8,128)(2,1)S(1)} collective-permute-done((bf16[160,384]{1,0:T(8,128)(2,1)S(1)}, bf16[160,384]{1,0:T(8,128)(2,1)S(1)}, u32[]{:S(2)}, u32[]{:S(2)}) %collective-permute-start.7) | collective-permute-done | bytes 122912 | tf_op jit(solution)/shard_map/ppermute | solution.py:74
  50.4 3.3 %collective-permute-done.8.zb = bf16[160,384]{1,0:T(8,128)(2,1)S(1)} collective-permute-done((bf16[160,384]{1,0:T(8,128)(2,1)S(1)}, bf16[160,384]{1,0:T(8,128)(2,1)S(1)}, u32[]{:S(2)}, u32[]{:S(2)}) %collective-permute-start.8) | collective-permute-done | bytes 122912 | tf_op jit(solution)/shard_map/ppermute | solution.py:74
  53.7 1.2 %shard_map.123 = (f32[128,384]{1,0:T(8,128)S(1)}, f32[256,384]{1,0:T(8,128)S(1)}, bf16[256,384]{1,0:T(8,128)(2,1)S(1)}) custom-call(s32[1]{0:T(128)} %bitcast.6.me, bf16[384,384]{1,0:T(8,128)(2,1)S(1)} %shard_map.119.pick, bf16[1,1,256,128]{3,2,1,0:T(8,128)(2,1)S(1)} %copy-done.7, bf16[1,1,256,256]{3,2,1,0:T(8,128)(2,1)S(1)} %copy-done.6, ...), custom_call_target="tpu_custom_call" | custom-call | flops 300000000 | bytes 2000000 | tf_op jit(solution)/shard_map/pallas_call | solution.py:51
  54.8 1.3 %collective-permute-start.11 = (bf16[256,384]{1,0:T(8,128)(2,1)S(1)}, bf16[256,384]{1,0:T(8,128)(2,1)S(1)}, u32[]{:S(2)}, u32[]{:S(2)}) collective-permute-start(bf16[256,384]{1,0:T(8,128)(2,1)S(1)} %get-tuple-element.50.ze.z0), channel_id=1, source_target_pairs={{0,1},{2,3},{4,5},{6,7},{8,9},{10,11},{12,13},{14,15},{16,17},{18,... | collective-permute-start | bytes 589832 | tf_op jit(solution)/shard_map/ppermute | solution.py:74
  56.1 2.6 %collective-permute-start.12 = (bf16[256,384]{1,0:T(8,128)(2,1)S(1)}, bf16[256,384]{1,0:T(8,128)(2,1)S(1)}, u32[]{:S(2)}, u32[]{:S(2)}) collective-permute-start(bf16[256,384]{1,0:T(8,128)(2,1)S(1)} %get-tuple-element.50.ze.z0), channel_id=1, source_target_pairs={{2,1},{4,3},{6,5},{8,7},{10,9},{12,11},{14,13},{16,15},{18,17},{20... | collective-permute-start | bytes 589832 | tf_op jit(solution)/shard_map/ppermute | solution.py:74
  58.8 1.9 %collective-permute-start.13 = (bf16[3,128,256]{2,1,0:T(8,128)(2,1)S(1)}, bf16[3,128,256]{2,1,0:T(8,128)(2,1)S(1)}, u32[]{:S(2)}, u32[]{:S(2)}) collective-permute-start(bf16[3,128,256]{2,1,0:T(8,128)(2,1)S(1)} %get-tuple-element.52), channel_id=1, source_target_pairs={{0,32},{1,33},{2,34},{3,35},{4,36},{5,37},{6,38},{7,39},{8,40},{9,... | collective-permute-start | bytes 589832 | tf_op jit(solution)/shard_map/ppermute | solution.py:74
  60.7 3.9 %collective-permute-start.14 = (bf16[3,128,256]{2,1,0:T(8,128)(2,1)S(1)}, bf16[3,128,256]{2,1,0:T(8,128)(2,1)S(1)}, u32[]{:S(2)}, u32[]{:S(2)}) collective-permute-start(bf16[3,128,256]{2,1,0:T(8,128)(2,1)S(1)} %get-tuple-element.53), channel_id=1, source_target_pairs={{32,0},{33,1},{34,2},{35,3},{36,4},{37,5},{38,6},{39,7},{40,8},{41... | collective-permute-start | bytes 589832 | tf_op jit(solution)/shard_map/ppermute | solution.py:74
  64.7 1.3 %collective-permute-start.15 = (bf16[256,384]{1,0:T(8,128)(2,1)S(1)}, bf16[256,384]{1,0:T(8,128)(2,1)S(1)}, u32[]{:S(2)}, u32[]{:S(2)}) collective-permute-start(bf16[256,384]{1,0:T(8,128)(2,1)S(1)} %get-tuple-element.54.zo.z1), channel_id=1, source_target_pairs={{1,2},{3,4},{5,6},{7,8},{9,10},{11,12},{13,14},{15,16},{17,18},{19... | collective-permute-start | bytes 589832 | tf_op jit(solution)/shard_map/ppermute | solution.py:74
  66.0 1.3 %collective-permute-start.16 = (bf16[256,384]{1,0:T(8,128)(2,1)S(1)}, bf16[256,384]{1,0:T(8,128)(2,1)S(1)}, u32[]{:S(2)}, u32[]{:S(2)}) collective-permute-start(bf16[256,384]{1,0:T(8,128)(2,1)S(1)} %get-tuple-element.54.zo.z1), channel_id=1, source_target_pairs={{1,0},{3,2},{5,4},{7,6},{9,8},{11,10},{13,12},{15,14},{17,16},{19,... | collective-permute-start | bytes 589832 | tf_op jit(solution)/shard_map/ppermute | solution.py:74
  68.3 5.5 %collective-permute-done.15.ol.al = bf16[256,384]{1,0:T(8,128)(2,1)S(1)} collective-permute-done((bf16[256,384]{1,0:T(8,128)(2,1)S(1)}, bf16[256,384]{1,0:T(8,128)(2,1)S(1)}, u32[]{:S(2)}, u32[]{:S(2)}) %collective-permute-start.15) | collective-permute-done | bytes 196640 | tf_op jit(solution)/shard_map/ppermute | solution.py:74
  74.2 1.3 %collective-permute-start.17 = (bf16[128,384]{1,0:T(8,128)(2,1)S(1)}, bf16[128,384]{1,0:T(8,128)(2,1)S(1)}, u32[]{:S(2)}, u32[]{:S(2)}) collective-permute-start(bf16[128,384]{1,0:T(8,128)(2,1)S(1)} %get-tuple-element.55), channel_id=1, source_target_pairs={{64,32},{65,33},{66,34},{67,35},{68,36},{69,37},{70,38},{71,39},{7... | collective-permute-start | bytes 294920 | tf_op jit(solution)/shard_map/ppermute | solution.py:74
  75.5 1.3 %collective-permute-start.18 = (bf16[128,384]{1,0:T(8,128)(2,1)S(1)}, bf16[128,384]{1,0:T(8,128)(2,1)S(1)}, u32[]{:S(2)}, u32[]{:S(2)}) collective-permute-start(bf16[128,384]{1,0:T(8,128)(2,1)S(1)} %get-tuple-element.56), channel_id=1, source_target_pairs={{0,32},{1,33},{2,34},{3,35},{4,36},{5,37},{6,38},{7,39},{8,40},{9,... | collective-permute-start | bytes 294920 | tf_op jit(solution)/shard_map/ppermute | solution.py:74
  77.7 1.3 %collective-permute-done.18.rest_1_.rest_3_ = bf16[128,384]{1,0:T(8,128)(2,1)S(1)} collective-permute-done((bf16[128,384]{1,0:T(8,128)(2,1)S(1)}, bf16[128,384]{1,0:T(8,128)(2,1)S(1)}, u32[]{:S(2)}, u32[]{:S(2)}) %collective-permute-start.18) | collective-permute-done | bytes 98336 | tf_op jit(solution)/shard_map/ppermute | solution.py:74
  81.9 1.3 %collective-permute-start.23 = (bf16[128,384]{1,0:T(8,128)(2,1)S(1)}, bf16[128,384]{1,0:T(8,128)(2,1)S(1)}, u32[]{:S(2)}, u32[]{:S(2)}) collective-permute-start(bf16[128,384]{1,0:T(8,128)(2,1)S(1)} %get-tuple-element.63), channel_id=1, source_target_pairs={{32,0},{33,1},{34,2},{35,3},{36,4},{37,5},{38,6},{39,7},{40,8},{41... | collective-permute-start | bytes 294920 | tf_op jit(solution)/shard_map/ppermute | solution.py:74
  83.2 1.3 %collective-permute-start.24 = (bf16[128,384]{1,0:T(8,128)(2,1)S(1)}, bf16[128,384]{1,0:T(8,128)(2,1)S(1)}, u32[]{:S(2)}, u32[]{:S(2)}) collective-permute-start(bf16[128,384]{1,0:T(8,128)(2,1)S(1)} %get-tuple-element.64), channel_id=1, source_target_pairs={{32,64},{33,65},{34,66},{35,67},{36,68},{37,69},{38,70},{39,71},{4... | collective-permute-start | bytes 294920 | tf_op jit(solution)/shard_map/ppermute | solution.py:74
  86.3 14.8 %collective-permute-done.23.a = bf16[128,384]{1,0:T(8,128)(2,1)S(1)} collective-permute-done((bf16[128,384]{1,0:T(8,128)(2,1)S(1)}, bf16[128,384]{1,0:T(8,128)(2,1)S(1)}, u32[]{:S(2)}, u32[]{:S(2)}) %collective-permute-start.23) | collective-permute-done | bytes 98336 | tf_op jit(solution)/shard_map/ppermute | solution.py:74
  101.1 3.7 %collective-permute-done.24.b = bf16[128,384]{1,0:T(8,128)(2,1)S(1)} collective-permute-done((bf16[128,384]{1,0:T(8,128)(2,1)S(1)}, bf16[128,384]{1,0:T(8,128)(2,1)S(1)}, u32[]{:S(2)}, u32[]{:S(2)}) %collective-permute-start.24) | collective-permute-done | bytes 98336 | tf_op jit(solution)/shard_map/ppermute | solution.py:74
  (58 shorter events, 12.6 us)
Async XLA Ops:
  0.6 9.4 %copy-start.8 = (s32[2,2,256]{2,1,0:T(2,128)S(1)}, s32[2,2,256]{2,1,0:T(2,128)}, u32[]{:S(2)}) copy-start(s32[2,2,256]{2,1,0:T(2,128)} %perm.4) | copy-start | bytes 12292
  0.6 9.4 %copy-start.3 = (bf16[2,2,160,96]{3,2,1,0:T(8,128)(2,1)S(1)}, bf16[2,2,160,96]{3,2,1,0:T(8,128)(2,1)}, u32[]{:S(2)}) copy-start(bf16[2,2,160,96]{3,2,1,0:T(8,128)(2,1)} %interp.20) | copy-start | bytes 368644
  0.7 9.4 %copy-start = (bf16[2,2,8,96,160]{3,4,2,1,0:T(8,128)(2,1)S(1)}, bf16[2,2,8,96,160]{3,4,2,1,0:T(8,128)(2,1)}, u32[]{:S(2)}) copy-start(bf16[2,2,8,96,160]{3,4,2,1,0:T(8,128)(2,1)} %param.13) | copy-start | bytes 2949124
  2.5 9.7 %collective-permute-start = (bf16[160,384]{1,0:T(8,128)(2,1)S(1)}, bf16[160,384]{1,0:T(8,128)(2,1)S(1)}, u32[]{:S(2)}, u32[]{:S(2)}) collective-permute-start(bf16[160,384]{1,0:T(8,128)(2,1)S(1)} %get-tuple-element.34.z.tie), channel_id=1, source_target_pairs={{1,0},{2,1},{3,2},{4,3},{5,4},{6,5},{7,6},{8,7},{9,8},{10,9},{11,1... | collective-permute-start | bytes 368648 | tf_op jit(solution)/shard_map/ppermute | solution.py:74
  7.1 22.2 %collective-permute-start.3 = (bf16[160,384]{1,0:T(8,128)(2,1)S(1)}, bf16[160,384]{1,0:T(8,128)(2,1)S(1)}, u32[]{:S(2)}, u32[]{:S(2)}) collective-permute-start(bf16[160,384]{1,0:T(8,128)(2,1)S(1)} %get-tuple-element.34.z.tie), channel_id=1, source_target_pairs={{32,0},{33,1},{34,2},{35,3},{36,4},{37,5},{38,6},{39,7},{40,8},{41... | collective-permute-start | bytes 368648 | tf_op jit(solution)/shard_map/ppermute | solution.py:74
  13.0 16.0 %copy-start.1 = (bf16[2,2,8,96,160]{3,4,2,1,0:T(8,128)(2,1)S(1)}, bf16[2,2,8,96,160]{3,4,2,1,0:T(8,128)(2,1)}, u32[]{:S(2)}) copy-start(bf16[2,2,8,96,160]{3,4,2,1,0:T(8,128)(2,1)} %param.13) | copy-start | bytes 2949124
  13.0 19.2 %collective-permute-start.1 = (bf16[160,384]{1,0:T(8,128)(2,1)S(1)}, bf16[160,384]{1,0:T(8,128)(2,1)S(1)}, u32[]{:S(2)}, u32[]{:S(2)}) collective-permute-start(bf16[160,384]{1,0:T(8,128)(2,1)S(1)} %get-tuple-element.38.refs_0_), channel_id=1, source_target_pairs={{0,1},{1,2},{2,3},{3,4},{4,5},{5,6},{6,7},{7,8},{8,9},{9,10},{10,1... | collective-permute-start | bytes 368648 | tf_op jit(solution)/shard_map/ppermute | solution.py:74
  15.1 17.2 %collective-permute-start.4 = (bf16[160,384]{1,0:T(8,128)(2,1)S(1)}, bf16[160,384]{1,0:T(8,128)(2,1)S(1)}, u32[]{:S(2)}, u32[]{:S(2)}) collective-permute-start(bf16[160,384]{1,0:T(8,128)(2,1)S(1)} %get-tuple-element.38.refs_0_), channel_id=1, source_target_pairs={{32,0},{33,1},{34,2},{35,3},{36,4},{37,5},{38,6},{39,7},{40,8},{41... | collective-permute-start | bytes 368648 | tf_op jit(solution)/shard_map/ppermute | solution.py:74
  18.0 14.3 %collective-permute-start.2 = (bf16[160,384]{1,0:T(8,128)(2,1)S(1)}, bf16[160,384]{1,0:T(8,128)(2,1)S(1)}, u32[]{:S(2)}, u32[]{:S(2)}) collective-permute-start(bf16[160,384]{1,0:T(8,128)(2,1)S(1)} %get-tuple-element.38.refs_0_), channel_id=1, source_target_pairs={{32,1},{33,2},{34,3},{35,4},{36,5},{37,6},{38,7},{39,8},{40,9},{41... | collective-permute-start | bytes 368648 | tf_op jit(solution)/shard_map/ppermute | solution.py:74
  20.4 15.1 %collective-permute-start.6 = (bf16[160,384]{1,0:T(8,128)(2,1)S(1)}, bf16[160,384]{1,0:T(8,128)(2,1)S(1)}, u32[]{:S(2)}, u32[]{:S(2)}) collective-permute-start(bf16[160,384]{1,0:T(8,128)(2,1)S(1)} %get-tuple-element.34.z.tie), channel_id=1, source_target_pairs={{33,0},{34,1},{35,2},{36,3},{37,4},{38,5},{39,6},{40,7},{41,8},{42... | collective-permute-start | bytes 368648 | tf_op jit(solution)/shard_map/ppermute | solution.py:74
  29.3 8.8 %collective-permute-start.9 = (bf16[5,160,96]{2,1,0:T(8,128)(2,1)S(1)}, bf16[5,160,96]{2,1,0:T(8,128)(2,1)S(1)}, u32[]{:S(2)}, u32[]{:S(2)}) collective-permute-start(bf16[5,160,96]{2,1,0:T(8,128)(2,1)S(1)} %get-tuple-element.43), channel_id=1, source_target_pairs={{32,0},{33,1},{34,2},{35,3},{36,4},{37,5},{38,6},{39,7},{40,8},{41... | collective-permute-start | bytes 460808 | tf_op jit(solution)/shard_map/ppermute | solution.py:74
  32.9 4.6 %collective-permute-start.5 = (bf16[160,384]{1,0:T(8,128)(2,1)S(1)}, bf16[160,384]{1,0:T(8,128)(2,1)S(1)}, u32[]{:S(2)}, u32[]{:S(2)}) collective-permute-start(bf16[160,384]{1,0:T(8,128)(2,1)S(1)} %get-tuple-element.40.refs_0_.left), channel_id=1, source_target_pairs={{1,0},{2,1},{3,2},{4,3},{5,4},{6,5},{7,6},{8,7},{9,8},{10,9},{11,1... | collective-permute-start | bytes 368648 | tf_op jit(solution)/shard_map/ppermute | solution.py:74
  35.5 10.4 %copy-start.9 = (s32[1,1,384]{2,1,0:T(1,128)S(1)}, s32[1,1,384]{2,1,0:T(1,128)}, u32[]{:S(2)}) copy-start(s32[1,1,384]{2,1,0:T(1,128)} %perm.5) | copy-start | bytes 4612
  39.1 14.5 %collective-permute-start.10 = (bf16[192,384]{1,0:T(8,128)(2,1)}, bf16[192,384]{1,0:T(8,128)(2,1)S(1)}, u32[]{:S(2)}, u32[]{:S(2)}) collective-permute-start(bf16[192,384]{1,0:T(8,128)(2,1)} %shard_map.121), channel_id=1, source_target_pairs={{0,32},{1,33},{2,34},{3,35},{4,36},{5,37},{6,38},{7,39},{8,40},{9,... | collective-permute-start | bytes 442376 | tf_op jit(solution)/shard_map/ppermute | solution.py:74
  42.0 8.3 %collective-permute-start.7 = (bf16[160,384]{1,0:T(8,128)(2,1)S(1)}, bf16[160,384]{1,0:T(8,128)(2,1)S(1)}, u32[]{:S(2)}, u32[]{:S(2)}) collective-permute-start(bf16[160,384]{1,0:T(8,128)(2,1)S(1)} %get-tuple-element.42.own.refs_0_), channel_id=1, source_target_pairs={{0,1},{1,2},{2,3},{3,4},{4,5},{5,6},{6,7},{7,8},{8,9},{9,10},{10,1... | collective-permute-start | bytes 368648 | tf_op jit(solution)/shard_map/ppermute | solution.py:74
  44.0 9.7 %collective-permute-start.8 = (bf16[160,384]{1,0:T(8,128)(2,1)S(1)}, bf16[160,384]{1,0:T(8,128)(2,1)S(1)}, u32[]{:S(2)}, u32[]{:S(2)}) collective-permute-start(bf16[160,384]{1,0:T(8,128)(2,1)S(1)} %get-tuple-element.42.own.refs_0_), channel_id=1, source_target_pairs={{0,33},{1,34},{2,35},{3,36},{4,37},{5,38},{6,39},{7,40},{8,41},{9,... | collective-permute-start | bytes 368648 | tf_op jit(solution)/shard_map/ppermute | solution.py:74
  46.1 7.5 %copy-start.6 = (bf16[1,1,256,256]{3,2,1,0:T(8,128)(2,1)S(1)}, bf16[1,1,256,256]{3,2,1,0:T(8,128)(2,1)}, u32[]{:S(2)}) copy-start(bf16[1,1,256,256]{3,2,1,0:T(8,128)(2,1)} %piv.15) | copy-start | bytes 393220
  46.5 18.2 %copy-start.2 = (bf16[1,1,8,128,256]{4,3,2,1,0:T(8,128)(2,1)S(1)}, bf16[1,1,8,128,256]{4,3,2,1,0:T(8,128)(2,1)}, u32[]{:S(2)}) copy-start(bf16[1,1,8,128,256]{4,3,2,1,0:T(8,128)(2,1)} %couple.7) | copy-start | bytes 1572868
  54.8 9.8 %collective-permute-start.11 = (bf16[256,384]{1,0:T(8,128)(2,1)S(1)}, bf16[256,384]{1,0:T(8,128)(2,1)S(1)}, u32[]{:S(2)}, u32[]{:S(2)}) collective-permute-start(bf16[256,384]{1,0:T(8,128)(2,1)S(1)} %get-tuple-element.50.ze.z0), channel_id=1, source_target_pairs={{0,1},{2,3},{4,5},{6,7},{8,9},{10,11},{12,13},{14,15},{16,17},{18,... | collective-permute-start | bytes 589832 | tf_op jit(solution)/shard_map/ppermute | solution.py:74
  56.1 8.5 %collective-permute-start.12 = (bf16[256,384]{1,0:T(8,128)(2,1)S(1)}, bf16[256,384]{1,0:T(8,128)(2,1)S(1)}, u32[]{:S(2)}, u32[]{:S(2)}) collective-permute-start(bf16[256,384]{1,0:T(8,128)(2,1)S(1)} %get-tuple-element.50.ze.z0), channel_id=1, source_target_pairs={{2,1},{4,3},{6,5},{8,7},{10,9},{12,11},{14,13},{16,15},{18,17},{20... | collective-permute-start | bytes 589832 | tf_op jit(solution)/shard_map/ppermute | solution.py:74
  58.8 8.5 %collective-permute-start.13 = (bf16[3,128,256]{2,1,0:T(8,128)(2,1)S(1)}, bf16[3,128,256]{2,1,0:T(8,128)(2,1)S(1)}, u32[]{:S(2)}, u32[]{:S(2)}) collective-permute-start(bf16[3,128,256]{2,1,0:T(8,128)(2,1)S(1)} %get-tuple-element.52), channel_id=1, source_target_pairs={{0,32},{1,33},{2,34},{3,35},{4,36},{5,37},{6,38},{7,39},{8,40},{9,... | collective-permute-start | bytes 589832 | tf_op jit(solution)/shard_map/ppermute | solution.py:74
  60.7 7.6 %collective-permute-start.14 = (bf16[3,128,256]{2,1,0:T(8,128)(2,1)S(1)}, bf16[3,128,256]{2,1,0:T(8,128)(2,1)S(1)}, u32[]{:S(2)}, u32[]{:S(2)}) collective-permute-start(bf16[3,128,256]{2,1,0:T(8,128)(2,1)S(1)} %get-tuple-element.53), channel_id=1, source_target_pairs={{32,0},{33,1},{34,2},{35,3},{36,4},{37,5},{38,6},{39,7},{40,8},{41... | collective-permute-start | bytes 589832 | tf_op jit(solution)/shard_map/ppermute | solution.py:74
  64.7 9.1 %collective-permute-start.15 = (bf16[256,384]{1,0:T(8,128)(2,1)S(1)}, bf16[256,384]{1,0:T(8,128)(2,1)S(1)}, u32[]{:S(2)}, u32[]{:S(2)}) collective-permute-start(bf16[256,384]{1,0:T(8,128)(2,1)S(1)} %get-tuple-element.54.zo.z1), channel_id=1, source_target_pairs={{1,2},{3,4},{5,6},{7,8},{9,10},{11,12},{13,14},{15,16},{17,18},{19... | collective-permute-start | bytes 589832 | tf_op jit(solution)/shard_map/ppermute | solution.py:74
  66.0 7.8 %collective-permute-start.16 = (bf16[256,384]{1,0:T(8,128)(2,1)S(1)}, bf16[256,384]{1,0:T(8,128)(2,1)S(1)}, u32[]{:S(2)}, u32[]{:S(2)}) collective-permute-start(bf16[256,384]{1,0:T(8,128)(2,1)S(1)} %get-tuple-element.54.zo.z1), channel_id=1, source_target_pairs={{1,0},{3,2},{5,4},{7,6},{9,8},{11,10},{13,12},{15,14},{17,16},{19,... | collective-permute-start | bytes 589832 | tf_op jit(solution)/shard_map/ppermute | solution.py:74
  74.2 3.5 %collective-permute-start.17 = (bf16[128,384]{1,0:T(8,128)(2,1)S(1)}, bf16[128,384]{1,0:T(8,128)(2,1)S(1)}, u32[]{:S(2)}, u32[]{:S(2)}) collective-permute-start(bf16[128,384]{1,0:T(8,128)(2,1)S(1)} %get-tuple-element.55), channel_id=1, source_target_pairs={{64,32},{65,33},{66,34},{67,35},{68,36},{69,37},{70,38},{71,39},{7... | collective-permute-start | bytes 294920 | tf_op jit(solution)/shard_map/ppermute | solution.py:74
  75.5 3.5 %collective-permute-start.18 = (bf16[128,384]{1,0:T(8,128)(2,1)S(1)}, bf16[128,384]{1,0:T(8,128)(2,1)S(1)}, u32[]{:S(2)}, u32[]{:S(2)}) collective-permute-start(bf16[128,384]{1,0:T(8,128)(2,1)S(1)} %get-tuple-element.56), channel_id=1, source_target_pairs={{0,32},{1,33},{2,34},{3,35},{4,36},{5,37},{6,38},{7,39},{8,40},{9,... | collective-permute-start | bytes 294920 | tf_op jit(solution)/shard_map/ppermute | solution.py:74
  79.0 1.4 %collective-permute-start.19 = (bf16[256,384]{1,0:T(8,128)(2,1)S(1)}, bf16[256,384]{1,0:T(8,128)(2,1)S(1)}, u32[]{:S(2)}, u32[]{:S(2)}) collective-permute-start(bf16[256,384]{1,0:T(8,128)(2,1)S(1)} %get-tuple-element.58.z2.ze), channel_id=1, source_target_pairs={{32,33},{34,35},{36,37},{38,39},{40,41},{42,43},{44,45},{46,47},{4... | collective-permute-start | bytes 589832 | tf_op jit(solution)/shard_map/ppermute | solution.py:74
  79.7 0.7 collective-permute-start.20
  80.4 1.4 %collective-permute-start.21 = (bf16[256,384]{1,0:T(8,128)(2,1)S(1)}, bf16[256,384]{1,0:T(8,128)(2,1)S(1)}, u32[]{:S(2)}, u32[]{:S(2)}) collective-permute-start(bf16[256,384]{1,0:T(8,128)(2,1)S(1)} %get-tuple-element.60.z3.zo), channel_id=1, source_target_pairs={{33,34},{35,36},{37,38},{39,40},{41,42},{43,44},{45,46},{47,48},{4... | collective-permute-start | bytes 589832 | tf_op jit(solution)/shard_map/ppermute | solution.py:74
  81.1 0.7 collective-permute-start.22
  81.9 19.3 %collective-permute-start.23 = (bf16[128,384]{1,0:T(8,128)(2,1)S(1)}, bf16[128,384]{1,0:T(8,128)(2,1)S(1)}, u32[]{:S(2)}, u32[]{:S(2)}) collective-permute-start(bf16[128,384]{1,0:T(8,128)(2,1)S(1)} %get-tuple-element.63), channel_id=1, source_target_pairs={{32,0},{33,1},{34,2},{35,3},{36,4},{37,5},{38,6},{39,7},{40,8},{41... | collective-permute-start | bytes 294920 | tf_op jit(solution)/shard_map/ppermute | solution.py:74
  83.2 21.7 %collective-permute-start.24 = (bf16[128,384]{1,0:T(8,128)(2,1)S(1)}, bf16[128,384]{1,0:T(8,128)(2,1)S(1)}, u32[]{:S(2)}, u32[]{:S(2)}) collective-permute-start(bf16[128,384]{1,0:T(8,128)(2,1)S(1)} %get-tuple-element.64), channel_id=1, source_target_pairs={{32,64},{33,65},{34,66},{35,67},{36,68},{37,69},{38,70},{39,71},{4... | collective-permute-start | bytes 294920 | tf_op jit(solution)/shard_map/ppermute | solution.py:74
  (3 other events, 9.9 us)

commit v3 on v1

--- a/solution.py
+++ b/solution.py
@@ -16,12 +16,22 @@
 F32, BF16 = jnp.float32, jnp.bfloat16
 LEAF_S, LEAF_R, LEAF_Z = ((4, S1, K), F32), ((3, R1, K), F32), ((R1, K), BF16)
 LEAF_W, LEAF_M = ((5, R1, S1), BF16), ((2 * S1, K), BF16)
-PAR_W = ((3, S2, R2), BF16)
 PAR_S, PAR_R, PAR_Z, PAR_M = ((S2, K), F32), ((R2, K), F32), ((R2, K), BF16), ((S2, K), BF16)
 
 
 UP_TERMS = [((1, 0), (6, 7)), ((1, 1), (5, 6, 7))]
 DOWN_TERMS = [((0, 0), (1, 2)), ((0, 1), (0, 1, 2))]
+
+PACKS = {
+    (1, 1): (6, 2, (0, 1)),
+    (1, -1): (5, 1, (1,)),
+    (1, 0): (5, 3, (0, 1, 2)),
+    (-1, 1): (1, 2, (0, 1)),
+    (-1, -1): (0, 1, (1,)),
+    (-1, 0): (0, 3, (0, 1, 2)),
+}
+CORNERS = [(-1, -1), (-1, 1), (1, -1), (1, 1)]
+ENDS = [(-1, 0), (1, 0)]
 
 
 def dot(a, b):
@@ -44,7 +54,7 @@
     return dot_t(pick, high) + dot_t(pick, low)
 
 
-SMEM, VMEM, HBM = (pl.BlockSpec(memory_space=s) for s in (pltpu.SMEM, pltpu.VMEM, pltpu.HBM))
+SMEM, VMEM, ANY, HBM = (pl.BlockSpec(memory_space=s) for s in (pltpu.SMEM, pltpu.VMEM, pl.ANY, pltpu.HBM))
 
 
 def call(body, ins, outs, specs=(), scratch=(), alias=None):
@@ -79,27 +89,31 @@
     return lax.optimization_barrier((x, value))
 
 
-def first_body(rhs, perm, interp, piv, couple, top, z_out, skel_out, up_out, down_out, below_out, above_out, *rest):
-    x, p, t, v, sems = rest
+def first_body(rhs, perm, interp, piv, z_out, skel_out, x, p, t, v, sems):
     jobs = [(rhs.at[0, 0], x), (perm, p), (interp.at[0, 0], t), (piv.at[0, 0], v)]
-    for terms, out in ((UP_TERMS, up_out), (DOWN_TERMS, down_out)):
-        at = 0
-        for (i, j), ks in terms:
-            jobs.append((couple.at[i, j, pl.ds(ks[0], len(ks))], out.at[pl.ds(at, len(ks))]))
-            at += len(ks)
-    jobs.append((top.at[0, 0, pl.ds(5, 3)], below_out))
-    jobs.append((top.at[0, 0, pl.ds(0, 3)], above_out))
     copies = [pltpu.make_async_copy(a, b, sems.at[n]) for n, (a, b) in enumerate(jobs)]
     for c in copies:
         c.start()
-    for c in copies[:4]:
+    for c in copies:
         c.wait()
     leaf = reordered(x[...], p[0, 0:1, :], P1)
     skel = leaf[:S1]
     diff = leaf[S1:] - dot(t[...], skel.astype(BF16))
     z_out[...] = dot(v[...], diff.astype(BF16)).astype(BF16)
     skel_out[...] = skel
-    for c in copies[4:]:
+
+
+def pack_body(couple, tie, up_out, down_out, sems):
+    jobs = []
+    for terms, out in ((UP_TERMS, up_out), (DOWN_TERMS, down_out)):
+        at = 0
+        for (i, j), ks in terms:
+            jobs.append((couple.at[i, j, pl.ds(ks[0], len(ks))], out.at[pl.ds(at, len(ks))]))
+            at += len(ks)
+    copies = [pltpu.make_async_copy(a, b, sems.at[n]) for n, (a, b) in enumerate(jobs)]
+    for c in copies:
+        c.start()
+    for c in copies:
         c.wait()
 
 
@@ -156,9 +170,18 @@
         out[n] = acc
 
 
-def pick_body(perm, pick_out):
+def pick_body(perm, couple, tie, pick_out, *rest):
+    packs, sems = rest[:-1], rest[-1]
+    copies = [
+        pltpu.make_async_copy(couple.at[0, 0, pl.ds(k, n)], out, sems.at[at])
+        for at, ((k, n, _), out) in enumerate(zip(PACKS.values(), packs))
+    ]
+    for c in copies:
+        c.start()
     hit = (lax.broadcasted_iota(jnp.int32, (P2, P2), 0) == perm[0]).astype(F32)
     pick_out[...] = hit.T.astype(BF16)
+    for c in copies:
+        c.wait()
 
 
 def jobs_of(order, drop=()):
@@ -198,46 +221,51 @@
         body = functools.partial(update_body, own, jobs_of(order, drop), len(order), part)
         return call(body, ins, [LEAF_S])[0]
 
-    z00, skel0, up_pack, down_pack, below_pack, above_pack = call(
+    z00, skel0 = call(
         first_body,
-        [pltpu.with_memory_space_constraint(x, pltpu.HBM) for x in (rhs, perm1, interp1, pivinv1, couple1, couple2)],
-        [LEAF_Z, ((S1, K), F32), LEAF_W, LEAF_W, PAR_W, PAR_W],
-        specs=[HBM] * 6,
+        [pltpu.with_memory_space_constraint(x, pltpu.HBM) for x in (rhs, perm1, interp1, pivinv1)],
+        [LEAF_Z, ((S1, K), F32)],
+        specs=[HBM] * 4,
         scratch=[
             pltpu.VMEM((P1, K), F32),
             pltpu.VMEM((2, 2, P1), jnp.int32),
             pltpu.VMEM((R1, S1), BF16),
             pltpu.VMEM((R1, R1), BF16),
-            pltpu.SemaphoreType.DMA((4 + 4 + 2,)),
+            pltpu.SemaphoreType.DMA((4,)),
         ],
     )
     have[(0, here)] = z00
     z00r = have[(0, (0, 1))] = shift(z00, (0, -1))
+    up_pack, down_pack = call(
+        pack_body,
+        [pltpu.with_memory_space_constraint(couple1, pltpu.HBM), z00],
+        [LEAF_W, LEAF_W],
+        specs=[HBM, ANY],
+        scratch=[pltpu.SemaphoreType.DMA((4,))],
+    )
     up_mats = shift(up_pack, (1, 0))
+    down_mats = shift(down_pack, (-1, 0))
     skels, reds = call(spread_body, [rhs, perm1, interp1, couple1, z00, skel0], [LEAF_S, LEAF_R])
     z01, skels = solve(1, {(0, (0, 1))}, skels, reds)
     have[(1, (1, -1))] = shift(z01, (-1, 1))
     from_below = shift(total(UP_TERMS, z00, z01, z00r, up_mats), (-1, 0))
     have[(1, (0, -1))] = shift(z01, (0, 1))
-    below_pack, z01 = after(below_pack, z01)
-    have[(1, here)] = z01
-    above_mats = shift(below_pack, (1, 0))
     skels = update(1, [(0, (0, 1))], skels, drop=[(1, (0, (0, 1)))])
     z10, skels = solve(2, {(1, (0, -1)), (1, (1, -1))}, skels, reds, arrived=from_below, part=0)
     z10r = have[(2, (0, 1))] = shift(z10, (0, -1))
-    down_pack, z10 = after(down_pack, z10)
-    have[(2, here)] = z10
-    down_mats = shift(down_pack, (-1, 0))
     skels = update(2, [(1, (0, -1))], skels, drop=[(2, (1, (0, -1)))], arrived=from_below, part=3)
     z11, skels = solve(3, {(2, (0, 1))}, skels, reds)
     have[(3, (-1, -1))] = shift(z11, (1, 1))
     from_above = shift(total(DOWN_TERMS, z10, z11, z10r, down_mats), (1, 0))
     have[(3, (0, -1))] = shift(z11, (0, 1))
-    above_pack, z11 = after(above_pack, z11)
-    have[(3, here)] = z11
-    below_mats = shift(above_pack, (-1, 0))
     skels = update(3, [(2, (0, 1))], skels, drop=[(3, (2, (0, 1)))])
-    (pick,) = call(pick_body, [perm2], [((P2, P2), BF16)])
+    pick, *packs = call(
+        pick_body,
+        [perm2, pltpu.with_memory_space_constraint(couple2, pltpu.HBM), z11],
+        [((P2, P2), BF16)] + [((n, S2, R2), BF16) for _, n, _ in PACKS.values()],
+        specs=[VMEM, HBM, ANY],
+        scratch=[pltpu.SemaphoreType.DMA((6,))],
+    )
     red1 = jnp.stack([z00, z01, z10, z11]).reshape(2, 2, R1, K)
 
     colour = ((lax.axis_index("bx") % 2) * 2 + lax.axis_index("by") % 2).astype(jnp.int32).reshape(1)
@@ -279,12 +307,10 @@
     def sides(z, c):
         return shift(z, (0, 1), (c,)), shift(z, (0, -1), (c,))
 
-    def ends(sums, row):
-        colours = (2 * row, 2 * row + 1)
-        return shift(sums[0], (-1, 0), colours), shift(sums[1], (1, 0), colours)
-
-    def parent_body(c, me, interp, piv, couple, skel, red, *rest):
-        *got, z_out, skel_out = rest
+    def odd_body(c, me, interp, piv, couple, skel, red, zl, zr, *rest):
+        if c == 3:
+            arrived, rest = rest[:2], rest[2:]
+        ws, (z_out, skel_out), sums = rest[:6], rest[6:8], rest[8:]
 
         @pl.when(me[0] != c)
         def _():
@@ -293,49 +319,57 @@
         @pl.when(me[0] == c)
         def _():
             acc = skel[...]
-            if c % 2:
-                acc = acc - (dot(couple[0, 0, 3], got[0][...]) + dot(couple[0, 0, 4], got[1][...]))
-            if c >= 2:
-                acc = acc - (got[-2][...].astype(F32) + got[-1][...].astype(F32))
+            if c == 3:
+                acc = acc - arrived[0][...].astype(F32) - arrived[1][...].astype(F32)
+            acc = acc - (dot(couple[0, 0, 3], zl[...]) + dot(couple[0, 0, 4], zr[...]))
+            skel_out[...] = acc
+            z = solve_parent(interp, piv, acc, red[...])
+            z_out[...] = z
+            values = (zl[...], z, zr[...])
+            for (_, _, which), w, out in zip(PACKS.values(), ws, sums):
+                total = None
+                for n, v in enumerate(which):
+                    term = dot(w[n], values[v])
+                    total = term if total is None else total + term
+                out[...] = total.astype(BF16)
+
+    def odd(c, skel, zl, zr, arrived=()):
+        ws = [mats[(-dx, -dy)] for dx, dy in PACKS]
+        z, skel, *sums = call(
+            functools.partial(odd_body, c),
+            [colour, interp2, pivinv2, couple2, skel, red, zl, zr, *arrived, *ws],
+            [PAR_Z, PAR_S] + [PAR_M] * 6,
+            specs=[SMEM],
+        )
+        got = {}
+        for way in CORNERS + ENDS:
+            got[way] = shift(sums[list(PACKS).index((-way[0], -way[1]))], way, (c,))
+        return z, skel, got
+
+    def even_body(me, interp, piv, skel, red, a, b, c, d, z_out, skel_out):
+        @pl.when(me[0] != 2)
+        def _():
+            skel_out[...] = skel[...]
+
+        @pl.when(me[0] == 2)
+        def _():
+            acc = skel[...] - (a[...].astype(F32) + b[...].astype(F32) + c[...].astype(F32) + d[...].astype(F32))
             skel_out[...] = acc
             z_out[...] = solve_parent(interp, piv, acc, red[...])
 
-    def parent(c, skel, got):
-        return call(
-            functools.partial(parent_body, c),
-            [colour, interp2, pivinv2, couple2, skel, red, *got],
-            [PAR_Z, PAR_S],
-            specs=[SMEM],
-        )
-
-    def row_body(row, me, above, below, el, er, ol, orr, ze, zo, up_out, down_out):
-        for c, (a, own, b) in ((2 * row, (ol, ze, orr)), (2 * row + 1, (el, zo, er))):
-
-            @pl.when(me[0] == c)
-            def _():
-                for w, out in ((above, up_out), (below, down_out)):
-                    total = dot(w[0], a[...]) + dot(w[1], own[...]) + dot(w[2], b[...])
-                    out[...] = total.astype(BF16)
-
-    def row(n, even, odd, z_even, z_odd):
-        return call(
-            functools.partial(row_body, n),
-            [colour, above_mats, below_mats, *even, *odd, z_even, z_odd],
-            [PAR_M, PAR_M],
-            specs=[SMEM],
-        )
-
-    side0 = sides(z0, 0)
-    z1, skel = parent(1, skel, side0)
+    zl, zr = sides(z0, 0)
+    packs, z0 = after(packs, z0)
+    mats = {(-to[0], -to[1]): shift(pack, to, (1, 3) if to[1] == 0 else (0, 2)) for to, pack in zip(PACKS, packs)}
+    z1, skel, got1 = odd(1, skel, zl, zr)
     side1 = sides(z1, 1)
-    end0 = ends(row(0, side0, side1, z0, z1), 0)
-    z2, skel = parent(2, skel, end0)
-    side2 = sides(z2, 2)
-    z3, skel = parent(3, skel, (*side2, *end0))
+    z2, skel = call(
+        even_body, [colour, interp2, pivinv2, skel, red, *[got1[way] for way in CORNERS]], [PAR_Z, PAR_S], specs=[SMEM]
+    )
+    zl, zr = sides(z2, 2)
+    z3, skel, got3 = odd(3, skel, zl, zr, [got1[way] for way in ENDS])
     side3 = sides(z3, 3)
-    end1 = ends(row(1, side2, side3, z2, z3), 1)
-
-    def early_body(me, interp, couple, skel, z0, z1, z2, z3, al, ar, bl, br, skel_out, z_out):
+
+    def early_body(me, interp, couple, skel, z0, z1, z2, z3, xl, xr, skel_out, z_out):
         for c, own in enumerate((z0, z1, z2, z3)):
 
             @pl.when(me[0] == c)
@@ -343,25 +377,36 @@
                 zc = own[...]
                 z_out[...] = zc
                 acc = skel[...] - dot_t(interp[0, 0], zc)
-                if c % 2 == 0:
-                    xl, xr = ((al, ar), (bl, br))[c // 2]
+                if c == 0:
                     acc = acc - (dot(couple[0, 0, 3], xl[...]) + dot(couple[0, 0, 4], xr[...]))
                 skel_out[...] = acc
 
     skel, red2 = call(
-        early_body, [colour, interp2, couple2, skel, z0, z1, z2, z3, *side1, *side3], [PAR_S, PAR_Z], specs=[SMEM]
-    )
-
-    def late_body(me, skel, a, b, skel_out):
-        @pl.when(me[0] < 2)
-        def _():
-            skel_out[...] = skel[...] - (a[...].astype(F32) + b[...].astype(F32))
-
-        @pl.when(me[0] >= 2)
+        early_body, [colour, interp2, couple2, skel, z0, z1, z2, z3, *side1], [PAR_S, PAR_Z], specs=[SMEM]
+    )
+
+    def late_body(me, couple, skel, a, b, c, d, e, f, xl, xr, skel_out):
+        @pl.when(me[0] == 0)
+        def _():
+            skel_out[...] = skel[...] - (
+                a[...].astype(F32) + b[...].astype(F32) + c[...].astype(F32) + d[...].astype(F32)
+            )
+
+        @pl.when(me[0] == 1)
+        def _():
+            skel_out[...] = skel[...] - (e[...].astype(F32) + f[...].astype(F32))
+
+        @pl.when(me[0] == 2)
+        def _():
+            skel_out[...] = skel[...] - (dot(couple[0, 0, 3], xl[...]) + dot(couple[0, 0, 4], xr[...]))
+
+        @pl.when(me[0] == 3)
         def _():
             skel_out[...] = skel[...]
 
-    (skel2,) = call(late_body, [colour, skel, *end1], [PAR_S], specs=[SMEM])
+    (skel2,) = call(
+        late_body, [colour, couple2, skel, *[got3[way] for way in CORNERS + ENDS], *side3], [PAR_S], specs=[SMEM]
+    )
     return (red1, red2[None, None], skel2[None, None])
 
 

time: 107 us -> 106 us (level)
  the two profiles are of different devices: /device:TPU:70 before, /device:TPU:85 now
where the time goes in v3:
time: 106 us
  starting transfers between devices  68.5 us (65%)
  waiting for transfers between devices  22.7 us (21%)
  Pallas kernels  11.9 us (11%)
  between operations  1.3 us (1%)
    ppermute x36, starting transfers between devices, shift(): return lax.ppermute(x, ('bx', 'by'), pairs(*to, colours))  68.5 us
    ppermute x36, waiting for transfers between devices, shift(): return lax.ppermute(x, ('bx', 'by'), pairs(*to, colours))  22.7 us
    pallas_call x18, Pallas kernels, call(): pl.pallas_call(body, out_shape=[jax.ShapeDtypeStruct(s, d) for s, d in ou...  11.9 us
  transfers between devices with their start and end apart: 36, of which 10 were waited for; matrix products, arithmetic and copies ran while one was open for 1% of the time, Pallas kernels for 5%

profile of v3, /device:TPU:85, one launch (start us, length us, event | category | flops | bytes accessed | tf_op | source)
XLA Modules:
  0.0 105.6 jit_solution(7166317677292270506)
XLA Ops:
  0.7 1.9 %shard_map.112 = (bf16[160,384]{1,0:T(8,128)(2,1)S(1)}, f32[96,384]{1,0:T(8,128)S(1)}) custom-call(f32[2,2,256,384]{3,2,1,0:T(8,128)} %rhs.3, s32[2,2,256]{2,1,0:T(2,128)} %perm.4, bf16[2,2,160,96]{3,2,1,0:T(8,128)(2,1)} %interp.20, bf16[2,2,160,160]{3,2,1,0:T(8,128)(2,1)} %piv.11), custom_call_target="tpu_custom_call" | custom-call | flops 300000000 | bytes 2000000 | tf_op jit(solution)/shard_map/pallas_call | solution.py:62
  3.6 3.5 %collective-permute-start.3 = (bf16[5,160,96]{2,1,0:T(8,128)(2,1)S(1)}, bf16[5,160,96]{2,1,0:T(8,128)(2,1)S(1)}, u32[]{:S(2)}, u32[]{:S(2)}) collective-permute-start(bf16[5,160,96]{2,1,0:T(8,128)(2,1)S(1)} %get-tuple-element.58), channel_id=1, source_target_pairs={{0,32},{1,33},{2,34},{3,35},{4,36},{5,37},{6,38},{7,39},{8,40},{9,... | collective-permute-start | bytes 460808 | tf_op jit(solution)/shard_map/ppermute | solution.py:85
  7.2 2.9 %collective-permute-start = (bf16[160,384]{1,0:T(8,128)(2,1)S(1)}, bf16[160,384]{1,0:T(8,128)(2,1)S(1)}, u32[]{:S(2)}, u32[]{:S(2)}) collective-permute-start(bf16[160,384]{1,0:T(8,128)(2,1)S(1)} %get-tuple-element.52.z.tie.left), channel_id=1, source_target_pairs={{1,0},{2,1},{3,2},{4,3},{5,4},{6,5},{7,6},{8,7},{9,8},{10,9},{11,1... | collective-permute-start | bytes 368648 | tf_op jit(solution)/shard_map/ppermute | solution.py:85
  10.8 2.6 %collective-permute-done.rest_0_.refs_1_.right = bf16[160,384]{1,0:T(8,128)(2,1)S(1)} collective-permute-done((bf16[160,384]{1,0:T(8,128)(2,1)S(1)}, bf16[160,384]{1,0:T(8,128)(2,1)S(1)}, u32[]{:S(2)}, u32[]{:S(2)}) %collective-permute-start) | collective-permute-done | bytes 122912 | tf_op jit(solution)/shard_map/ppermute | solution.py:85
  14.4 1.9 %collective-permute-start.4 = (bf16[192,384]{1,0:T(8,128)(2,1)S(1)}, bf16[192,384]{1,0:T(8,128)(2,1)S(1)}, u32[]{:S(2)}, u32[]{:S(2)}) collective-permute-start(bf16[192,384]{1,0:T(8,128)(2,1)S(1)} %shard_map.117), channel_id=1, source_target_pairs={{32,0},{33,1},{34,2},{35,3},{36,4},{37,5},{38,6},{39,7},{40,8},{41... | collective-permute-start | bytes 442376 | tf_op jit(solution)/shard_map/ppermute | solution.py:85
  16.3 1.9 %collective-permute-start.2 = (bf16[160,384]{1,0:T(8,128)(2,1)S(1)}, bf16[160,384]{1,0:T(8,128)(2,1)S(1)}, u32[]{:S(2)}, u32[]{:S(2)}) collective-permute-start(bf16[160,384]{1,0:T(8,128)(2,1)S(1)} %get-tuple-element.56.refs_0_.own), channel_id=1, source_target_pairs={{32,1},{33,2},{34,3},{35,4},{36,5},{37,6},{38,7},{39,8},{40,9},{41... | collective-permute-start | bytes 368648 | tf_op jit(solution)/shard_map/ppermute | solution.py:85
  18.2 5.0 %collective-permute-start.1 = (bf16[160,384]{1,0:T(8,128)(2,1)S(1)}, bf16[160,384]{1,0:T(8,128)(2,1)S(1)}, u32[]{:S(2)}, u32[]{:S(2)}) collective-permute-start(bf16[160,384]{1,0:T(8,128)(2,1)S(1)} %get-tuple-element.56.refs_0_.own), channel_id=1, source_target_pairs={{0,1},{1,2},{2,3},{3,4},{4,5},{5,6},{6,7},{7,8},{8,9},{9,10},{10,1... | collective-permute-start | bytes 368648 | tf_op jit(solution)/shard_map/ppermute | solution.py:85
  23.2 1.9 %collective-permute-start.8 = (bf16[5,160,96]{2,1,0:T(8,128)(2,1)S(1)}, bf16[5,160,96]{2,1,0:T(8,128)(2,1)S(1)}, u32[]{:S(2)}, u32[]{:S(2)}) collective-permute-start(bf16[5,160,96]{2,1,0:T(8,128)(2,1)S(1)} %get-tuple-element.63), channel_id=1, source_target_pairs={{32,0},{33,1},{34,2},{35,3},{36,4},{37,5},{38,6},{39,7},{40,8},{41... | collective-permute-start | bytes 460808 | tf_op jit(solution)/shard_map/ppermute | solution.py:85
  26.2 2.2 %collective-permute-start.5 = (bf16[160,384]{1,0:T(8,128)(2,1)S(1)}, bf16[160,384]{1,0:T(8,128)(2,1)S(1)}, u32[]{:S(2)}, u32[]{:S(2)}) collective-permute-start(bf16[160,384]{1,0:T(8,128)(2,1)S(1)} %get-tuple-element.59.refs_0_.left), channel_id=1, source_target_pairs={{1,0},{2,1},{3,2},{4,3},{5,4},{6,5},{7,6},{8,7},{9,8},{10,9},{11,1... | collective-permute-start | bytes 368648 | tf_op jit(solution)/shard_map/ppermute | solution.py:85
  28.8 4.4 %collective-permute-done.5.rest_0_.right.refs_1_ = bf16[160,384]{1,0:T(8,128)(2,1)S(1)} collective-permute-done((bf16[160,384]{1,0:T(8,128)(2,1)S(1)}, bf16[160,384]{1,0:T(8,128)(2,1)S(1)}, u32[]{:S(2)}, u32[]{:S(2)}) %collective-permute-start.5) | collective-permute-done | bytes 122912 | tf_op jit(solution)/shard_map/ppermute | solution.py:85
  34.1 4.0 %collective-permute-start.9 = (bf16[192,384]{1,0:T(8,128)(2,1)S(1)}, bf16[192,384]{1,0:T(8,128)(2,1)S(1)}, u32[]{:S(2)}, u32[]{:S(2)}) collective-permute-start(bf16[192,384]{1,0:T(8,128)(2,1)S(1)} %shard_map.122), channel_id=1, source_target_pairs={{0,32},{1,33},{2,34},{3,35},{4,36},{5,37},{6,38},{7,39},{8,40},{9,... | collective-permute-start | bytes 442376 | tf_op jit(solution)/shard_map/ppermute | solution.py:85
  38.0 4.8 %collective-permute-start.7 = (bf16[160,384]{1,0:T(8,128)(2,1)S(1)}, bf16[160,384]{1,0:T(8,128)(2,1)S(1)}, u32[]{:S(2)}, u32[]{:S(2)}) collective-permute-start(bf16[160,384]{1,0:T(8,128)(2,1)S(1)} %get-tuple-element.61.tie.own.refs_0_), channel_id=1, source_target_pairs={{0,33},{1,34},{2,35},{3,36},{4,37},{5,38},{6,39},{7,40},{8,41},{9,... | collective-permute-start | bytes 368648 | tf_op jit(solution)/shard_map/ppermute | solution.py:85
  42.9 4.9 %collective-permute-start.6 = (bf16[160,384]{1,0:T(8,128)(2,1)S(1)}, bf16[160,384]{1,0:T(8,128)(2,1)S(1)}, u32[]{:S(2)}, u32[]{:S(2)}) collective-permute-start(bf16[160,384]{1,0:T(8,128)(2,1)S(1)} %get-tuple-element.61.tie.own.refs_0_), channel_id=1, source_target_pairs={{0,1},{1,2},{2,3},{3,4},{4,5},{5,6},{6,7},{7,8},{8,9},{9,10},{10,1... | collective-permute-start | bytes 368648 | tf_op jit(solution)/shard_map/ppermute | solution.py:85
  50.8 1.3 %collective-permute-start.12 = (bf16[2,128,256]{2,1,0:T(8,128)(2,1)S(1)}, bf16[2,128,256]{2,1,0:T(8,128)(2,1)S(1)}, u32[]{:S(2)}, u32[]{:S(2)}) collective-permute-start(bf16[2,128,256]{2,1,0:T(8,128)(2,1)S(1)} %get-tuple-element.74), channel_id=1, source_target_pairs={{0,33},{2,35},{4,37},{6,39},{8,41},{10,43},{12,45},{14,47},{16,49}... | collective-permute-start | bytes 393224 | tf_op jit(solution)/shard_map/ppermute | solution.py:85
  52.1 1.3 %collective-permute-start.13 = (bf16[1,128,256]{2,1,0:T(8,128)(2,1)S(1)}, bf16[1,128,256]{2,1,0:T(8,128)(2,1)S(1)}, u32[]{:S(2)}, u32[]{:S(2)}) collective-permute-start(bf16[1,128,256]{2,1,0:T(8,128)(2,1)S(1)} %get-tuple-element.75), channel_id=1, source_target_pairs={{2,33},{4,35},{6,37},{8,39},{10,41},{12,43},{14,45},{16,47},{18,49... | collective-permute-start | bytes 196616 | tf_op jit(solution)/shard_map/ppermute | solution.py:85
  53.4 1.3 %collective-permute-start.16 = (bf16[1,128,256]{2,1,0:T(8,128)(2,1)S(1)}, bf16[1,128,256]{2,1,0:T(8,128)(2,1)S(1)}, u32[]{:S(2)}, u32[]{:S(2)}) collective-permute-start(bf16[1,128,256]{2,1,0:T(8,128)(2,1)S(1)} %get-tuple-element.78), channel_id=1, source_target_pairs={{34,1},{36,3},{38,5},{40,7},{42,9},{44,11},{46,13},{48,15},{50,17}... | collective-permute-start | bytes 196616 | tf_op jit(solution)/shard_map/ppermute | solution.py:85
  54.7 1.3 %collective-permute-start.11 = (bf16[256,384]{1,0:T(8,128)(2,1)S(1)}, bf16[256,384]{1,0:T(8,128)(2,1)S(1)}, u32[]{:S(2)}, u32[]{:S(2)}) collective-permute-start(bf16[256,384]{1,0:T(8,128)(2,1)S(1)} %get-tuple-element.90.z0), channel_id=1, source_target_pairs={{2,1},{4,3},{6,5},{8,7},{10,9},{12,11},{14,13},{16,15},{18,17},{20... | collective-permute-start | bytes 589832 | tf_op jit(solution)/shard_map/ppermute | solution.py:85
  56.0 2.4 %collective-permute-start.14 = (bf16[3,128,256]{2,1,0:T(8,128)(2,1)S(1)}, bf16[3,128,256]{2,1,0:T(8,128)(2,1)S(1)}, u32[]{:S(2)}, u32[]{:S(2)}) collective-permute-start(bf16[3,128,256]{2,1,0:T(8,128)(2,1)S(1)} %get-tuple-element.76), channel_id=1, source_target_pairs={{1,33},{3,35},{5,37},{7,39},{9,41},{11,43},{13,45},{15,47},{17,49}... | collective-permute-start | bytes 589832 | tf_op jit(solution)/shard_map/ppermute | solution.py:85
  58.5 2.7 %collective-permute-start.17 = (bf16[3,128,256]{2,1,0:T(8,128)(2,1)S(1)}, bf16[3,128,256]{2,1,0:T(8,128)(2,1)S(1)}, u32[]{:S(2)}, u32[]{:S(2)}) collective-permute-start(bf16[3,128,256]{2,1,0:T(8,128)(2,1)S(1)} %get-tuple-element.79), channel_id=1, source_target_pairs={{33,1},{35,3},{37,5},{39,7},{41,9},{43,11},{45,13},{47,15},{49,17}... | collective-permute-start | bytes 589832 | tf_op jit(solution)/shard_map/ppermute | solution.py:85
  62.9 1.3 %collective-permute-start.15 = (bf16[2,128,256]{2,1,0:T(8,128)(2,1)S(1)}, bf16[2,128,256]{2,1,0:T(8,128)(2,1)S(1)}, u32[]{:S(2)}, u32[]{:S(2)}) collective-permute-start(bf16[2,128,256]{2,1,0:T(8,128)(2,1)S(1)} %get-tuple-element.77), channel_id=1, source_target_pairs={{32,1},{34,3},{36,5},{38,7},{40,9},{42,11},{44,13},{46,15},{48,17}... | collective-permute-start | bytes 393224 | tf_op jit(solution)/shard_map/ppermute | solution.py:85
  64.2 5.0 %collective-permute-done.15.rest_3_.rest_5_ = bf16[2,128,256]{2,1,0:T(8,128)(2,1)S(1)} collective-permute-done((bf16[2,128,256]{2,1,0:T(8,128)(2,1)S(1)}, bf16[2,128,256]{2,1,0:T(8,128)(2,1)S(1)}, u32[]{:S(2)}, u32[]{:S(2)}) %collective-permute-start.15) | collective-permute-done | bytes 131104 | tf_op jit(solution)/shard_map/ppermute | solution.py:85
  70.4 1.3 %collective-permute-start.18 = (bf16[128,384]{1,0:T(8,128)(2,1)S(1)}, bf16[128,384]{1,0:T(8,128)(2,1)S(1)}, u32[]{:S(2)}, u32[]{:S(2)}) collective-permute-start(bf16[128,384]{1,0:T(8,128)(2,1)S(1)} %get-tuple-element.81), channel_id=1, source_target_pairs={{65,32},{67,34},{69,36},{71,38},{73,40},{75,42},{77,44},{79,46},{8... | collective-permute-start | bytes 294920 | tf_op jit(solution)/shard_map/ppermute | solution.py:85
  71.7 1.3 %collective-permute-start.19 = (bf16[128,384]{1,0:T(8,128)(2,1)S(1)}, bf16[128,384]{1,0:T(8,128)(2,1)S(1)}, u32[]{:S(2)}, u32[]{:S(2)}) collective-permute-start(bf16[128,384]{1,0:T(8,128)(2,1)S(1)} %get-tuple-element.82), channel_id=1, source_target_pairs={{65,34},{67,36},{69,38},{71,40},{73,42},{75,44},{77,46},{79,48},{8... | collective-permute-start | bytes 294920 | tf_op jit(solution)/shard_map/ppermute | solution.py:85
  73.0 1.3 %collective-permute-start.20 = (bf16[128,384]{1,0:T(8,128)(2,1)S(1)}, bf16[128,384]{1,0:T(8,128)(2,1)S(1)}, u32[]{:S(2)}, u32[]{:S(2)}) collective-permute-start(bf16[128,384]{1,0:T(8,128)(2,1)S(1)} %get-tuple-element.83), channel_id=1, source_target_pairs={{1,32},{3,34},{5,36},{7,38},{9,40},{11,42},{13,44},{15,46},{17,48}... | collective-permute-start | bytes 294920 | tf_op jit(solution)/shard_map/ppermute | solution.py:85
  74.3 2.7 %collective-permute-start.21 = (bf16[128,384]{1,0:T(8,128)(2,1)S(1)}, bf16[128,384]{1,0:T(8,128)(2,1)S(1)}, u32[]{:S(2)}, u32[]{:S(2)}) collective-permute-start(bf16[128,384]{1,0:T(8,128)(2,1)S(1)} %get-tuple-element.84), channel_id=1, source_target_pairs={{1,34},{3,36},{5,38},{7,40},{9,42},{11,44},{13,46},{15,48},{17,50}... | collective-permute-start | bytes 294920 | tf_op jit(solution)/shard_map/ppermute | solution.py:85
  77.1 1.3 %collective-permute-start.24 = (bf16[128,384]{1,0:T(8,128)(2,1)S(1)}, bf16[128,384]{1,0:T(8,128)(2,1)S(1)}, u32[]{:S(2)}, u32[]{:S(2)}) collective-permute-start(bf16[128,384]{1,0:T(8,128)(2,1)S(1)} %get-tuple-element.87), channel_id=1, source_target_pairs={{65,33},{67,35},{69,37},{71,39},{73,41},{75,43},{77,45},{79,47},{8... | collective-permute-start | bytes 294920 | tf_op jit(solution)/shard_map/ppermute | solution.py:85
  80.1 1.3 %collective-permute-start.27 = (bf16[256,384]{1,0:T(8,128)(2,1)S(1)}, bf16[256,384]{1,0:T(8,128)(2,1)S(1)}, u32[]{:S(2)}, u32[]{:S(2)}) collective-permute-start(bf16[256,384]{1,0:T(8,128)(2,1)S(1)} %get-tuple-element.91.z1), channel_id=1, source_target_pairs={{1,0},{3,2},{5,4},{7,6},{9,8},{11,10},{13,12},{15,14},{17,16},{19,... | collective-permute-start | bytes 589832 | tf_op jit(solution)/shard_map/ppermute | solution.py:85
  81.4 1.3 %collective-permute-start.26 = (bf16[256,384]{1,0:T(8,128)(2,1)S(1)}, bf16[256,384]{1,0:T(8,128)(2,1)S(1)}, u32[]{:S(2)}, u32[]{:S(2)}) collective-permute-start(bf16[256,384]{1,0:T(8,128)(2,1)S(1)} %get-tuple-element.91.z1), channel_id=1, source_target_pairs={{1,2},{3,4},{5,6},{7,8},{9,10},{11,12},{13,14},{15,16},{17,18},{19... | collective-permute-start | bytes 589832 | tf_op jit(solution)/shard_map/ppermute | solution.py:85
  82.7 4.1 %collective-permute-start.25 = (bf16[128,384]{1,0:T(8,128)(2,1)S(1)}, bf16[128,384]{1,0:T(8,128)(2,1)S(1)}, u32[]{:S(2)}, u32[]{:S(2)}) collective-permute-start(bf16[128,384]{1,0:T(8,128)(2,1)S(1)} %get-tuple-element.88), channel_id=1, source_target_pairs={{1,33},{3,35},{5,37},{7,39},{9,41},{11,43},{13,45},{15,47},{17,49}... | collective-permute-start | bytes 294920 | tf_op jit(solution)/shard_map/ppermute | solution.py:85
  86.8 1.6 %collective-permute-done.25.rest_1_ = bf16[128,384]{1,0:T(8,128)(2,1)S(1)} collective-permute-done((bf16[128,384]{1,0:T(8,128)(2,1)S(1)}, bf16[128,384]{1,0:T(8,128)(2,1)S(1)}, u32[]{:S(2)}, u32[]{:S(2)}) %collective-permute-start.25) | collective-permute-done | bytes 98336 | tf_op jit(solution)/shard_map/ppermute | solution.py:85
  92.6 1.3 %collective-permute-start.32 = (bf16[128,384]{1,0:T(8,128)(2,1)S(1)}, bf16[128,384]{1,0:T(8,128)(2,1)S(1)}, u32[]{:S(2)}, u32[]{:S(2)}) collective-permute-start(bf16[128,384]{1,0:T(8,128)(2,1)S(1)} %get-tuple-element.99), channel_id=1, source_target_pairs={{33,1},{35,3},{37,5},{39,7},{41,9},{43,11},{45,13},{47,15},{49,17}... | collective-permute-start | bytes 294920 | tf_op jit(solution)/shard_map/ppermute | solution.py:85
  97.0 7.9 %collective-permute-done.32.e = bf16[128,384]{1,0:T(8,128)(2,1)S(1)} collective-permute-done((bf16[128,384]{1,0:T(8,128)(2,1)S(1)}, bf16[128,384]{1,0:T(8,128)(2,1)S(1)}, u32[]{:S(2)}, u32[]{:S(2)}) %collective-permute-start.32) | collective-permute-done | bytes 98336 | tf_op jit(solution)/shard_map/ppermute | solution.py:85
  (77 shorter events, 20.4 us)
Async XLA Ops:
  3.6 10.4 %collective-permute-start.3 = (bf16[5,160,96]{2,1,0:T(8,128)(2,1)S(1)}, bf16[5,160,96]{2,1,0:T(8,128)(2,1)S(1)}, u32[]{:S(2)}, u32[]{:S(2)}) collective-permute-start(bf16[5,160,96]{2,1,0:T(8,128)(2,1)S(1)} %get-tuple-element.58), channel_id=1, source_target_pairs={{0,32},{1,33},{2,34},{3,35},{4,36},{5,37},{6,38},{7,39},{8,40},{9,... | collective-permute-start | bytes 460808 | tf_op jit(solution)/shard_map/ppermute | solution.py:85
  7.2 6.3 %collective-permute-start = (bf16[160,384]{1,0:T(8,128)(2,1)S(1)}, bf16[160,384]{1,0:T(8,128)(2,1)S(1)}, u32[]{:S(2)}, u32[]{:S(2)}) collective-permute-start(bf16[160,384]{1,0:T(8,128)(2,1)S(1)} %get-tuple-element.52.z.tie.left), channel_id=1, source_target_pairs={{1,0},{2,1},{3,2},{4,3},{5,4},{6,5},{7,6},{8,7},{9,8},{10,9},{11,1... | collective-permute-start | bytes 368648 | tf_op jit(solution)/shard_map/ppermute | solution.py:85
  14.4 11.3 %collective-permute-start.4 = (bf16[192,384]{1,0:T(8,128)(2,1)S(1)}, bf16[192,384]{1,0:T(8,128)(2,1)S(1)}, u32[]{:S(2)}, u32[]{:S(2)}) collective-permute-start(bf16[192,384]{1,0:T(8,128)(2,1)S(1)} %shard_map.117), channel_id=1, source_target_pairs={{32,0},{33,1},{34,2},{35,3},{36,4},{37,5},{38,6},{39,7},{40,8},{41... | collective-permute-start | bytes 442376 | tf_op jit(solution)/shard_map/ppermute | solution.py:85
  16.3 9.2 %collective-permute-start.2 = (bf16[160,384]{1,0:T(8,128)(2,1)S(1)}, bf16[160,384]{1,0:T(8,128)(2,1)S(1)}, u32[]{:S(2)}, u32[]{:S(2)}) collective-permute-start(bf16[160,384]{1,0:T(8,128)(2,1)S(1)} %get-tuple-element.56.refs_0_.own), channel_id=1, source_target_pairs={{32,1},{33,2},{34,3},{35,4},{36,5},{37,6},{38,7},{39,8},{40,9},{41... | collective-permute-start | bytes 368648 | tf_op jit(solution)/shard_map/ppermute | solution.py:85
  18.2 7.4 %collective-permute-start.1 = (bf16[160,384]{1,0:T(8,128)(2,1)S(1)}, bf16[160,384]{1,0:T(8,128)(2,1)S(1)}, u32[]{:S(2)}, u32[]{:S(2)}) collective-permute-start(bf16[160,384]{1,0:T(8,128)(2,1)S(1)} %get-tuple-element.56.refs_0_.own), channel_id=1, source_target_pairs={{0,1},{1,2},{2,3},{3,4},{4,5},{5,6},{6,7},{7,8},{8,9},{9,10},{10,1... | collective-permute-start | bytes 368648 | tf_op jit(solution)/shard_map/ppermute | solution.py:85
  23.2 10.5 %collective-permute-start.8 = (bf16[5,160,96]{2,1,0:T(8,128)(2,1)S(1)}, bf16[5,160,96]{2,1,0:T(8,128)(2,1)S(1)}, u32[]{:S(2)}, u32[]{:S(2)}) collective-permute-start(bf16[5,160,96]{2,1,0:T(8,128)(2,1)S(1)} %get-tuple-element.63), channel_id=1, source_target_pairs={{32,0},{33,1},{34,2},{35,3},{36,4},{37,5},{38,6},{39,7},{40,8},{41... | collective-permute-start | bytes 460808 | tf_op jit(solution)/shard_map/ppermute | solution.py:85
  26.2 6.9 %collective-permute-start.5 = (bf16[160,384]{1,0:T(8,128)(2,1)S(1)}, bf16[160,384]{1,0:T(8,128)(2,1)S(1)}, u32[]{:S(2)}, u32[]{:S(2)}) collective-permute-start(bf16[160,384]{1,0:T(8,128)(2,1)S(1)} %get-tuple-element.59.refs_0_.left), channel_id=1, source_target_pairs={{1,0},{2,1},{3,2},{4,3},{5,4},{6,5},{7,6},{8,7},{9,8},{10,9},{11,1... | collective-permute-start | bytes 368648 | tf_op jit(solution)/shard_map/ppermute | solution.py:85
  34.1 15.5 %collective-permute-start.9 = (bf16[192,384]{1,0:T(8,128)(2,1)S(1)}, bf16[192,384]{1,0:T(8,128)(2,1)S(1)}, u32[]{:S(2)}, u32[]{:S(2)}) collective-permute-start(bf16[192,384]{1,0:T(8,128)(2,1)S(1)} %shard_map.122), channel_id=1, source_target_pairs={{0,32},{1,33},{2,34},{3,35},{4,36},{5,37},{6,38},{7,39},{8,40},{9,... | collective-permute-start | bytes 442376 | tf_op jit(solution)/shard_map/ppermute | solution.py:85
  38.0 11.4 %collective-permute-start.7 = (bf16[160,384]{1,0:T(8,128)(2,1)S(1)}, bf16[160,384]{1,0:T(8,128)(2,1)S(1)}, u32[]{:S(2)}, u32[]{:S(2)}) collective-permute-start(bf16[160,384]{1,0:T(8,128)(2,1)S(1)} %get-tuple-element.61.tie.own.refs_0_), channel_id=1, source_target_pairs={{0,33},{1,34},{2,35},{3,36},{4,37},{5,38},{6,39},{7,40},{8,41},{9,... | collective-permute-start | bytes 368648 | tf_op jit(solution)/shard_map/ppermute | solution.py:85
  42.9 6.7 %collective-permute-start.6 = (bf16[160,384]{1,0:T(8,128)(2,1)S(1)}, bf16[160,384]{1,0:T(8,128)(2,1)S(1)}, u32[]{:S(2)}, u32[]{:S(2)}) collective-permute-start(bf16[160,384]{1,0:T(8,128)(2,1)S(1)} %get-tuple-element.61.tie.own.refs_0_), channel_id=1, source_target_pairs={{0,1},{1,2},{2,3},{3,4},{4,5},{5,6},{6,7},{7,8},{8,9},{9,10},{10,1... | collective-permute-start | bytes 368648 | tf_op jit(solution)/shard_map/ppermute | solution.py:85
  50.8 12.2 %collective-permute-start.12 = (bf16[2,128,256]{2,1,0:T(8,128)(2,1)S(1)}, bf16[2,128,256]{2,1,0:T(8,128)(2,1)S(1)}, u32[]{:S(2)}, u32[]{:S(2)}) collective-permute-start(bf16[2,128,256]{2,1,0:T(8,128)(2,1)S(1)} %get-tuple-element.74), channel_id=1, source_target_pairs={{0,33},{2,35},{4,37},{6,39},{8,41},{10,43},{12,45},{14,47},{16,49}... | collective-permute-start | bytes 393224 | tf_op jit(solution)/shard_map/ppermute | solution.py:85
  52.1 6.5 %collective-permute-start.13 = (bf16[1,128,256]{2,1,0:T(8,128)(2,1)S(1)}, bf16[1,128,256]{2,1,0:T(8,128)(2,1)S(1)}, u32[]{:S(2)}, u32[]{:S(2)}) collective-permute-start(bf16[1,128,256]{2,1,0:T(8,128)(2,1)S(1)} %get-tuple-element.75), channel_id=1, source_target_pairs={{2,33},{4,35},{6,37},{8,39},{10,41},{12,43},{14,45},{16,47},{18,49... | collective-permute-start | bytes 196616 | tf_op jit(solution)/shard_map/ppermute | solution.py:85
  53.4 8.3 %collective-permute-start.16 = (bf16[1,128,256]{2,1,0:T(8,128)(2,1)S(1)}, bf16[1,128,256]{2,1,0:T(8,128)(2,1)S(1)}, u32[]{:S(2)}, u32[]{:S(2)}) collective-permute-start(bf16[1,128,256]{2,1,0:T(8,128)(2,1)S(1)} %get-tuple-element.78), channel_id=1, source_target_pairs={{34,1},{36,3},{38,5},{40,7},{42,9},{44,11},{46,13},{48,15},{50,17}... | collective-permute-start | bytes 196616 | tf_op jit(solution)/shard_map/ppermute | solution.py:85
  54.7 14.6 %collective-permute-start.11 = (bf16[256,384]{1,0:T(8,128)(2,1)S(1)}, bf16[256,384]{1,0:T(8,128)(2,1)S(1)}, u32[]{:S(2)}, u32[]{:S(2)}) collective-permute-start(bf16[256,384]{1,0:T(8,128)(2,1)S(1)} %get-tuple-element.90.z0), channel_id=1, source_target_pairs={{2,1},{4,3},{6,5},{8,7},{10,9},{12,11},{14,13},{16,15},{18,17},{20... | collective-permute-start | bytes 589832 | tf_op jit(solution)/shard_map/ppermute | solution.py:85
  56.0 13.3 %collective-permute-start.14 = (bf16[3,128,256]{2,1,0:T(8,128)(2,1)S(1)}, bf16[3,128,256]{2,1,0:T(8,128)(2,1)S(1)}, u32[]{:S(2)}, u32[]{:S(2)}) collective-permute-start(bf16[3,128,256]{2,1,0:T(8,128)(2,1)S(1)} %get-tuple-element.76), channel_id=1, source_target_pairs={{1,33},{3,35},{5,37},{7,39},{9,41},{11,43},{13,45},{15,47},{17,49}... | collective-permute-start | bytes 589832 | tf_op jit(solution)/shard_map/ppermute | solution.py:85
  58.5 10.7 %collective-permute-start.17 = (bf16[3,128,256]{2,1,0:T(8,128)(2,1)S(1)}, bf16[3,128,256]{2,1,0:T(8,128)(2,1)S(1)}, u32[]{:S(2)}, u32[]{:S(2)}) collective-permute-start(bf16[3,128,256]{2,1,0:T(8,128)(2,1)S(1)} %get-tuple-element.79), channel_id=1, source_target_pairs={{33,1},{35,3},{37,5},{39,7},{41,9},{43,11},{45,13},{47,15},{49,17}... | collective-permute-start | bytes 589832 | tf_op jit(solution)/shard_map/ppermute | solution.py:85
  61.6 7.6 %collective-permute-start.10 = (bf16[256,384]{1,0:T(8,128)(2,1)S(1)}, bf16[256,384]{1,0:T(8,128)(2,1)S(1)}, u32[]{:S(2)}, u32[]{:S(2)}) collective-permute-start(bf16[256,384]{1,0:T(8,128)(2,1)S(1)} %get-tuple-element.90.z0), channel_id=1, source_target_pairs={{0,1},{2,3},{4,5},{6,7},{8,9},{10,11},{12,13},{14,15},{16,17},{18,... | collective-permute-start | bytes 589832 | tf_op jit(solution)/shard_map/ppermute | solution.py:85
  62.9 6.3 %collective-permute-start.15 = (bf16[2,128,256]{2,1,0:T(8,128)(2,1)S(1)}, bf16[2,128,256]{2,1,0:T(8,128)(2,1)S(1)}, u32[]{:S(2)}, u32[]{:S(2)}) collective-permute-start(bf16[2,128,256]{2,1,0:T(8,128)(2,1)S(1)} %get-tuple-element.77), channel_id=1, source_target_pairs={{32,1},{34,3},{36,5},{38,7},{40,9},{42,11},{44,13},{46,15},{48,17}... | collective-permute-start | bytes 393224 | tf_op jit(solution)/shard_map/ppermute | solution.py:85
  70.4 8.0 %collective-permute-start.18 = (bf16[128,384]{1,0:T(8,128)(2,1)S(1)}, bf16[128,384]{1,0:T(8,128)(2,1)S(1)}, u32[]{:S(2)}, u32[]{:S(2)}) collective-permute-start(bf16[128,384]{1,0:T(8,128)(2,1)S(1)} %get-tuple-element.81), channel_id=1, source_target_pairs={{65,32},{67,34},{69,36},{71,38},{73,40},{75,42},{77,44},{79,46},{8... | collective-permute-start | bytes 294920 | tf_op jit(solution)/shard_map/ppermute | solution.py:85
  71.7 6.7 %collective-permute-start.19 = (bf16[128,384]{1,0:T(8,128)(2,1)S(1)}, bf16[128,384]{1,0:T(8,128)(2,1)S(1)}, u32[]{:S(2)}, u32[]{:S(2)}) collective-permute-start(bf16[128,384]{1,0:T(8,128)(2,1)S(1)} %get-tuple-element.82), channel_id=1, source_target_pairs={{65,34},{67,36},{69,38},{71,40},{73,42},{75,44},{77,46},{79,48},{8... | collective-permute-start | bytes 294920 | tf_op jit(solution)/shard_map/ppermute | solution.py:85
  73.0 5.4 %collective-permute-start.20 = (bf16[128,384]{1,0:T(8,128)(2,1)S(1)}, bf16[128,384]{1,0:T(8,128)(2,1)S(1)}, u32[]{:S(2)}, u32[]{:S(2)}) collective-permute-start(bf16[128,384]{1,0:T(8,128)(2,1)S(1)} %get-tuple-element.83), channel_id=1, source_target_pairs={{1,32},{3,34},{5,36},{7,38},{9,40},{11,42},{13,44},{15,46},{17,48}... | collective-permute-start | bytes 294920 | tf_op jit(solution)/shard_map/ppermute | solution.py:85
  77.1 5.6 %collective-permute-start.24 = (bf16[128,384]{1,0:T(8,128)(2,1)S(1)}, bf16[128,384]{1,0:T(8,128)(2,1)S(1)}, u32[]{:S(2)}, u32[]{:S(2)}) collective-permute-start(bf16[128,384]{1,0:T(8,128)(2,1)S(1)} %get-tuple-element.87), channel_id=1, source_target_pairs={{65,33},{67,35},{69,37},{71,39},{73,41},{75,43},{77,45},{79,47},{8... | collective-permute-start | bytes 294920 | tf_op jit(solution)/shard_map/ppermute | solution.py:85
  78.7 9.7 %collective-permute-start.23 = (bf16[256,384]{1,0:T(8,128)(2,1)S(1)}, bf16[256,384]{1,0:T(8,128)(2,1)S(1)}, u32[]{:S(2)}, u32[]{:S(2)}) collective-permute-start(bf16[256,384]{1,0:T(8,128)(2,1)S(1)} %get-tuple-element.86.z2), channel_id=1, source_target_pairs={{34,33},{36,35},{38,37},{40,39},{42,41},{44,43},{46,45},{48,47},{5... | collective-permute-start | bytes 589832 | tf_op jit(solution)/shard_map/ppermute | solution.py:85
  79.4 9.0 %collective-permute-start.22 = (bf16[256,384]{1,0:T(8,128)(2,1)S(1)}, bf16[256,384]{1,0:T(8,128)(2,1)S(1)}, u32[]{:S(2)}, u32[]{:S(2)}) collective-permute-start(bf16[256,384]{1,0:T(8,128)(2,1)S(1)} %get-tuple-element.86.z2), channel_id=1, source_target_pairs={{32,33},{34,35},{36,37},{38,39},{40,41},{42,43},{44,45},{46,47},{4... | collective-permute-start | bytes 589832 | tf_op jit(solution)/shard_map/ppermute | solution.py:85
  80.1 10.4 %collective-permute-start.27 = (bf16[256,384]{1,0:T(8,128)(2,1)S(1)}, bf16[256,384]{1,0:T(8,128)(2,1)S(1)}, u32[]{:S(2)}, u32[]{:S(2)}) collective-permute-start(bf16[256,384]{1,0:T(8,128)(2,1)S(1)} %get-tuple-element.91.z1), channel_id=1, source_target_pairs={{1,0},{3,2},{5,4},{7,6},{9,8},{11,10},{13,12},{15,14},{17,16},{19,... | collective-permute-start | bytes 589832 | tf_op jit(solution)/shard_map/ppermute | solution.py:85
  81.4 9.8 %collective-permute-start.26 = (bf16[256,384]{1,0:T(8,128)(2,1)S(1)}, bf16[256,384]{1,0:T(8,128)(2,1)S(1)}, u32[]{:S(2)}, u32[]{:S(2)}) collective-permute-start(bf16[256,384]{1,0:T(8,128)(2,1)S(1)} %get-tuple-element.91.z1), channel_id=1, source_target_pairs={{1,2},{3,4},{5,6},{7,8},{9,10},{11,12},{13,14},{15,16},{17,18},{19... | collective-permute-start | bytes 589832 | tf_op jit(solution)/shard_map/ppermute | solution.py:85
  82.7 5.7 %collective-permute-start.25 = (bf16[128,384]{1,0:T(8,128)(2,1)S(1)}, bf16[128,384]{1,0:T(8,128)(2,1)S(1)}, u32[]{:S(2)}, u32[]{:S(2)}) collective-permute-start(bf16[128,384]{1,0:T(8,128)(2,1)S(1)} %get-tuple-element.88), channel_id=1, source_target_pairs={{1,33},{3,35},{5,37},{7,39},{9,41},{11,43},{13,45},{15,47},{17,49}... | collective-permute-start | bytes 294920 | tf_op jit(solution)/shard_map/ppermute | solution.py:85
  90.5 14.4 %collective-permute-start.35 = (bf16[256,384]{1,0:T(8,128)(2,1)S(1)}, bf16[256,384]{1,0:T(8,128)(2,1)S(1)}, u32[]{:S(2)}, u32[]{:S(2)}) collective-permute-start(bf16[256,384]{1,0:T(8,128)(2,1)S(1)} %get-tuple-element.92.z3), channel_id=1, source_target_pairs={{33,32},{35,34},{37,36},{39,38},{41,40},{43,42},{45,44},{47,46},{4... | collective-permute-start | bytes 589832 | tf_op jit(solution)/shard_map/ppermute | solution.py:85
  91.2 13.7 %collective-permute-start.34 = (bf16[256,384]{1,0:T(8,128)(2,1)S(1)}, bf16[256,384]{1,0:T(8,128)(2,1)S(1)}, u32[]{:S(2)}, u32[]{:S(2)}) collective-permute-start(bf16[256,384]{1,0:T(8,128)(2,1)S(1)} %get-tuple-element.92.z3), channel_id=1, source_target_pairs={{33,34},{35,36},{37,38},{39,40},{41,42},{43,44},{45,46},{47,48},{4... | collective-permute-start | bytes 589832 | tf_op jit(solution)/shard_map/ppermute | solution.py:85
  91.9 5.1 %collective-permute-start.31 = (bf16[128,384]{1,0:T(8,128)(2,1)S(1)}, bf16[128,384]{1,0:T(8,128)(2,1)S(1)}, u32[]{:S(2)}, u32[]{:S(2)}) collective-permute-start(bf16[128,384]{1,0:T(8,128)(2,1)S(1)} %get-tuple-element.98), channel_id=1, source_target_pairs={{33,66},{35,68},{37,70},{39,72},{41,74},{43,76},{45,78},{47,80},{4... | collective-permute-start | bytes 294920 | tf_op jit(solution)/shard_map/ppermute | solution.py:85
  92.6 12.3 %collective-permute-start.32 = (bf16[128,384]{1,0:T(8,128)(2,1)S(1)}, bf16[128,384]{1,0:T(8,128)(2,1)S(1)}, u32[]{:S(2)}, u32[]{:S(2)}) collective-permute-start(bf16[128,384]{1,0:T(8,128)(2,1)S(1)} %get-tuple-element.99), channel_id=1, source_target_pairs={{33,1},{35,3},{37,5},{39,7},{41,9},{43,11},{45,13},{47,15},{49,17}... | collective-permute-start | bytes 294920 | tf_op jit(solution)/shard_map/ppermute | solution.py:85
  93.9 11.0 %collective-permute-start.33 = (bf16[128,384]{1,0:T(8,128)(2,1)S(1)}, bf16[128,384]{1,0:T(8,128)(2,1)S(1)}, u32[]{:S(2)}, u32[]{:S(2)}) collective-permute-start(bf16[128,384]{1,0:T(8,128)(2,1)S(1)} %get-tuple-element.100), channel_id=1, source_target_pairs={{33,65},{35,67},{37,69},{39,71},{41,73},{43,75},{45,77},{47,79},{4... | collective-permute-start | bytes 294920 | tf_op jit(solution)/shard_map/ppermute | solution.py:85
  (13 other events, 96.9 us)

commit v4 on v1

--- a/solution.py
+++ b/solution.py
@@ -15,13 +15,16 @@
 BOXES = [(0, 0), (0, 1), (1, 0), (1, 1)]
 F32, BF16 = jnp.float32, jnp.bfloat16
 LEAF_S, LEAF_R, LEAF_Z = ((4, S1, K), F32), ((3, R1, K), F32), ((R1, K), BF16)
+PAR_W = ((3, S2, R2), BF16)
 LEAF_W, LEAF_M = ((5, R1, S1), BF16), ((2 * S1, K), BF16)
-PAR_W = ((3, S2, R2), BF16)
 PAR_S, PAR_R, PAR_Z, PAR_M = ((S2, K), F32), ((R2, K), F32), ((R2, K), BF16), ((S2, K), BF16)
 
 
 UP_TERMS = [((1, 0), (6, 7)), ((1, 1), (5, 6, 7))]
 DOWN_TERMS = [((0, 0), (1, 2)), ((0, 1), (0, 1, 2))]
+
+CORNERS = [0, 2, 5, 7]
+ENDS = [1, 6]
 
 
 def dot(a, b):
@@ -44,7 +47,7 @@
     return dot_t(pick, high) + dot_t(pick, low)
 
 
-SMEM, VMEM, HBM = (pl.BlockSpec(memory_space=s) for s in (pltpu.SMEM, pltpu.VMEM, pltpu.HBM))
+SMEM, VMEM, ANY, HBM = (pl.BlockSpec(memory_space=s) for s in (pltpu.SMEM, pltpu.VMEM, pl.ANY, pltpu.HBM))
 
 
 def call(body, ins, outs, specs=(), scratch=(), alias=None):
@@ -79,27 +82,31 @@
     return lax.optimization_barrier((x, value))
 
 
-def first_body(rhs, perm, interp, piv, couple, top, z_out, skel_out, up_out, down_out, below_out, above_out, *rest):
-    x, p, t, v, sems = rest
+def first_body(rhs, perm, interp, piv, z_out, skel_out, x, p, t, v, sems):
     jobs = [(rhs.at[0, 0], x), (perm, p), (interp.at[0, 0], t), (piv.at[0, 0], v)]
-    for terms, out in ((UP_TERMS, up_out), (DOWN_TERMS, down_out)):
-        at = 0
-        for (i, j), ks in terms:
-            jobs.append((couple.at[i, j, pl.ds(ks[0], len(ks))], out.at[pl.ds(at, len(ks))]))
-            at += len(ks)
-    jobs.append((top.at[0, 0, pl.ds(5, 3)], below_out))
-    jobs.append((top.at[0, 0, pl.ds(0, 3)], above_out))
     copies = [pltpu.make_async_copy(a, b, sems.at[n]) for n, (a, b) in enumerate(jobs)]
     for c in copies:
         c.start()
-    for c in copies[:4]:
+    for c in copies:
         c.wait()
     leaf = reordered(x[...], p[0, 0:1, :], P1)
     skel = leaf[:S1]
     diff = leaf[S1:] - dot(t[...], skel.astype(BF16))
     z_out[...] = dot(v[...], diff.astype(BF16)).astype(BF16)
     skel_out[...] = skel
-    for c in copies[4:]:
+
+
+def pack_body(couple, tie, up_out, down_out, sems):
+    jobs = []
+    for terms, out in ((UP_TERMS, up_out), (DOWN_TERMS, down_out)):
+        at = 0
+        for (i, j), ks in terms:
+            jobs.append((couple.at[i, j, pl.ds(ks[0], len(ks))], out.at[pl.ds(at, len(ks))]))
+            at += len(ks)
+    copies = [pltpu.make_async_copy(a, b, sems.at[n]) for n, (a, b) in enumerate(jobs)]
+    for c in copies:
+        c.start()
+    for c in copies:
         c.wait()
 
 
@@ -156,9 +163,17 @@
         out[n] = acc
 
 
-def pick_body(perm, pick_out):
+def pick_body(perm, couple, tie, pick_out, below_out, above_out, sems):
+    copies = [
+        pltpu.make_async_copy(couple.at[0, 0, pl.ds(k, 3)], out, sems.at[at])
+        for at, (k, out) in enumerate(((5, below_out), (0, above_out)))
+    ]
+    for c in copies:
+        c.start()
     hit = (lax.broadcasted_iota(jnp.int32, (P2, P2), 0) == perm[0]).astype(F32)
     pick_out[...] = hit.T.astype(BF16)
+    for c in copies:
+        c.wait()
 
 
 def jobs_of(order, drop=()):
@@ -198,46 +213,51 @@
         body = functools.partial(update_body, own, jobs_of(order, drop), len(order), part)
         return call(body, ins, [LEAF_S])[0]
 
-    z00, skel0, up_pack, down_pack, below_pack, above_pack = call(
+    z00, skel0 = call(
         first_body,
-        [pltpu.with_memory_space_constraint(x, pltpu.HBM) for x in (rhs, perm1, interp1, pivinv1, couple1, couple2)],
-        [LEAF_Z, ((S1, K), F32), LEAF_W, LEAF_W, PAR_W, PAR_W],
-        specs=[HBM] * 6,
+        [pltpu.with_memory_space_constraint(x, pltpu.HBM) for x in (rhs, perm1, interp1, pivinv1)],
+        [LEAF_Z, ((S1, K), F32)],
+        specs=[HBM] * 4,
         scratch=[
             pltpu.VMEM((P1, K), F32),
             pltpu.VMEM((2, 2, P1), jnp.int32),
             pltpu.VMEM((R1, S1), BF16),
             pltpu.VMEM((R1, R1), BF16),
-            pltpu.SemaphoreType.DMA((4 + 4 + 2,)),
+            pltpu.SemaphoreType.DMA((4,)),
         ],
     )
     have[(0, here)] = z00
     z00r = have[(0, (0, 1))] = shift(z00, (0, -1))
+    up_pack, down_pack = call(
+        pack_body,
+        [pltpu.with_memory_space_constraint(couple1, pltpu.HBM), z00],
+        [LEAF_W, LEAF_W],
+        specs=[HBM, ANY],
+        scratch=[pltpu.SemaphoreType.DMA((4,))],
+    )
     up_mats = shift(up_pack, (1, 0))
+    down_mats = shift(down_pack, (-1, 0))
     skels, reds = call(spread_body, [rhs, perm1, interp1, couple1, z00, skel0], [LEAF_S, LEAF_R])
     z01, skels = solve(1, {(0, (0, 1))}, skels, reds)
     have[(1, (1, -1))] = shift(z01, (-1, 1))
     from_below = shift(total(UP_TERMS, z00, z01, z00r, up_mats), (-1, 0))
     have[(1, (0, -1))] = shift(z01, (0, 1))
-    below_pack, z01 = after(below_pack, z01)
-    have[(1, here)] = z01
-    above_mats = shift(below_pack, (1, 0))
     skels = update(1, [(0, (0, 1))], skels, drop=[(1, (0, (0, 1)))])
     z10, skels = solve(2, {(1, (0, -1)), (1, (1, -1))}, skels, reds, arrived=from_below, part=0)
     z10r = have[(2, (0, 1))] = shift(z10, (0, -1))
-    down_pack, z10 = after(down_pack, z10)
-    have[(2, here)] = z10
-    down_mats = shift(down_pack, (-1, 0))
     skels = update(2, [(1, (0, -1))], skels, drop=[(2, (1, (0, -1)))], arrived=from_below, part=3)
     z11, skels = solve(3, {(2, (0, 1))}, skels, reds)
     have[(3, (-1, -1))] = shift(z11, (1, 1))
     from_above = shift(total(DOWN_TERMS, z10, z11, z10r, down_mats), (1, 0))
     have[(3, (0, -1))] = shift(z11, (0, 1))
-    above_pack, z11 = after(above_pack, z11)
-    have[(3, here)] = z11
-    below_mats = shift(above_pack, (-1, 0))
     skels = update(3, [(2, (0, 1))], skels, drop=[(3, (2, (0, 1)))])
-    (pick,) = call(pick_body, [perm2], [((P2, P2), BF16)])
+    pick, below_pack, above_pack = call(
+        pick_body,
+        [perm2, pltpu.with_memory_space_constraint(couple2, pltpu.HBM), z11],
+        [((P2, P2), BF16), PAR_W, PAR_W],
+        specs=[VMEM, HBM, ANY],
+        scratch=[pltpu.SemaphoreType.DMA((2,))],
+    )
     red1 = jnp.stack([z00, z01, z10, z11]).reshape(2, 2, R1, K)
 
     colour = ((lax.axis_index("bx") % 2) * 2 + lax.axis_index("by") % 2).astype(jnp.int32).reshape(1)
@@ -279,12 +299,11 @@
     def sides(z, c):
         return shift(z, (0, 1), (c,)), shift(z, (0, -1), (c,))
 
-    def ends(sums, row):
-        colours = (2 * row, 2 * row + 1)
-        return shift(sums[0], (-1, 0), colours), shift(sums[1], (1, 0), colours)
-
-    def parent_body(c, me, interp, piv, couple, skel, red, *rest):
-        *got, z_out, skel_out = rest
+    def ends(up, down, colours):
+        return shift(up, (-1, 0), colours), shift(down, (1, 0), colours)
+
+    def parent_body(c, ks, n_sums, me, interp, piv, couple, skel, red, *rest):
+        zs, sums, (z_out, skel_out) = rest[: len(ks)], rest[len(ks) : len(ks) + n_sums], rest[len(ks) + n_sums :]
 
         @pl.when(me[0] != c)
         def _():
@@ -293,47 +312,54 @@
         @pl.when(me[0] == c)
         def _():
             acc = skel[...]
-            if c % 2:
-                acc = acc - (dot(couple[0, 0, 3], got[0][...]) + dot(couple[0, 0, 4], got[1][...]))
-            if c >= 2:
-                acc = acc - (got[-2][...].astype(F32) + got[-1][...].astype(F32))
+            for x in sums:
+                acc = acc - x[...].astype(F32)
+            for k, z in zip(ks, zs):
+                acc = acc - dot(couple[0, 0, k], z[...])
             skel_out[...] = acc
             z_out[...] = solve_parent(interp, piv, acc, red[...])
 
-    def parent(c, skel, got):
+    def parent(c, skel, ks, zs, sums=()):
         return call(
-            functools.partial(parent_body, c),
-            [colour, interp2, pivinv2, couple2, skel, red, *got],
+            functools.partial(parent_body, c, ks, len(sums)),
+            [colour, interp2, pivinv2, couple2, skel, red, *zs, *sums],
             [PAR_Z, PAR_S],
             specs=[SMEM],
         )
 
-    def row_body(row, me, above, below, el, er, ol, orr, ze, zo, up_out, down_out):
-        for c, (a, own, b) in ((2 * row, (ol, ze, orr)), (2 * row + 1, (el, zo, er))):
+    def row_body(colours, me, above, below, *rest):
+        values, (up_out, down_out) = rest[:-2], rest[-2:]
+        for n, c in enumerate(colours):
 
             @pl.when(me[0] == c)
             def _():
+                a, own, b = (v[...] for v in values[3 * n : 3 * n + 3])
                 for w, out in ((above, up_out), (below, down_out)):
-                    total = dot(w[0], a[...]) + dot(w[1], own[...]) + dot(w[2], b[...])
-                    out[...] = total.astype(BF16)
-
-    def row(n, even, odd, z_even, z_odd):
+                    out[...] = (dot(w[0], a) + dot(w[1], own) + dot(w[2], b)).astype(BF16)
+
+    def row(colours, values):
         return call(
-            functools.partial(row_body, n),
-            [colour, above_mats, below_mats, *even, *odd, z_even, z_odd],
+            functools.partial(row_body, colours),
+            [colour, above_mats, below_mats, *values],
             [PAR_M, PAR_M],
             specs=[SMEM],
         )
 
     side0 = sides(z0, 0)
-    z1, skel = parent(1, skel, side0)
+    (below_pack, above_pack), z0 = after([below_pack, above_pack], z0)
+    above_mats = shift(below_pack, (1, 0), (0, 1, 3))
+    below_mats = shift(above_pack, (-1, 0), (0, 1, 3))
+    from_below, from_above = ends(z0, z0, (0,))
+    z1, skel = parent(1, skel, [3, 4], side0)
+    corners = [shift(z1, (-OFFSETS[k][0], -OFFSETS[k][1]), (1,)) for k in CORNERS]
+    sums1 = ends(*row((1,), (side0[0], z1, side0[1])), (1,))
     side1 = sides(z1, 1)
-    end0 = ends(row(0, side0, side1, z0, z1), 0)
-    z2, skel = parent(2, skel, end0)
+    z2, skel = parent(2, skel, [*ENDS, *CORNERS], [from_above, from_below, *corners])
     side2 = sides(z2, 2)
-    z3, skel = parent(3, skel, (*side2, *end0))
+    z3, skel = parent(3, skel, [3, 4], side2, sums1)
     side3 = sides(z3, 3)
-    end1 = ends(row(1, side2, side3, z2, z3), 1)
+    values = (side3[0], z2, side3[1], side2[0], z3, side2[1])
+    end1 = ends(*row((2, 3), values), (2, 3))
 
     def early_body(me, interp, couple, skel, z0, z1, z2, z3, al, ar, bl, br, skel_out, z_out):
         for c, own in enumerate((z0, z1, z2, z3)):

time: 107 us -> 103 us (0.963)
  waiting for transfers between devices: 46.8 us -> 36.2 us
  starting transfers between devices: 47.4 us -> 53 us
    ppermute x24 -> x30, waiting for transfers between devices: 46.8 us -> 36.2 us  [shift(): return lax.ppermute(x, ('bx', 'by'), pairs(*to, colours))]
    ppermute x24 -> x30, starting transfers between devices: 47.4 us -> 53 us  [shift(): return lax.ppermute(x, ('bx', 'by'), pairs(*to, colours))]
    pallas_call x19 -> x20, Pallas kernels: 10.1 us -> 11 us  [call(): pl.pallas_call(body, out_shape=[jax.ShapeDtypeStruct(s, d) for s, d in ou...]
  transfers between devices with their start and end apart: 24 -> 30, of which waited for: 12 -> 12; matrix products, arithmetic and copies ran while one was open for 1% -> 1% of each run, Pallas kernels for 4% -> 5%
where the time goes in v4:
time: 103 us; the launch traced here: 102 us
  starting transfers between devices  53 us (51%)
  waiting for transfers between devices  36.2 us (35%)
  Pallas kernels  11 us (11%)
  between operations  1.24 us (1%)
    ppermute x30, starting transfers between devices, shift(): return lax.ppermute(x, ('bx', 'by'), pairs(*to, colours))  53 us
    ppermute x30, waiting for transfers between devices, shift(): return lax.ppermute(x, ('bx', 'by'), pairs(*to, colours))  36.2 us
    pallas_call x20, Pallas kernels, call(): pl.pallas_call(body, out_shape=[jax.ShapeDtypeStruct(s, d) for s, d in ou...  11 us
  transfers between devices with their start and end apart: 30, of which 12 were waited for; matrix products, arithmetic and copies ran while one was open for 1% of the time, Pallas kernels for 5%

profile of v4, /device:TPU:70, one launch (start us, length us, event | category | flops | bytes accessed | tf_op | source)
XLA Modules:
  0.0 102.4 jit_solution(12408212594315544161)
XLA Ops:
  0.7 1.9 %shard_map.112 = (bf16[160,384]{1,0:T(8,128)(2,1)S(1)}, f32[96,384]{1,0:T(8,128)S(1)}) custom-call(f32[2,2,256,384]{3,2,1,0:T(8,128)} %rhs.3, s32[2,2,256]{2,1,0:T(2,128)} %perm.4, bf16[2,2,160,96]{3,2,1,0:T(8,128)(2,1)} %interp.20, bf16[2,2,160,160]{3,2,1,0:T(8,128)(2,1)} %piv.11), custom_call_target="tpu_custom_call" | custom-call | flops 300000000 | bytes 2000000 | tf_op jit(solution)/shard_map/pallas_call | solution.py:55
  3.6 3.8 %collective-permute-start.3 = (bf16[5,160,96]{2,1,0:T(8,128)(2,1)S(1)}, bf16[5,160,96]{2,1,0:T(8,128)(2,1)S(1)}, u32[]{:S(2)}, u32[]{:S(2)}) collective-permute-start(bf16[5,160,96]{2,1,0:T(8,128)(2,1)S(1)} %get-tuple-element.42), channel_id=1, source_target_pairs={{0,32},{1,33},{2,34},{3,35},{4,36},{5,37},{6,38},{7,39},{8,40},{9,... | collective-permute-start | bytes 460808 | tf_op jit(solution)/shard_map/ppermute | solution.py:78
  7.5 4.3 %collective-permute-start = (bf16[160,384]{1,0:T(8,128)(2,1)S(1)}, bf16[160,384]{1,0:T(8,128)(2,1)S(1)}, u32[]{:S(2)}, u32[]{:S(2)}) collective-permute-start(bf16[160,384]{1,0:T(8,128)(2,1)S(1)} %get-tuple-element.36.z.tie.left), channel_id=1, source_target_pairs={{1,0},{2,1},{3,2},{4,3},{5,4},{6,5},{7,6},{8,7},{9,8},{10,9},{11,1... | collective-permute-start | bytes 368648 | tf_op jit(solution)/shard_map/ppermute | solution.py:78
  12.6 1.6 %collective-permute-done.rest_0_.refs_1_.right = bf16[160,384]{1,0:T(8,128)(2,1)S(1)} collective-permute-done((bf16[160,384]{1,0:T(8,128)(2,1)S(1)}, bf16[160,384]{1,0:T(8,128)(2,1)S(1)}, u32[]{:S(2)}, u32[]{:S(2)}) %collective-permute-start) | collective-permute-done | bytes 122912 | tf_op jit(solution)/shard_map/ppermute | solution.py:78
  15.1 2.0 %collective-permute-start.4 = (bf16[192,384]{1,0:T(8,128)(2,1)S(1)}, bf16[192,384]{1,0:T(8,128)(2,1)S(1)}, u32[]{:S(2)}, u32[]{:S(2)}) collective-permute-start(bf16[192,384]{1,0:T(8,128)(2,1)S(1)} %shard_map.117), channel_id=1, source_target_pairs={{32,0},{33,1},{34,2},{35,3},{36,4},{37,5},{38,6},{39,7},{40,8},{41... | collective-permute-start | bytes 442376 | tf_op jit(solution)/shard_map/ppermute | solution.py:78
  17.1 1.9 %collective-permute-start.1 = (bf16[160,384]{1,0:T(8,128)(2,1)S(1)}, bf16[160,384]{1,0:T(8,128)(2,1)S(1)}, u32[]{:S(2)}, u32[]{:S(2)}) collective-permute-start(bf16[160,384]{1,0:T(8,128)(2,1)S(1)} %get-tuple-element.40.refs_0_.own), channel_id=1, source_target_pairs={{0,1},{1,2},{2,3},{3,4},{4,5},{5,6},{6,7},{7,8},{8,9},{9,10},{10,1... | collective-permute-start | bytes 368648 | tf_op jit(solution)/shard_map/ppermute | solution.py:78
  19.1 1.9 %collective-permute-start.2 = (bf16[160,384]{1,0:T(8,128)(2,1)S(1)}, bf16[160,384]{1,0:T(8,128)(2,1)S(1)}, u32[]{:S(2)}, u32[]{:S(2)}) collective-permute-start(bf16[160,384]{1,0:T(8,128)(2,1)S(1)} %get-tuple-element.40.refs_0_.own), channel_id=1, source_target_pairs={{32,1},{33,2},{34,3},{35,4},{36,5},{37,6},{38,7},{39,8},{40,9},{41... | collective-permute-start | bytes 368648 | tf_op jit(solution)/shard_map/ppermute | solution.py:78
  21.0 2.0 %collective-permute-start.8 = (bf16[5,160,96]{2,1,0:T(8,128)(2,1)S(1)}, bf16[5,160,96]{2,1,0:T(8,128)(2,1)S(1)}, u32[]{:S(2)}, u32[]{:S(2)}) collective-permute-start(bf16[5,160,96]{2,1,0:T(8,128)(2,1)S(1)} %get-tuple-element.47), channel_id=1, source_target_pairs={{32,0},{33,1},{34,2},{35,3},{36,4},{37,5},{38,6},{39,7},{40,8},{41... | collective-permute-start | bytes 460808 | tf_op jit(solution)/shard_map/ppermute | solution.py:78
  23.4 2.1 %collective-permute-done.1.rest_0_.refs_1_ = bf16[160,384]{1,0:T(8,128)(2,1)S(1)} collective-permute-done((bf16[160,384]{1,0:T(8,128)(2,1)S(1)}, bf16[160,384]{1,0:T(8,128)(2,1)S(1)}, u32[]{:S(2)}, u32[]{:S(2)}) %collective-permute-start.1) | collective-permute-done | bytes 122912 | tf_op jit(solution)/shard_map/ppermute | solution.py:78
  25.5 5.1 %collective-permute-done.2.rest_1_ = bf16[160,384]{1,0:T(8,128)(2,1)S(1)} collective-permute-done((bf16[160,384]{1,0:T(8,128)(2,1)S(1)}, bf16[160,384]{1,0:T(8,128)(2,1)S(1)}, u32[]{:S(2)}, u32[]{:S(2)}) %collective-permute-start.2) | collective-permute-done | bytes 122912 | tf_op jit(solution)/shard_map/ppermute | solution.py:78
  31.2 3.3 %collective-permute-start.5 = (bf16[160,384]{1,0:T(8,128)(2,1)S(1)}, bf16[160,384]{1,0:T(8,128)(2,1)S(1)}, u32[]{:S(2)}, u32[]{:S(2)}) collective-permute-start(bf16[160,384]{1,0:T(8,128)(2,1)S(1)} %get-tuple-element.43.refs_0_.left), channel_id=1, source_target_pairs={{1,0},{2,1},{3,2},{4,3},{5,4},{6,5},{7,6},{8,7},{9,8},{10,9},{11,1... | collective-permute-start | bytes 368648 | tf_op jit(solution)/shard_map/ppermute | solution.py:78
  34.8 2.1 %collective-permute-done.5.rest_0_.right.refs_1_ = bf16[160,384]{1,0:T(8,128)(2,1)S(1)} collective-permute-done((bf16[160,384]{1,0:T(8,128)(2,1)S(1)}, bf16[160,384]{1,0:T(8,128)(2,1)S(1)}, u32[]{:S(2)}, u32[]{:S(2)}) %collective-permute-start.5) | collective-permute-done | bytes 122912 | tf_op jit(solution)/shard_map/ppermute | solution.py:78
  37.8 5.1 %collective-permute-start.9 = (bf16[192,384]{1,0:T(8,128)(2,1)S(1)}, bf16[192,384]{1,0:T(8,128)(2,1)S(1)}, u32[]{:S(2)}, u32[]{:S(2)}) collective-permute-start(bf16[192,384]{1,0:T(8,128)(2,1)S(1)} %shard_map.122), channel_id=1, source_target_pairs={{0,32},{1,33},{2,34},{3,35},{4,36},{5,37},{6,38},{7,39},{8,40},{9,... | collective-permute-start | bytes 442376 | tf_op jit(solution)/shard_map/ppermute | solution.py:78
  42.9 1.9 %collective-permute-start.6 = (bf16[160,384]{1,0:T(8,128)(2,1)S(1)}, bf16[160,384]{1,0:T(8,128)(2,1)S(1)}, u32[]{:S(2)}, u32[]{:S(2)}) collective-permute-start(bf16[160,384]{1,0:T(8,128)(2,1)S(1)} %get-tuple-element.45.tie.own.refs_0_), channel_id=1, source_target_pairs={{0,1},{1,2},{2,3},{3,4},{4,5},{5,6},{6,7},{7,8},{8,9},{9,10},{10,1... | collective-permute-start | bytes 368648 | tf_op jit(solution)/shard_map/ppermute | solution.py:78
  44.9 1.9 %collective-permute-start.7 = (bf16[160,384]{1,0:T(8,128)(2,1)S(1)}, bf16[160,384]{1,0:T(8,128)(2,1)S(1)}, u32[]{:S(2)}, u32[]{:S(2)}) collective-permute-start(bf16[160,384]{1,0:T(8,128)(2,1)S(1)} %get-tuple-element.45.tie.own.refs_0_), channel_id=1, source_target_pairs={{0,33},{1,34},{2,35},{3,36},{4,37},{5,38},{6,39},{7,40},{8,41},{9,... | collective-permute-start | bytes 368648 | tf_op jit(solution)/shard_map/ppermute | solution.py:78
  48.2 3.0 %collective-permute-done.6.za = bf16[160,384]{1,0:T(8,128)(2,1)S(1)} collective-permute-done((bf16[160,384]{1,0:T(8,128)(2,1)S(1)}, bf16[160,384]{1,0:T(8,128)(2,1)S(1)}, u32[]{:S(2)}, u32[]{:S(2)}) %collective-permute-start.6) | collective-permute-done | bytes 122912 | tf_op jit(solution)/shard_map/ppermute | solution.py:78
  51.2 3.3 %collective-permute-done.7.zb = bf16[160,384]{1,0:T(8,128)(2,1)S(1)} collective-permute-done((bf16[160,384]{1,0:T(8,128)(2,1)S(1)}, bf16[160,384]{1,0:T(8,128)(2,1)S(1)}, u32[]{:S(2)}, u32[]{:S(2)}) %collective-permute-start.7) | collective-permute-done | bytes 122912 | tf_op jit(solution)/shard_map/ppermute | solution.py:78
  54.5 1.2 %shard_map.124 = (f32[128,384]{1,0:T(8,128)S(1)}, f32[256,384]{1,0:T(8,128)S(1)}, bf16[256,384]{1,0:T(8,128)(2,1)S(1)}) custom-call(s32[1]{0:T(128)} %bitcast.6.me, bf16[384,384]{1,0:T(8,128)(2,1)S(1)} %get-tuple-element.46.pick, bf16[1,1,256,128]{3,2,1,0:T(8,128)(2,1)S(1)} %copy-done.6, bf16[1,1,256,256]{3,2,1,0:T(8,128)(2,1)S(1)} %copy-done.5, ...), custom_call_target="tpu_custom_call" | custom-call | flops 300000000 | bytes 2000000 | tf_op jit(solution)/shard_map/pallas_call | solution.py:55
  55.7 1.3 %collective-permute-start.10 = (bf16[256,384]{1,0:T(8,128)(2,1)S(1)}, bf16[256,384]{1,0:T(8,128)(2,1)S(1)}, u32[]{:S(2)}, u32[]{:S(2)}) collective-permute-start(bf16[256,384]{1,0:T(8,128)(2,1)S(1)} %get-tuple-element.55.z0), channel_id=1, source_target_pairs={{0,1},{2,3},{4,5},{6,7},{8,9},{10,11},{12,13},{14,15},{16,17},{18,... | collective-permute-start | bytes 589832 | tf_op jit(solution)/shard_map/ppermute | solution.py:78
  57.0 2.6 %collective-permute-start.11 = (bf16[256,384]{1,0:T(8,128)(2,1)S(1)}, bf16[256,384]{1,0:T(8,128)(2,1)S(1)}, u32[]{:S(2)}, u32[]{:S(2)}) collective-permute-start(bf16[256,384]{1,0:T(8,128)(2,1)S(1)} %get-tuple-element.55.z0), channel_id=1, source_target_pairs={{2,1},{4,3},{6,5},{8,7},{10,9},{12,11},{14,13},{16,15},{18,17},{20... | collective-permute-start | bytes 589832 | tf_op jit(solution)/shard_map/ppermute | solution.py:78
  59.7 1.3 %collective-permute-start.12 = (bf16[256,384]{1,0:T(8,128)(2,1)S(1)}, bf16[256,384]{1,0:T(8,128)(2,1)S(1)}, u32[]{:S(2)}, u32[]{:S(2)}) collective-permute-start(bf16[256,384]{1,0:T(8,128)(2,1)S(1)} %get-tuple-element.55.z0), channel_id=1, source_target_pairs={{0,32},{2,34},{4,36},{6,38},{8,40},{10,42},{12,44},{14,46},{16,48}... | collective-permute-start | bytes 589832 | tf_op jit(solution)/shard_map/ppermute | solution.py:78
  61.0 1.3 %collective-permute-start.13 = (bf16[256,384]{1,0:T(8,128)(2,1)S(1)}, bf16[256,384]{1,0:T(8,128)(2,1)S(1)}, u32[]{:S(2)}, u32[]{:S(2)}) collective-permute-start(bf16[256,384]{1,0:T(8,128)(2,1)S(1)} %get-tuple-element.55.z0), channel_id=1, source_target_pairs={{64,32},{66,34},{68,36},{70,38},{72,40},{74,42},{76,44},{78,46},{8... | collective-permute-start | bytes 589832 | tf_op jit(solution)/shard_map/ppermute | solution.py:78
  64.9 1.3 %collective-permute-done.12.rest_0_ = bf16[256,384]{1,0:T(8,128)(2,1)S(1)} collective-permute-done((bf16[256,384]{1,0:T(8,128)(2,1)S(1)}, bf16[256,384]{1,0:T(8,128)(2,1)S(1)}, u32[]{:S(2)}, u32[]{:S(2)}) %collective-permute-start.12) | collective-permute-done | bytes 196640 | tf_op jit(solution)/shard_map/ppermute | solution.py:78
  66.9 5.0 %collective-permute-start.20 = (bf16[3,128,256]{2,1,0:T(8,128)(2,1)S(1)}, bf16[3,128,256]{2,1,0:T(8,128)(2,1)S(1)}, u32[]{:S(2)}, u32[]{:S(2)}) collective-permute-start(bf16[3,128,256]{2,1,0:T(8,128)(2,1)S(1)} %get-tuple-element.59), channel_id=1, source_target_pairs={{0,32},{1,33},{2,34},{3,35},{4,36},{5,37},{6,38},{7,39},{8,40},{9,... | collective-permute-start | bytes 589832 | tf_op jit(solution)/shard_map/ppermute | solution.py:78
  72.0 1.3 %collective-permute-start.21 = (bf16[3,128,256]{2,1,0:T(8,128)(2,1)S(1)}, bf16[3,128,256]{2,1,0:T(8,128)(2,1)S(1)}, u32[]{:S(2)}, u32[]{:S(2)}) collective-permute-start(bf16[3,128,256]{2,1,0:T(8,128)(2,1)S(1)} %get-tuple-element.60), channel_id=1, source_target_pairs={{33,1},{35,3},{37,5},{39,7},{41,9},{43,11},{45,13},{47,15},{49,17}... | collective-permute-start | bytes 589832 | tf_op jit(solution)/shard_map/ppermute | solution.py:78
  75.1 1.5 %collective-permute-done.21.below = bf16[3,128,256]{2,1,0:T(8,128)(2,1)S(1)} collective-permute-done((bf16[3,128,256]{2,1,0:T(8,128)(2,1)S(1)}, bf16[3,128,256]{2,1,0:T(8,128)(2,1)S(1)}, u32[]{:S(2)}, u32[]{:S(2)}) %collective-permute-start.21) | collective-permute-done | bytes 196640 | tf_op jit(solution)/shard_map/ppermute | solution.py:78
  79.4 1.3 %collective-permute-start.24 = (bf16[256,384]{1,0:T(8,128)(2,1)S(1)}, bf16[256,384]{1,0:T(8,128)(2,1)S(1)}, u32[]{:S(2)}, u32[]{:S(2)}) collective-permute-start(bf16[256,384]{1,0:T(8,128)(2,1)S(1)} %get-tuple-element.56.rest_1_.z1), channel_id=1, source_target_pairs={{1,2},{3,4},{5,6},{7,8},{9,10},{11,12},{13,14},{15,16},{17,18},{19... | collective-permute-start | bytes 589832 | tf_op jit(solution)/shard_map/ppermute | solution.py:78
  80.7 1.3 %collective-permute-start.25 = (bf16[256,384]{1,0:T(8,128)(2,1)S(1)}, bf16[256,384]{1,0:T(8,128)(2,1)S(1)}, u32[]{:S(2)}, u32[]{:S(2)}) collective-permute-start(bf16[256,384]{1,0:T(8,128)(2,1)S(1)} %get-tuple-element.56.rest_1_.z1), channel_id=1, source_target_pairs={{1,0},{3,2},{5,4},{7,6},{9,8},{11,10},{13,12},{15,14},{17,16},{19,... | collective-permute-start | bytes 589832 | tf_op jit(solution)/shard_map/ppermute | solution.py:78
  82.0 1.3 %collective-permute-start.28 = (bf16[128,384]{1,0:T(8,128)(2,1)S(1)}, bf16[128,384]{1,0:T(8,128)(2,1)S(1)}, u32[]{:S(2)}, u32[]{:S(2)}) collective-permute-start(bf16[128,384]{1,0:T(8,128)(2,1)S(1)} %get-tuple-element.67), channel_id=1, source_target_pairs={{32,0},{33,1},{34,2},{35,3},{36,4},{37,5},{38,6},{39,7},{40,8},{41... | collective-permute-start | bytes 294920 | tf_op jit(solution)/shard_map/ppermute | solution.py:78
  83.3 1.3 %collective-permute-start.29 = (bf16[128,384]{1,0:T(8,128)(2,1)S(1)}, bf16[128,384]{1,0:T(8,128)(2,1)S(1)}, u32[]{:S(2)}, u32[]{:S(2)}) collective-permute-start(bf16[128,384]{1,0:T(8,128)(2,1)S(1)} %get-tuple-element.68), channel_id=1, source_target_pairs={{32,64},{33,65},{34,66},{35,67},{36,68},{37,69},{38,70},{39,71},{4... | collective-permute-start | bytes 294920 | tf_op jit(solution)/shard_map/ppermute | solution.py:78
  85.5 10.6 %collective-permute-done.24.al = bf16[256,384]{1,0:T(8,128)(2,1)S(1)} collective-permute-done((bf16[256,384]{1,0:T(8,128)(2,1)S(1)}, bf16[256,384]{1,0:T(8,128)(2,1)S(1)}, u32[]{:S(2)}, u32[]{:S(2)}) %collective-permute-start.24) | collective-permute-done | bytes 196640 | tf_op jit(solution)/shard_map/ppermute | solution.py:78
  97.1 4.6 %collective-permute-done.28.a = bf16[128,384]{1,0:T(8,128)(2,1)S(1)} collective-permute-done((bf16[128,384]{1,0:T(8,128)(2,1)S(1)}, bf16[128,384]{1,0:T(8,128)(2,1)S(1)}, u32[]{:S(2)}, u32[]{:S(2)}) %collective-permute-start.28) | collective-permute-done | bytes 98336 | tf_op jit(solution)/shard_map/ppermute | solution.py:78
  (67 shorter events, 16.6 us)
Async XLA Ops:
  3.6 11.2 %collective-permute-start.3 = (bf16[5,160,96]{2,1,0:T(8,128)(2,1)S(1)}, bf16[5,160,96]{2,1,0:T(8,128)(2,1)S(1)}, u32[]{:S(2)}, u32[]{:S(2)}) collective-permute-start(bf16[5,160,96]{2,1,0:T(8,128)(2,1)S(1)} %get-tuple-element.42), channel_id=1, source_target_pairs={{0,32},{1,33},{2,34},{3,35},{4,36},{5,37},{6,38},{7,39},{8,40},{9,... | collective-permute-start | bytes 460808 | tf_op jit(solution)/shard_map/ppermute | solution.py:78
  7.5 6.8 %collective-permute-start = (bf16[160,384]{1,0:T(8,128)(2,1)S(1)}, bf16[160,384]{1,0:T(8,128)(2,1)S(1)}, u32[]{:S(2)}, u32[]{:S(2)}) collective-permute-start(bf16[160,384]{1,0:T(8,128)(2,1)S(1)} %get-tuple-element.36.z.tie.left), channel_id=1, source_target_pairs={{1,0},{2,1},{3,2},{4,3},{5,4},{6,5},{7,6},{8,7},{9,8},{10,9},{11,1... | collective-permute-start | bytes 368648 | tf_op jit(solution)/shard_map/ppermute | solution.py:78
  15.1 15.5 %collective-permute-start.4 = (bf16[192,384]{1,0:T(8,128)(2,1)S(1)}, bf16[192,384]{1,0:T(8,128)(2,1)S(1)}, u32[]{:S(2)}, u32[]{:S(2)}) collective-permute-start(bf16[192,384]{1,0:T(8,128)(2,1)S(1)} %shard_map.117), channel_id=1, source_target_pairs={{32,0},{33,1},{34,2},{35,3},{36,4},{37,5},{38,6},{39,7},{40,8},{41... | collective-permute-start | bytes 442376 | tf_op jit(solution)/shard_map/ppermute | solution.py:78
  17.1 8.3 %collective-permute-start.1 = (bf16[160,384]{1,0:T(8,128)(2,1)S(1)}, bf16[160,384]{1,0:T(8,128)(2,1)S(1)}, u32[]{:S(2)}, u32[]{:S(2)}) collective-permute-start(bf16[160,384]{1,0:T(8,128)(2,1)S(1)} %get-tuple-element.40.refs_0_.own), channel_id=1, source_target_pairs={{0,1},{1,2},{2,3},{3,4},{4,5},{5,6},{6,7},{7,8},{8,9},{9,10},{10,1... | collective-permute-start | bytes 368648 | tf_op jit(solution)/shard_map/ppermute | solution.py:78
  19.1 11.5 %collective-permute-start.2 = (bf16[160,384]{1,0:T(8,128)(2,1)S(1)}, bf16[160,384]{1,0:T(8,128)(2,1)S(1)}, u32[]{:S(2)}, u32[]{:S(2)}) collective-permute-start(bf16[160,384]{1,0:T(8,128)(2,1)S(1)} %get-tuple-element.40.refs_0_.own), channel_id=1, source_target_pairs={{32,1},{33,2},{34,3},{35,4},{36,5},{37,6},{38,7},{39,8},{40,9},{41... | collective-permute-start | bytes 368648 | tf_op jit(solution)/shard_map/ppermute | solution.py:78
  21.0 16.4 %collective-permute-start.8 = (bf16[5,160,96]{2,1,0:T(8,128)(2,1)S(1)}, bf16[5,160,96]{2,1,0:T(8,128)(2,1)S(1)}, u32[]{:S(2)}, u32[]{:S(2)}) collective-permute-start(bf16[5,160,96]{2,1,0:T(8,128)(2,1)S(1)} %get-tuple-element.47), channel_id=1, source_target_pairs={{32,0},{33,1},{34,2},{35,3},{36,4},{37,5},{38,6},{39,7},{40,8},{41... | collective-permute-start | bytes 460808 | tf_op jit(solution)/shard_map/ppermute | solution.py:78
  31.2 5.7 %collective-permute-start.5 = (bf16[160,384]{1,0:T(8,128)(2,1)S(1)}, bf16[160,384]{1,0:T(8,128)(2,1)S(1)}, u32[]{:S(2)}, u32[]{:S(2)}) collective-permute-start(bf16[160,384]{1,0:T(8,128)(2,1)S(1)} %get-tuple-element.43.refs_0_.left), channel_id=1, source_target_pairs={{1,0},{2,1},{3,2},{4,3},{5,4},{6,5},{7,6},{8,7},{9,8},{10,9},{11,1... | collective-permute-start | bytes 368648 | tf_op jit(solution)/shard_map/ppermute | solution.py:78
  34.8 12.0 %copy-start.8 = (s32[1,1,384]{2,1,0:T(1,128)S(1)}, s32[1,1,384]{2,1,0:T(1,128)}, u32[]{:S(2)}) copy-start(s32[1,1,384]{2,1,0:T(1,128)} %perm.5) | copy-start | bytes 4612
  37.8 16.8 %collective-permute-start.9 = (bf16[192,384]{1,0:T(8,128)(2,1)S(1)}, bf16[192,384]{1,0:T(8,128)(2,1)S(1)}, u32[]{:S(2)}, u32[]{:S(2)}) collective-permute-start(bf16[192,384]{1,0:T(8,128)(2,1)S(1)} %shard_map.122), channel_id=1, source_target_pairs={{0,32},{1,33},{2,34},{3,35},{4,36},{5,37},{6,38},{7,39},{8,40},{9,... | collective-permute-start | bytes 442376 | tf_op jit(solution)/shard_map/ppermute | solution.py:78
  42.9 8.3 %collective-permute-start.6 = (bf16[160,384]{1,0:T(8,128)(2,1)S(1)}, bf16[160,384]{1,0:T(8,128)(2,1)S(1)}, u32[]{:S(2)}, u32[]{:S(2)}) collective-permute-start(bf16[160,384]{1,0:T(8,128)(2,1)S(1)} %get-tuple-element.45.tie.own.refs_0_), channel_id=1, source_target_pairs={{0,1},{1,2},{2,3},{3,4},{4,5},{5,6},{6,7},{7,8},{8,9},{9,10},{10,1... | collective-permute-start | bytes 368648 | tf_op jit(solution)/shard_map/ppermute | solution.py:78
  44.9 9.7 %collective-permute-start.7 = (bf16[160,384]{1,0:T(8,128)(2,1)S(1)}, bf16[160,384]{1,0:T(8,128)(2,1)S(1)}, u32[]{:S(2)}, u32[]{:S(2)}) collective-permute-start(bf16[160,384]{1,0:T(8,128)(2,1)S(1)} %get-tuple-element.45.tie.own.refs_0_), channel_id=1, source_target_pairs={{0,33},{1,34},{2,35},{3,36},{4,37},{5,38},{6,39},{7,40},{8,41},{9,... | collective-permute-start | bytes 368648 | tf_op jit(solution)/shard_map/ppermute | solution.py:78
  48.2 14.6 %copy-start.2 = (bf16[1,1,8,128,256]{4,3,2,1,0:T(8,128)(2,1)S(1)}, bf16[1,1,8,128,256]{4,3,2,1,0:T(8,128)(2,1)}, u32[]{:S(2)}) copy-start(bf16[1,1,8,128,256]{4,3,2,1,0:T(8,128)(2,1)} %couple.9) | copy-start | bytes 1572868
  55.7 6.6 %collective-permute-start.10 = (bf16[256,384]{1,0:T(8,128)(2,1)S(1)}, bf16[256,384]{1,0:T(8,128)(2,1)S(1)}, u32[]{:S(2)}, u32[]{:S(2)}) collective-permute-start(bf16[256,384]{1,0:T(8,128)(2,1)S(1)} %get-tuple-element.55.z0), channel_id=1, source_target_pairs={{0,1},{2,3},{4,5},{6,7},{8,9},{10,11},{12,13},{14,15},{16,17},{18,... | collective-permute-start | bytes 589832 | tf_op jit(solution)/shard_map/ppermute | solution.py:78
  57.0 5.8 %collective-permute-start.11 = (bf16[256,384]{1,0:T(8,128)(2,1)S(1)}, bf16[256,384]{1,0:T(8,128)(2,1)S(1)}, u32[]{:S(2)}, u32[]{:S(2)}) collective-permute-start(bf16[256,384]{1,0:T(8,128)(2,1)S(1)} %get-tuple-element.55.z0), channel_id=1, source_target_pairs={{2,1},{4,3},{6,5},{8,7},{10,9},{12,11},{14,13},{16,15},{18,17},{20... | collective-permute-start | bytes 589832 | tf_op jit(solution)/shard_map/ppermute | solution.py:78
  59.7 6.6 %collective-permute-start.12 = (bf16[256,384]{1,0:T(8,128)(2,1)S(1)}, bf16[256,384]{1,0:T(8,128)(2,1)S(1)}, u32[]{:S(2)}, u32[]{:S(2)}) collective-permute-start(bf16[256,384]{1,0:T(8,128)(2,1)S(1)} %get-tuple-element.55.z0), channel_id=1, source_target_pairs={{0,32},{2,34},{4,36},{6,38},{8,40},{10,42},{12,44},{14,46},{16,48}... | collective-permute-start | bytes 589832 | tf_op jit(solution)/shard_map/ppermute | solution.py:78
  61.0 5.9 %collective-permute-start.13 = (bf16[256,384]{1,0:T(8,128)(2,1)S(1)}, bf16[256,384]{1,0:T(8,128)(2,1)S(1)}, u32[]{:S(2)}, u32[]{:S(2)}) collective-permute-start(bf16[256,384]{1,0:T(8,128)(2,1)S(1)} %get-tuple-element.55.z0), channel_id=1, source_target_pairs={{64,32},{66,34},{68,36},{70,38},{72,40},{74,42},{76,44},{78,46},{8... | collective-permute-start | bytes 589832 | tf_op jit(solution)/shard_map/ppermute | solution.py:78
  62.9 9.1 %collective-permute-start.14 = (bf16[256,384]{1,0:T(8,128)(2,1)S(1)}, bf16[256,384]{1,0:T(8,128)(2,1)S(1)}, u32[]{:S(2)}, u32[]{:S(2)}) collective-permute-start(bf16[256,384]{1,0:T(8,128)(2,1)S(1)} %get-tuple-element.56.rest_1_.z1), channel_id=1, source_target_pairs={{1,34},{3,36},{5,38},{7,40},{9,42},{11,44},{13,46},{15,48},{17,50}... | collective-permute-start | bytes 589832 | tf_op jit(solution)/shard_map/ppermute | solution.py:78
  63.6 9.7 %collective-permute-start.15 = (bf16[256,384]{1,0:T(8,128)(2,1)S(1)}, bf16[256,384]{1,0:T(8,128)(2,1)S(1)}, u32[]{:S(2)}, u32[]{:S(2)}) collective-permute-start(bf16[256,384]{1,0:T(8,128)(2,1)S(1)} %get-tuple-element.56.rest_1_.z1), channel_id=1, source_target_pairs={{1,32},{3,34},{5,36},{7,38},{9,40},{11,42},{13,44},{15,46},{17,48}... | collective-permute-start | bytes 589832 | tf_op jit(solution)/shard_map/ppermute | solution.py:78
  64.2 9.1 %collective-permute-start.16 = (bf16[256,384]{1,0:T(8,128)(2,1)S(1)}, bf16[256,384]{1,0:T(8,128)(2,1)S(1)}, u32[]{:S(2)}, u32[]{:S(2)}) collective-permute-start(bf16[256,384]{1,0:T(8,128)(2,1)S(1)} %get-tuple-element.56.rest_1_.z1), channel_id=1, source_target_pairs={{65,34},{67,36},{69,38},{71,40},{73,42},{75,44},{77,46},{79,48},{8... | collective-permute-start | bytes 589832 | tf_op jit(solution)/shard_map/ppermute | solution.py:78
  66.3 7.0 %collective-permute-start.17 = (bf16[256,384]{1,0:T(8,128)(2,1)S(1)}, bf16[256,384]{1,0:T(8,128)(2,1)S(1)}, u32[]{:S(2)}, u32[]{:S(2)}) collective-permute-start(bf16[256,384]{1,0:T(8,128)(2,1)S(1)} %get-tuple-element.56.rest_1_.z1), channel_id=1, source_target_pairs={{65,32},{67,34},{69,36},{71,38},{73,40},{75,42},{77,44},{79,46},{8... | collective-permute-start | bytes 589832 | tf_op jit(solution)/shard_map/ppermute | solution.py:78
  66.9 8.2 %collective-permute-start.20 = (bf16[3,128,256]{2,1,0:T(8,128)(2,1)S(1)}, bf16[3,128,256]{2,1,0:T(8,128)(2,1)S(1)}, u32[]{:S(2)}, u32[]{:S(2)}) collective-permute-start(bf16[3,128,256]{2,1,0:T(8,128)(2,1)S(1)} %get-tuple-element.59), channel_id=1, source_target_pairs={{0,32},{1,33},{2,34},{3,35},{4,36},{5,37},{6,38},{7,39},{8,40},{9,... | collective-permute-start | bytes 589832 | tf_op jit(solution)/shard_map/ppermute | solution.py:78
  72.0 4.6 %collective-permute-start.21 = (bf16[3,128,256]{2,1,0:T(8,128)(2,1)S(1)}, bf16[3,128,256]{2,1,0:T(8,128)(2,1)S(1)}, u32[]{:S(2)}, u32[]{:S(2)}) collective-permute-start(bf16[3,128,256]{2,1,0:T(8,128)(2,1)S(1)} %get-tuple-element.60), channel_id=1, source_target_pairs={{33,1},{35,3},{37,5},{39,7},{41,9},{43,11},{45,13},{47,15},{49,17}... | collective-permute-start | bytes 589832 | tf_op jit(solution)/shard_map/ppermute | solution.py:78
  73.3 4.6 %collective-permute-start.18 = (bf16[256,384]{1,0:T(8,128)(2,1)S(1)}, bf16[256,384]{1,0:T(8,128)(2,1)S(1)}, u32[]{:S(2)}, u32[]{:S(2)}) collective-permute-start(bf16[256,384]{1,0:T(8,128)(2,1)S(1)} %get-tuple-element.58.z2.rest_1_), channel_id=1, source_target_pairs={{32,33},{34,35},{36,37},{38,39},{40,41},{42,43},{44,45},{46,47},{4... | collective-permute-start | bytes 589832 | tf_op jit(solution)/shard_map/ppermute | solution.py:78
  74.0 3.9 %collective-permute-start.19 = (bf16[256,384]{1,0:T(8,128)(2,1)S(1)}, bf16[256,384]{1,0:T(8,128)(2,1)S(1)}, u32[]{:S(2)}, u32[]{:S(2)}) collective-permute-start(bf16[256,384]{1,0:T(8,128)(2,1)S(1)} %get-tuple-element.58.z2.rest_1_), channel_id=1, source_target_pairs={{34,33},{36,35},{38,37},{40,39},{42,41},{44,43},{46,45},{48,47},{5... | collective-permute-start | bytes 589832 | tf_op jit(solution)/shard_map/ppermute | solution.py:78
  76.6 1.3 %collective-permute-start.22 = (bf16[128,384]{1,0:T(8,128)(2,1)S(1)}, bf16[128,384]{1,0:T(8,128)(2,1)S(1)}, u32[]{:S(2)}, u32[]{:S(2)}) collective-permute-start(bf16[128,384]{1,0:T(8,128)(2,1)S(1)} %get-tuple-element.61), channel_id=1, source_target_pairs={{65,33},{67,35},{69,37},{71,39},{73,41},{75,43},{77,45},{79,47},{8... | collective-permute-start | bytes 294920 | tf_op jit(solution)/shard_map/ppermute | solution.py:78
  77.3 0.7 collective-permute-start.23
  78.0 4.0 %collective-permute-start.26 = (bf16[256,384]{1,0:T(8,128)(2,1)S(1)}, bf16[256,384]{1,0:T(8,128)(2,1)S(1)}, u32[]{:S(2)}, u32[]{:S(2)}) collective-permute-start(bf16[256,384]{1,0:T(8,128)(2,1)S(1)} %get-tuple-element.64.z3.rest_4_), channel_id=1, source_target_pairs={{33,34},{35,36},{37,38},{39,40},{41,42},{43,44},{45,46},{47,48},{4... | collective-permute-start | bytes 589832 | tf_op jit(solution)/shard_map/ppermute | solution.py:78
  78.7 3.3 %collective-permute-start.27 = (bf16[256,384]{1,0:T(8,128)(2,1)S(1)}, bf16[256,384]{1,0:T(8,128)(2,1)S(1)}, u32[]{:S(2)}, u32[]{:S(2)}) collective-permute-start(bf16[256,384]{1,0:T(8,128)(2,1)S(1)} %get-tuple-element.64.z3.rest_4_), channel_id=1, source_target_pairs={{33,32},{35,34},{37,36},{39,38},{41,40},{43,42},{45,44},{47,46},{4... | collective-permute-start | bytes 589832 | tf_op jit(solution)/shard_map/ppermute | solution.py:78
  79.4 16.7 %collective-permute-start.24 = (bf16[256,384]{1,0:T(8,128)(2,1)S(1)}, bf16[256,384]{1,0:T(8,128)(2,1)S(1)}, u32[]{:S(2)}, u32[]{:S(2)}) collective-permute-start(bf16[256,384]{1,0:T(8,128)(2,1)S(1)} %get-tuple-element.56.rest_1_.z1), channel_id=1, source_target_pairs={{1,2},{3,4},{5,6},{7,8},{9,10},{11,12},{13,14},{15,16},{17,18},{19... | collective-permute-start | bytes 589832 | tf_op jit(solution)/shard_map/ppermute | solution.py:78
  80.7 15.4 %collective-permute-start.25 = (bf16[256,384]{1,0:T(8,128)(2,1)S(1)}, bf16[256,384]{1,0:T(8,128)(2,1)S(1)}, u32[]{:S(2)}, u32[]{:S(2)}) collective-permute-start(bf16[256,384]{1,0:T(8,128)(2,1)S(1)} %get-tuple-element.56.rest_1_.z1), channel_id=1, source_target_pairs={{1,0},{3,2},{5,4},{7,6},{9,8},{11,10},{13,12},{15,14},{17,16},{19,... | collective-permute-start | bytes 589832 | tf_op jit(solution)/shard_map/ppermute | solution.py:78
  82.0 19.6 %collective-permute-start.28 = (bf16[128,384]{1,0:T(8,128)(2,1)S(1)}, bf16[128,384]{1,0:T(8,128)(2,1)S(1)}, u32[]{:S(2)}, u32[]{:S(2)}) collective-permute-start(bf16[128,384]{1,0:T(8,128)(2,1)S(1)} %get-tuple-element.67), channel_id=1, source_target_pairs={{32,0},{33,1},{34,2},{35,3},{36,4},{37,5},{38,6},{39,7},{40,8},{41... | collective-permute-start | bytes 294920 | tf_op jit(solution)/shard_map/ppermute | solution.py:78
  83.3 18.3 %collective-permute-start.29 = (bf16[128,384]{1,0:T(8,128)(2,1)S(1)}, bf16[128,384]{1,0:T(8,128)(2,1)S(1)}, u32[]{:S(2)}, u32[]{:S(2)}) collective-permute-start(bf16[128,384]{1,0:T(8,128)(2,1)S(1)} %get-tuple-element.68), channel_id=1, source_target_pairs={{32,64},{33,65},{34,66},{35,67},{36,68},{37,69},{38,70},{39,71},{4... | collective-permute-start | bytes 294920 | tf_op jit(solution)/shard_map/ppermute | solution.py:78
  (7 other events, 60.4 us)

commit v5 on v4

--- a/solution.py
+++ b/solution.py
@@ -296,14 +296,20 @@
         specs=[SMEM],
     )
 
-    def sides(z, c):
-        return shift(z, (0, 1), (c,)), shift(z, (0, -1), (c,))
+    def sides(z, colours):
+        return shift(z, (0, 1), colours), shift(z, (0, -1), colours)
 
     def ends(up, down, colours):
         return shift(up, (-1, 0), colours), shift(down, (1, 0), colours)
 
     def parent_body(c, ks, n_sums, me, interp, piv, couple, skel, red, *rest):
-        zs, sums, (z_out, skel_out) = rest[: len(ks)], rest[len(ks) : len(ks) + n_sums], rest[len(ks) + n_sums :]
+        zs, sums = rest[: len(ks)], rest[len(ks) : len(ks) + n_sums]
+        *held, z_out, skel_out = rest[len(ks) + n_sums :]
+        if held:
+
+            @pl.when(me[0] == c - 1)
+            def _():
+                z_out[...] = held[0][...]
 
         @pl.when(me[0] != c)
         def _():
@@ -319,10 +325,10 @@
             skel_out[...] = acc
             z_out[...] = solve_parent(interp, piv, acc, red[...])
 
-    def parent(c, skel, ks, zs, sums=()):
+    def parent(c, skel, ks, zs, sums=(), held=()):
         return call(
             functools.partial(parent_body, c, ks, len(sums)),
-            [colour, interp2, pivinv2, couple2, skel, red, *zs, *sums],
+            [colour, interp2, pivinv2, couple2, skel, red, *zs, *sums, *held],
             [PAR_Z, PAR_S],
             specs=[SMEM],
         )
@@ -345,19 +351,18 @@
             specs=[SMEM],
         )
 
-    side0 = sides(z0, 0)
+    side0 = sides(z0, (0,))
+    z1, skel = parent(1, skel, [3, 4], side0)
+    corners = [shift(z1, (-OFFSETS[k][0], -OFFSETS[k][1]), (1,)) for k in CORNERS]
     (below_pack, above_pack), z0 = after([below_pack, above_pack], z0)
     above_mats = shift(below_pack, (1, 0), (0, 1, 3))
     below_mats = shift(above_pack, (-1, 0), (0, 1, 3))
     from_below, from_above = ends(z0, z0, (0,))
-    z1, skel = parent(1, skel, [3, 4], side0)
-    corners = [shift(z1, (-OFFSETS[k][0], -OFFSETS[k][1]), (1,)) for k in CORNERS]
+    z2, skel = parent(2, skel, [*ENDS, *CORNERS], [from_above, from_below, *corners], held=[z1])
+    side2 = sides(z2, (1, 2))
     sums1 = ends(*row((1,), (side0[0], z1, side0[1])), (1,))
-    side1 = sides(z1, 1)
-    z2, skel = parent(2, skel, [*ENDS, *CORNERS], [from_above, from_below, *corners])
-    side2 = sides(z2, 2)
     z3, skel = parent(3, skel, [3, 4], side2, sums1)
-    side3 = sides(z3, 3)
+    side3 = sides(z3, (3,))
     values = (side3[0], z2, side3[1], side2[0], z3, side2[1])
     end1 = ends(*row((2, 3), values), (2, 3))
 
@@ -375,7 +380,7 @@
                 skel_out[...] = acc
 
     skel, red2 = call(
-        early_body, [colour, interp2, couple2, skel, z0, z1, z2, z3, *side1, *side3], [PAR_S, PAR_Z], specs=[SMEM]
+        early_body, [colour, interp2, couple2, skel, z0, z1, z2, z3, *side2, *side3], [PAR_S, PAR_Z], specs=[SMEM]
     )
 
     def late_body(me, skel, a, b, skel_out):

time: 103 us -> 103 us (level)
  waiting for transfers between devices: 36.2 us -> 38.9 us
  starting transfers between devices: 53 us -> 50.7 us
    ppermute x30 -> x28, waiting for transfers between devices: 36.2 us -> 38.9 us  [shift(): return lax.ppermute(x, ('bx', 'by'), pairs(*to, colours))]
    ppermute x30 -> x28, starting transfers between devices: 53 us -> 50.7 us  [shift(): return lax.ppermute(x, ('bx', 'by'), pairs(*to, colours))]
  transfers between devices with their start and end apart: 30 -> 28, of which waited for: 12 -> 11; matrix products, arithmetic and copies ran while one was open for 1% -> 1% of each run, Pallas kernels for 5% -> 5%
where the time goes in v5:
time: 103 us
  starting transfers between devices  50.7 us (49%)
  waiting for transfers between devices  38.9 us (38%)
  Pallas kernels  11 us (11%)
  between operations  1.23 us (1%)
    ppermute x28, starting transfers between devices, shift(): return lax.ppermute(x, ('bx', 'by'), pairs(*to, colours))  50.7 us
    ppermute x28, waiting for transfers between devices, shift(): return lax.ppermute(x, ('bx', 'by'), pairs(*to, colours))  38.9 us
    pallas_call x20, Pallas kernels, call(): pl.pallas_call(body, out_shape=[jax.ShapeDtypeStruct(s, d) for s, d in ou...  11 us
  transfers between devices with their start and end apart: 28, of which 11 were waited for; matrix products, arithmetic and copies ran while one was open for 1% of the time, Pallas kernels for 5%

profile of v5, /device:TPU:70, one launch (start us, length us, event | category | flops | bytes accessed | tf_op | source)
XLA Modules:
  0.0 102.7 jit_solution(2225276443181986903)
XLA Ops:
  0.7 1.9 %shard_map.112 = (bf16[160,384]{1,0:T(8,128)(2,1)S(1)}, f32[96,384]{1,0:T(8,128)S(1)}) custom-call(f32[2,2,256,384]{3,2,1,0:T(8,128)} %rhs.3, s32[2,2,256]{2,1,0:T(2,128)} %perm.4, bf16[2,2,160,96]{3,2,1,0:T(8,128)(2,1)} %interp.20, bf16[2,2,160,160]{3,2,1,0:T(8,128)(2,1)} %piv.11), custom_call_target="tpu_custom_call" | custom-call | flops 300000000 | bytes 2000000 | tf_op jit(solution)/shard_map/pallas_call | solution.py:55
  2.5 1.1 %shard_map.116 = (bf16[5,160,96]{2,1,0:T(8,128)(2,1)S(1)}, bf16[5,160,96]{2,1,0:T(8,128)(2,1)S(1)}) custom-call(bf16[2,2,8,160,96]{4,3,2,1,0:T(8,128)(2,1)} %bitcast.9, bf16[160,384]{1,0:T(8,128)(2,1)S(1)} %get-tuple-element.36.z.tie.left), custom_call_target="tpu_custom_call" | custom-call | flops 300000000 | bytes 2000000 | tf_op jit(solution)/shard_map/pallas_call | solution.py:55
  3.6 3.8 %collective-permute-start.3 = (bf16[5,160,96]{2,1,0:T(8,128)(2,1)S(1)}, bf16[5,160,96]{2,1,0:T(8,128)(2,1)S(1)}, u32[]{:S(2)}, u32[]{:S(2)}) collective-permute-start(bf16[5,160,96]{2,1,0:T(8,128)(2,1)S(1)} %get-tuple-element.42), channel_id=1, source_target_pairs={{0,32},{1,33},{2,34},{3,35},{4,36},{5,37},{6,38},{7,39},{8,40},{9,... | collective-permute-start | bytes 460808 | tf_op jit(solution)/shard_map/ppermute | solution.py:78
  7.5 4.3 %collective-permute-start = (bf16[160,384]{1,0:T(8,128)(2,1)S(1)}, bf16[160,384]{1,0:T(8,128)(2,1)S(1)}, u32[]{:S(2)}, u32[]{:S(2)}) collective-permute-start(bf16[160,384]{1,0:T(8,128)(2,1)S(1)} %get-tuple-element.36.z.tie.left), channel_id=1, source_target_pairs={{1,0},{2,1},{3,2},{4,3},{5,4},{6,5},{7,6},{8,7},{9,8},{10,9},{11,1... | collective-permute-start | bytes 368648 | tf_op jit(solution)/shard_map/ppermute | solution.py:78
  12.6 1.6 %collective-permute-done.rest_0_.refs_1_.right = bf16[160,384]{1,0:T(8,128)(2,1)S(1)} collective-permute-done((bf16[160,384]{1,0:T(8,128)(2,1)S(1)}, bf16[160,384]{1,0:T(8,128)(2,1)S(1)}, u32[]{:S(2)}, u32[]{:S(2)}) %collective-permute-start) | collective-permute-done | bytes 122912 | tf_op jit(solution)/shard_map/ppermute | solution.py:78
  15.1 2.0 %collective-permute-start.4 = (bf16[192,384]{1,0:T(8,128)(2,1)S(1)}, bf16[192,384]{1,0:T(8,128)(2,1)S(1)}, u32[]{:S(2)}, u32[]{:S(2)}) collective-permute-start(bf16[192,384]{1,0:T(8,128)(2,1)S(1)} %shard_map.117), channel_id=1, source_target_pairs={{32,0},{33,1},{34,2},{35,3},{36,4},{37,5},{38,6},{39,7},{40,8},{41... | collective-permute-start | bytes 442376 | tf_op jit(solution)/shard_map/ppermute | solution.py:78
  17.1 1.9 %collective-permute-start.2 = (bf16[160,384]{1,0:T(8,128)(2,1)S(1)}, bf16[160,384]{1,0:T(8,128)(2,1)S(1)}, u32[]{:S(2)}, u32[]{:S(2)}) collective-permute-start(bf16[160,384]{1,0:T(8,128)(2,1)S(1)} %get-tuple-element.40.refs_0_.own), channel_id=1, source_target_pairs={{32,1},{33,2},{34,3},{35,4},{36,5},{37,6},{38,7},{39,8},{40,9},{41... | collective-permute-start | bytes 368648 | tf_op jit(solution)/shard_map/ppermute | solution.py:78
  19.1 1.9 %collective-permute-start.1 = (bf16[160,384]{1,0:T(8,128)(2,1)S(1)}, bf16[160,384]{1,0:T(8,128)(2,1)S(1)}, u32[]{:S(2)}, u32[]{:S(2)}) collective-permute-start(bf16[160,384]{1,0:T(8,128)(2,1)S(1)} %get-tuple-element.40.refs_0_.own), channel_id=1, source_target_pairs={{0,1},{1,2},{2,3},{3,4},{4,5},{5,6},{6,7},{7,8},{8,9},{9,10},{10,1... | collective-permute-start | bytes 368648 | tf_op jit(solution)/shard_map/ppermute | solution.py:78
  21.0 2.0 %collective-permute-start.8 = (bf16[5,160,96]{2,1,0:T(8,128)(2,1)S(1)}, bf16[5,160,96]{2,1,0:T(8,128)(2,1)S(1)}, u32[]{:S(2)}, u32[]{:S(2)}) collective-permute-start(bf16[5,160,96]{2,1,0:T(8,128)(2,1)S(1)} %get-tuple-element.47), channel_id=1, source_target_pairs={{32,0},{33,1},{34,2},{35,3},{36,4},{37,5},{38,6},{39,7},{40,8},{41... | collective-permute-start | bytes 460808 | tf_op jit(solution)/shard_map/ppermute | solution.py:78
  23.4 5.6 %collective-permute-done.2.rest_1_ = bf16[160,384]{1,0:T(8,128)(2,1)S(1)} collective-permute-done((bf16[160,384]{1,0:T(8,128)(2,1)S(1)}, bf16[160,384]{1,0:T(8,128)(2,1)S(1)}, u32[]{:S(2)}, u32[]{:S(2)}) %collective-permute-start.2) | collective-permute-done | bytes 122912 | tf_op jit(solution)/shard_map/ppermute | solution.py:78
  29.6 1.9 %collective-permute-start.5 = (bf16[160,384]{1,0:T(8,128)(2,1)S(1)}, bf16[160,384]{1,0:T(8,128)(2,1)S(1)}, u32[]{:S(2)}, u32[]{:S(2)}) collective-permute-start(bf16[160,384]{1,0:T(8,128)(2,1)S(1)} %get-tuple-element.43.refs_0_.left), channel_id=1, source_target_pairs={{1,0},{2,1},{3,2},{4,3},{5,4},{6,5},{7,6},{8,7},{9,8},{10,9},{11,1... | collective-permute-start | bytes 368648 | tf_op jit(solution)/shard_map/ppermute | solution.py:78
  31.9 2.1 %collective-permute-done.5.rest_0_.right.refs_1_ = bf16[160,384]{1,0:T(8,128)(2,1)S(1)} collective-permute-done((bf16[160,384]{1,0:T(8,128)(2,1)S(1)}, bf16[160,384]{1,0:T(8,128)(2,1)S(1)}, u32[]{:S(2)}, u32[]{:S(2)}) %collective-permute-start.5) | collective-permute-done | bytes 122912 | tf_op jit(solution)/shard_map/ppermute | solution.py:78
  34.9 5.2 %collective-permute-start.9 = (bf16[192,384]{1,0:T(8,128)(2,1)S(1)}, bf16[192,384]{1,0:T(8,128)(2,1)S(1)}, u32[]{:S(2)}, u32[]{:S(2)}) collective-permute-start(bf16[192,384]{1,0:T(8,128)(2,1)S(1)} %shard_map.122), channel_id=1, source_target_pairs={{0,32},{1,33},{2,34},{3,35},{4,36},{5,37},{6,38},{7,39},{8,40},{9,... | collective-permute-start | bytes 442376 | tf_op jit(solution)/shard_map/ppermute | solution.py:78
  40.0 2.1 %collective-permute-start.7 = (bf16[160,384]{1,0:T(8,128)(2,1)S(1)}, bf16[160,384]{1,0:T(8,128)(2,1)S(1)}, u32[]{:S(2)}, u32[]{:S(2)}) collective-permute-start(bf16[160,384]{1,0:T(8,128)(2,1)S(1)} %get-tuple-element.45.tie.own.refs_0_), channel_id=1, source_target_pairs={{0,33},{1,34},{2,35},{3,36},{4,37},{5,38},{6,39},{7,40},{8,41},{9,... | collective-permute-start | bytes 368648 | tf_op jit(solution)/shard_map/ppermute | solution.py:78
  42.1 1.9 %collective-permute-start.6 = (bf16[160,384]{1,0:T(8,128)(2,1)S(1)}, bf16[160,384]{1,0:T(8,128)(2,1)S(1)}, u32[]{:S(2)}, u32[]{:S(2)}) collective-permute-start(bf16[160,384]{1,0:T(8,128)(2,1)S(1)} %get-tuple-element.45.tie.own.refs_0_), channel_id=1, source_target_pairs={{0,1},{1,2},{2,3},{3,4},{4,5},{5,6},{6,7},{7,8},{8,9},{9,10},{10,1... | collective-permute-start | bytes 368648 | tf_op jit(solution)/shard_map/ppermute | solution.py:78
  44.1 1.0 %shard_map.121 = (bf16[384,384]{1,0:T(8,128)(2,1)S(1)}, bf16[3,128,256]{2,1,0:T(8,128)(2,1)S(1)}, bf16[3,128,256]{2,1,0:T(8,128)(2,1)S(1)}) custom-call(s32[1,1,384]{2,1,0:T(1,128)S(1)} %copy-done.8, bf16[1,1,8,128,256]{4,3,2,1,0:T(8,128)(2,1)} %couple.9, bf16[160,384]{1,0:T(8,128)(2,1)S(1)} %get-tuple-element.45.tie.own.refs_0_), custom_call_target="tpu_custom_call" | custom-call | flops 300000000 | bytes 2000000 | tf_op jit(solution)/shard_map/pallas_call | solution.py:55
  45.5 4.4 %collective-permute-done.7.zb = bf16[160,384]{1,0:T(8,128)(2,1)S(1)} collective-permute-done((bf16[160,384]{1,0:T(8,128)(2,1)S(1)}, bf16[160,384]{1,0:T(8,128)(2,1)S(1)}, u32[]{:S(2)}, u32[]{:S(2)}) %collective-permute-start.7) | collective-permute-done | bytes 122912 | tf_op jit(solution)/shard_map/ppermute | solution.py:78
  49.9 1.8 %collective-permute-done.6.za = bf16[160,384]{1,0:T(8,128)(2,1)S(1)} collective-permute-done((bf16[160,384]{1,0:T(8,128)(2,1)S(1)}, bf16[160,384]{1,0:T(8,128)(2,1)S(1)}, u32[]{:S(2)}, u32[]{:S(2)}) %collective-permute-start.6) | collective-permute-done | bytes 122912 | tf_op jit(solution)/shard_map/ppermute | solution.py:78
  51.6 1.2 %shard_map.124 = (f32[128,384]{1,0:T(8,128)S(1)}, f32[256,384]{1,0:T(8,128)S(1)}, bf16[256,384]{1,0:T(8,128)(2,1)S(1)}) custom-call(s32[1]{0:T(128)} %bitcast.6.me, bf16[384,384]{1,0:T(8,128)(2,1)S(1)} %get-tuple-element.46.pick, bf16[1,1,256,128]{3,2,1,0:T(8,128)(2,1)S(1)} %copy-done.6, bf16[1,1,256,256]{3,2,1,0:T(8,128)(2,1)S(1)} %copy-done.5, ...), custom_call_target="tpu_custom_call" | custom-call | flops 300000000 | bytes 2000000 | tf_op jit(solution)/shard_map/pallas_call | solution.py:55
  52.8 1.3 %collective-permute-start.11 = (bf16[256,384]{1,0:T(8,128)(2,1)S(1)}, bf16[256,384]{1,0:T(8,128)(2,1)S(1)}, u32[]{:S(2)}, u32[]{:S(2)}) collective-permute-start(bf16[256,384]{1,0:T(8,128)(2,1)S(1)} %get-tuple-element.55.z0), channel_id=1, source_target_pairs={{2,1},{4,3},{6,5},{8,7},{10,9},{12,11},{14,13},{16,15},{18,17},{20... | collective-permute-start | bytes 589832 | tf_op jit(solution)/shard_map/ppermute | solution.py:78
  54.1 1.3 %collective-permute-start.10 = (bf16[256,384]{1,0:T(8,128)(2,1)S(1)}, bf16[256,384]{1,0:T(8,128)(2,1)S(1)}, u32[]{:S(2)}, u32[]{:S(2)}) collective-permute-start(bf16[256,384]{1,0:T(8,128)(2,1)S(1)} %get-tuple-element.55.z0), channel_id=1, source_target_pairs={{0,1},{2,3},{4,5},{6,7},{8,9},{10,11},{12,13},{14,15},{16,17},{18,... | collective-permute-start | bytes 589832 | tf_op jit(solution)/shard_map/ppermute | solution.py:78
  55.4 1.3 %collective-permute-start.13 = (bf16[256,384]{1,0:T(8,128)(2,1)S(1)}, bf16[256,384]{1,0:T(8,128)(2,1)S(1)}, u32[]{:S(2)}, u32[]{:S(2)}) collective-permute-start(bf16[256,384]{1,0:T(8,128)(2,1)S(1)} %get-tuple-element.55.z0), channel_id=1, source_target_pairs={{64,32},{66,34},{68,36},{70,38},{72,40},{74,42},{76,44},{78,46},{8... | collective-permute-start | bytes 589832 | tf_op jit(solution)/shard_map/ppermute | solution.py:78
  56.7 1.7 %collective-permute-start.12 = (bf16[256,384]{1,0:T(8,128)(2,1)S(1)}, bf16[256,384]{1,0:T(8,128)(2,1)S(1)}, u32[]{:S(2)}, u32[]{:S(2)}) collective-permute-start(bf16[256,384]{1,0:T(8,128)(2,1)S(1)} %get-tuple-element.55.z0), channel_id=1, source_target_pairs={{0,32},{2,34},{4,36},{6,38},{8,40},{10,42},{12,44},{14,46},{16,48}... | collective-permute-start | bytes 589832 | tf_op jit(solution)/shard_map/ppermute | solution.py:78
  61.6 6.1 %collective-permute-start.20 = (bf16[3,128,256]{2,1,0:T(8,128)(2,1)S(1)}, bf16[3,128,256]{2,1,0:T(8,128)(2,1)S(1)}, u32[]{:S(2)}, u32[]{:S(2)}) collective-permute-start(bf16[3,128,256]{2,1,0:T(8,128)(2,1)S(1)} %get-tuple-element.59), channel_id=1, source_target_pairs={{0,32},{1,33},{2,34},{3,35},{4,36},{5,37},{6,38},{7,39},{8,40},{9,... | collective-permute-start | bytes 589832 | tf_op jit(solution)/shard_map/ppermute | solution.py:78
  67.7 1.3 %collective-permute-start.21 = (bf16[3,128,256]{2,1,0:T(8,128)(2,1)S(1)}, bf16[3,128,256]{2,1,0:T(8,128)(2,1)S(1)}, u32[]{:S(2)}, u32[]{:S(2)}) collective-permute-start(bf16[3,128,256]{2,1,0:T(8,128)(2,1)S(1)} %get-tuple-element.60), channel_id=1, source_target_pairs={{33,1},{35,3},{37,5},{39,7},{41,9},{43,11},{45,13},{47,15},{49,17}... | collective-permute-start | bytes 589832 | tf_op jit(solution)/shard_map/ppermute | solution.py:78
  69.1 1.3 %collective-permute-start.19 = (bf16[256,384]{1,0:T(8,128)(2,1)S(1)}, bf16[256,384]{1,0:T(8,128)(2,1)S(1)}, u32[]{:S(2)}, u32[]{:S(2)}) collective-permute-start(bf16[256,384]{1,0:T(8,128)(2,1)S(1)} %get-tuple-element.58.z2.rest_1_), channel_id=1, source_target_pairs={{1,0},{3,2},{5,4},{7,6},{9,8},{11,10},{13,12},{15,14},{17,16},{19,... | collective-permute-start | bytes 589832 | tf_op jit(solution)/shard_map/ppermute | solution.py:78
  70.4 1.3 %collective-permute-start.18 = (bf16[256,384]{1,0:T(8,128)(2,1)S(1)}, bf16[256,384]{1,0:T(8,128)(2,1)S(1)}, u32[]{:S(2)}, u32[]{:S(2)}) collective-permute-start(bf16[256,384]{1,0:T(8,128)(2,1)S(1)} %get-tuple-element.58.z2.rest_1_), channel_id=1, source_target_pairs={{1,2},{3,4},{5,6},{7,8},{9,10},{11,12},{13,14},{15,16},{17,18},{19... | collective-permute-start | bytes 589832 | tf_op jit(solution)/shard_map/ppermute | solution.py:78
  72.2 1.5 %collective-permute-done.21.below = bf16[3,128,256]{2,1,0:T(8,128)(2,1)S(1)} collective-permute-done((bf16[3,128,256]{2,1,0:T(8,128)(2,1)S(1)}, bf16[3,128,256]{2,1,0:T(8,128)(2,1)S(1)}, u32[]{:S(2)}, u32[]{:S(2)}) %collective-permute-start.21) | collective-permute-done | bytes 196640 | tf_op jit(solution)/shard_map/ppermute | solution.py:78
  75.1 6.0 %collective-permute-done.18.rest_0_.al.rest_3_ = bf16[256,384]{1,0:T(8,128)(2,1)S(1)} collective-permute-done((bf16[256,384]{1,0:T(8,128)(2,1)S(1)}, bf16[256,384]{1,0:T(8,128)(2,1)S(1)}, u32[]{:S(2)}, u32[]{:S(2)}) %collective-permute-start.18) | collective-permute-done | bytes 196640 | tf_op jit(solution)/shard_map/ppermute | solution.py:78
  82.5 1.3 %collective-permute-start.26 = (bf16[128,384]{1,0:T(8,128)(2,1)S(1)}, bf16[128,384]{1,0:T(8,128)(2,1)S(1)}, u32[]{:S(2)}, u32[]{:S(2)}) collective-permute-start(bf16[128,384]{1,0:T(8,128)(2,1)S(1)} %get-tuple-element.67), channel_id=1, source_target_pairs={{32,0},{33,1},{34,2},{35,3},{36,4},{37,5},{38,6},{39,7},{40,8},{41... | collective-permute-start | bytes 294920 | tf_op jit(solution)/shard_map/ppermute | solution.py:78
  83.8 1.3 %collective-permute-start.27 = (bf16[128,384]{1,0:T(8,128)(2,1)S(1)}, bf16[128,384]{1,0:T(8,128)(2,1)S(1)}, u32[]{:S(2)}, u32[]{:S(2)}) collective-permute-start(bf16[128,384]{1,0:T(8,128)(2,1)S(1)} %get-tuple-element.68), channel_id=1, source_target_pairs={{32,64},{33,65},{34,66},{35,67},{36,68},{37,69},{38,70},{39,71},{4... | collective-permute-start | bytes 294920 | tf_op jit(solution)/shard_map/ppermute | solution.py:78
  87.0 15.0 %collective-permute-done.26.a = bf16[128,384]{1,0:T(8,128)(2,1)S(1)} collective-permute-done((bf16[128,384]{1,0:T(8,128)(2,1)S(1)}, bf16[128,384]{1,0:T(8,128)(2,1)S(1)}, u32[]{:S(2)}, u32[]{:S(2)}) %collective-permute-start.26) | collective-permute-done | bytes 98336 | tf_op jit(solution)/shard_map/ppermute | solution.py:78
  (63 shorter events, 13.0 us)
Async XLA Ops:
  0.6 11.2 %copy-start.1 = (bf16[2,2,160,96]{3,2,1,0:T(8,128)(2,1)S(1)}, bf16[2,2,160,96]{3,2,1,0:T(8,128)(2,1)}, u32[]{:S(2)}) copy-start(bf16[2,2,160,96]{3,2,1,0:T(8,128)(2,1)} %interp.20) | copy-start | bytes 368644
  0.6 11.2 %copy-start.7 = (s32[2,2,256]{2,1,0:T(2,128)S(1)}, s32[2,2,256]{2,1,0:T(2,128)}, u32[]{:S(2)}) copy-start(s32[2,2,256]{2,1,0:T(2,128)} %perm.4) | copy-start | bytes 12292
  3.6 11.2 %collective-permute-start.3 = (bf16[5,160,96]{2,1,0:T(8,128)(2,1)S(1)}, bf16[5,160,96]{2,1,0:T(8,128)(2,1)S(1)}, u32[]{:S(2)}, u32[]{:S(2)}) collective-permute-start(bf16[5,160,96]{2,1,0:T(8,128)(2,1)S(1)} %get-tuple-element.42), channel_id=1, source_target_pairs={{0,32},{1,33},{2,34},{3,35},{4,36},{5,37},{6,38},{7,39},{8,40},{9,... | collective-permute-start | bytes 460808 | tf_op jit(solution)/shard_map/ppermute | solution.py:78
  7.5 6.8 %collective-permute-start = (bf16[160,384]{1,0:T(8,128)(2,1)S(1)}, bf16[160,384]{1,0:T(8,128)(2,1)S(1)}, u32[]{:S(2)}, u32[]{:S(2)}) collective-permute-start(bf16[160,384]{1,0:T(8,128)(2,1)S(1)} %get-tuple-element.36.z.tie.left), channel_id=1, source_target_pairs={{1,0},{2,1},{3,2},{4,3},{5,4},{6,5},{7,6},{8,7},{9,8},{10,9},{11,1... | collective-permute-start | bytes 368648 | tf_op jit(solution)/shard_map/ppermute | solution.py:78
  15.1 13.9 %collective-permute-start.4 = (bf16[192,384]{1,0:T(8,128)(2,1)S(1)}, bf16[192,384]{1,0:T(8,128)(2,1)S(1)}, u32[]{:S(2)}, u32[]{:S(2)}) collective-permute-start(bf16[192,384]{1,0:T(8,128)(2,1)S(1)} %shard_map.117), channel_id=1, source_target_pairs={{32,0},{33,1},{34,2},{35,3},{36,4},{37,5},{38,6},{39,7},{40,8},{41... | collective-permute-start | bytes 442376 | tf_op jit(solution)/shard_map/ppermute | solution.py:78
  17.1 11.9 %collective-permute-start.2 = (bf16[160,384]{1,0:T(8,128)(2,1)S(1)}, bf16[160,384]{1,0:T(8,128)(2,1)S(1)}, u32[]{:S(2)}, u32[]{:S(2)}) collective-permute-start(bf16[160,384]{1,0:T(8,128)(2,1)S(1)} %get-tuple-element.40.refs_0_.own), channel_id=1, source_target_pairs={{32,1},{33,2},{34,3},{35,4},{36,5},{37,6},{38,7},{39,8},{40,9},{41... | collective-permute-start | bytes 368648 | tf_op jit(solution)/shard_map/ppermute | solution.py:78
  19.1 10.0 %collective-permute-start.1 = (bf16[160,384]{1,0:T(8,128)(2,1)S(1)}, bf16[160,384]{1,0:T(8,128)(2,1)S(1)}, u32[]{:S(2)}, u32[]{:S(2)}) collective-permute-start(bf16[160,384]{1,0:T(8,128)(2,1)S(1)} %get-tuple-element.40.refs_0_.own), channel_id=1, source_target_pairs={{0,1},{1,2},{2,3},{3,4},{4,5},{5,6},{6,7},{7,8},{8,9},{9,10},{10,1... | collective-permute-start | bytes 368648 | tf_op jit(solution)/shard_map/ppermute | solution.py:78
  21.0 13.5 %collective-permute-start.8 = (bf16[5,160,96]{2,1,0:T(8,128)(2,1)S(1)}, bf16[5,160,96]{2,1,0:T(8,128)(2,1)S(1)}, u32[]{:S(2)}, u32[]{:S(2)}) collective-permute-start(bf16[5,160,96]{2,1,0:T(8,128)(2,1)S(1)} %get-tuple-element.47), channel_id=1, source_target_pairs={{32,0},{33,1},{34,2},{35,3},{36,4},{37,5},{38,6},{39,7},{40,8},{41... | collective-permute-start | bytes 460808 | tf_op jit(solution)/shard_map/ppermute | solution.py:78
  29.6 4.4 %collective-permute-start.5 = (bf16[160,384]{1,0:T(8,128)(2,1)S(1)}, bf16[160,384]{1,0:T(8,128)(2,1)S(1)}, u32[]{:S(2)}, u32[]{:S(2)}) collective-permute-start(bf16[160,384]{1,0:T(8,128)(2,1)S(1)} %get-tuple-element.43.refs_0_.left), channel_id=1, source_target_pairs={{1,0},{2,1},{3,2},{4,3},{5,4},{6,5},{7,6},{8,7},{9,8},{10,9},{11,1... | collective-permute-start | bytes 368648 | tf_op jit(solution)/shard_map/ppermute | solution.py:78
  31.9 12.2 %copy-start.8 = (s32[1,1,384]{2,1,0:T(1,128)S(1)}, s32[1,1,384]{2,1,0:T(1,128)}, u32[]{:S(2)}) copy-start(s32[1,1,384]{2,1,0:T(1,128)} %perm.5) | copy-start | bytes 4612
  34.9 16.8 %collective-permute-start.9 = (bf16[192,384]{1,0:T(8,128)(2,1)S(1)}, bf16[192,384]{1,0:T(8,128)(2,1)S(1)}, u32[]{:S(2)}, u32[]{:S(2)}) collective-permute-start(bf16[192,384]{1,0:T(8,128)(2,1)S(1)} %shard_map.122), channel_id=1, source_target_pairs={{0,32},{1,33},{2,34},{3,35},{4,36},{5,37},{6,38},{7,39},{8,40},{9,... | collective-permute-start | bytes 442376 | tf_op jit(solution)/shard_map/ppermute | solution.py:78
  40.0 9.8 %collective-permute-start.7 = (bf16[160,384]{1,0:T(8,128)(2,1)S(1)}, bf16[160,384]{1,0:T(8,128)(2,1)S(1)}, u32[]{:S(2)}, u32[]{:S(2)}) collective-permute-start(bf16[160,384]{1,0:T(8,128)(2,1)S(1)} %get-tuple-element.45.tie.own.refs_0_), channel_id=1, source_target_pairs={{0,33},{1,34},{2,35},{3,36},{4,37},{5,38},{6,39},{7,40},{8,41},{9,... | collective-permute-start | bytes 368648 | tf_op jit(solution)/shard_map/ppermute | solution.py:78
  42.1 9.5 %collective-permute-start.6 = (bf16[160,384]{1,0:T(8,128)(2,1)S(1)}, bf16[160,384]{1,0:T(8,128)(2,1)S(1)}, u32[]{:S(2)}, u32[]{:S(2)}) collective-permute-start(bf16[160,384]{1,0:T(8,128)(2,1)S(1)} %get-tuple-element.45.tie.own.refs_0_), channel_id=1, source_target_pairs={{0,1},{1,2},{2,3},{3,4},{4,5},{5,6},{6,7},{7,8},{8,9},{9,10},{10,1... | collective-permute-start | bytes 368648 | tf_op jit(solution)/shard_map/ppermute | solution.py:78
  45.5 13.0 %copy-start.2 = (bf16[1,1,8,128,256]{4,3,2,1,0:T(8,128)(2,1)S(1)}, bf16[1,1,8,128,256]{4,3,2,1,0:T(8,128)(2,1)}, u32[]{:S(2)}) copy-start(bf16[1,1,8,128,256]{4,3,2,1,0:T(8,128)(2,1)} %couple.9) | copy-start | bytes 1572868
  52.8 5.6 %collective-permute-start.11 = (bf16[256,384]{1,0:T(8,128)(2,1)S(1)}, bf16[256,384]{1,0:T(8,128)(2,1)S(1)}, u32[]{:S(2)}, u32[]{:S(2)}) collective-permute-start(bf16[256,384]{1,0:T(8,128)(2,1)S(1)} %get-tuple-element.55.z0), channel_id=1, source_target_pairs={{2,1},{4,3},{6,5},{8,7},{10,9},{12,11},{14,13},{16,15},{18,17},{20... | collective-permute-start | bytes 589832 | tf_op jit(solution)/shard_map/ppermute | solution.py:78
  54.1 4.3 %collective-permute-start.10 = (bf16[256,384]{1,0:T(8,128)(2,1)S(1)}, bf16[256,384]{1,0:T(8,128)(2,1)S(1)}, u32[]{:S(2)}, u32[]{:S(2)}) collective-permute-start(bf16[256,384]{1,0:T(8,128)(2,1)S(1)} %get-tuple-element.55.z0), channel_id=1, source_target_pairs={{0,1},{2,3},{4,5},{6,7},{8,9},{10,11},{12,13},{14,15},{16,17},{18,... | collective-permute-start | bytes 589832 | tf_op jit(solution)/shard_map/ppermute | solution.py:78
  55.4 5.2 %collective-permute-start.13 = (bf16[256,384]{1,0:T(8,128)(2,1)S(1)}, bf16[256,384]{1,0:T(8,128)(2,1)S(1)}, u32[]{:S(2)}, u32[]{:S(2)}) collective-permute-start(bf16[256,384]{1,0:T(8,128)(2,1)S(1)} %get-tuple-element.55.z0), channel_id=1, source_target_pairs={{64,32},{66,34},{68,36},{70,38},{72,40},{74,42},{76,44},{78,46},{8... | collective-permute-start | bytes 589832 | tf_op jit(solution)/shard_map/ppermute | solution.py:78
  56.7 4.8 %collective-permute-start.12 = (bf16[256,384]{1,0:T(8,128)(2,1)S(1)}, bf16[256,384]{1,0:T(8,128)(2,1)S(1)}, u32[]{:S(2)}, u32[]{:S(2)}) collective-permute-start(bf16[256,384]{1,0:T(8,128)(2,1)S(1)} %get-tuple-element.55.z0), channel_id=1, source_target_pairs={{0,32},{2,34},{4,36},{6,38},{8,40},{10,42},{12,44},{14,46},{16,48}... | collective-permute-start | bytes 589832 | tf_op jit(solution)/shard_map/ppermute | solution.py:78
  58.5 9.2 %collective-permute-start.17 = (bf16[256,384]{1,0:T(8,128)(2,1)S(1)}, bf16[256,384]{1,0:T(8,128)(2,1)S(1)}, u32[]{:S(2)}, u32[]{:S(2)}) collective-permute-start(bf16[256,384]{1,0:T(8,128)(2,1)S(1)} %get-tuple-element.56.rest_6_.rest_1_.z1), channel_id=1, source_target_pairs={{65,32},{67,34},{69,36},{71,38},{73,40},{75,42},{77,44},{79,46},{8... | collective-permute-start | bytes 589832 | tf_op jit(solution)/shard_map/ppermute | solution.py:78
  59.2 9.9 %collective-permute-start.16 = (bf16[256,384]{1,0:T(8,128)(2,1)S(1)}, bf16[256,384]{1,0:T(8,128)(2,1)S(1)}, u32[]{:S(2)}, u32[]{:S(2)}) collective-permute-start(bf16[256,384]{1,0:T(8,128)(2,1)S(1)} %get-tuple-element.56.rest_6_.rest_1_.z1), channel_id=1, source_target_pairs={{65,34},{67,36},{69,38},{71,40},{73,42},{75,44},{77,46},{79,48},{8... | collective-permute-start | bytes 589832 | tf_op jit(solution)/shard_map/ppermute | solution.py:78
  59.9 9.2 %collective-permute-start.15 = (bf16[256,384]{1,0:T(8,128)(2,1)S(1)}, bf16[256,384]{1,0:T(8,128)(2,1)S(1)}, u32[]{:S(2)}, u32[]{:S(2)}) collective-permute-start(bf16[256,384]{1,0:T(8,128)(2,1)S(1)} %get-tuple-element.56.rest_6_.rest_1_.z1), channel_id=1, source_target_pairs={{1,32},{3,34},{5,36},{7,38},{9,40},{11,42},{13,44},{15,46},{17,48}... | collective-permute-start | bytes 589832 | tf_op jit(solution)/shard_map/ppermute | solution.py:78
  60.7 8.4 %collective-permute-start.14 = (bf16[256,384]{1,0:T(8,128)(2,1)S(1)}, bf16[256,384]{1,0:T(8,128)(2,1)S(1)}, u32[]{:S(2)}, u32[]{:S(2)}) collective-permute-start(bf16[256,384]{1,0:T(8,128)(2,1)S(1)} %get-tuple-element.56.rest_6_.rest_1_.z1), channel_id=1, source_target_pairs={{1,34},{3,36},{5,38},{7,40},{9,42},{11,44},{13,46},{15,48},{17,50}... | collective-permute-start | bytes 589832 | tf_op jit(solution)/shard_map/ppermute | solution.py:78
  61.6 10.6 %collective-permute-start.20 = (bf16[3,128,256]{2,1,0:T(8,128)(2,1)S(1)}, bf16[3,128,256]{2,1,0:T(8,128)(2,1)S(1)}, u32[]{:S(2)}, u32[]{:S(2)}) collective-permute-start(bf16[3,128,256]{2,1,0:T(8,128)(2,1)S(1)} %get-tuple-element.59), channel_id=1, source_target_pairs={{0,32},{1,33},{2,34},{3,35},{4,36},{5,37},{6,38},{7,39},{8,40},{9,... | collective-permute-start | bytes 589832 | tf_op jit(solution)/shard_map/ppermute | solution.py:78
  67.7 6.0 %collective-permute-start.21 = (bf16[3,128,256]{2,1,0:T(8,128)(2,1)S(1)}, bf16[3,128,256]{2,1,0:T(8,128)(2,1)S(1)}, u32[]{:S(2)}, u32[]{:S(2)}) collective-permute-start(bf16[3,128,256]{2,1,0:T(8,128)(2,1)S(1)} %get-tuple-element.60), channel_id=1, source_target_pairs={{33,1},{35,3},{37,5},{39,7},{41,9},{43,11},{45,13},{47,15},{49,17}... | collective-permute-start | bytes 589832 | tf_op jit(solution)/shard_map/ppermute | solution.py:78
  69.1 6.0 %collective-permute-start.19 = (bf16[256,384]{1,0:T(8,128)(2,1)S(1)}, bf16[256,384]{1,0:T(8,128)(2,1)S(1)}, u32[]{:S(2)}, u32[]{:S(2)}) collective-permute-start(bf16[256,384]{1,0:T(8,128)(2,1)S(1)} %get-tuple-element.58.z2.rest_1_), channel_id=1, source_target_pairs={{1,0},{3,2},{5,4},{7,6},{9,8},{11,10},{13,12},{15,14},{17,16},{19,... | collective-permute-start | bytes 589832 | tf_op jit(solution)/shard_map/ppermute | solution.py:78
  70.4 10.6 %collective-permute-start.18 = (bf16[256,384]{1,0:T(8,128)(2,1)S(1)}, bf16[256,384]{1,0:T(8,128)(2,1)S(1)}, u32[]{:S(2)}, u32[]{:S(2)}) collective-permute-start(bf16[256,384]{1,0:T(8,128)(2,1)S(1)} %get-tuple-element.58.z2.rest_1_), channel_id=1, source_target_pairs={{1,2},{3,4},{5,6},{7,8},{9,10},{11,12},{13,14},{15,16},{17,18},{19... | collective-permute-start | bytes 589832 | tf_op jit(solution)/shard_map/ppermute | solution.py:78
  73.7 1.3 %collective-permute-start.22 = (bf16[128,384]{1,0:T(8,128)(2,1)S(1)}, bf16[128,384]{1,0:T(8,128)(2,1)S(1)}, u32[]{:S(2)}, u32[]{:S(2)}) collective-permute-start(bf16[128,384]{1,0:T(8,128)(2,1)S(1)} %get-tuple-element.61), channel_id=1, source_target_pairs={{65,33},{67,35},{69,37},{71,39},{73,41},{75,43},{77,45},{79,47},{8... | collective-permute-start | bytes 294920 | tf_op jit(solution)/shard_map/ppermute | solution.py:78
  74.4 0.7 collective-permute-start.23
  81.1 1.4 %collective-permute-start.25 = (bf16[256,384]{1,0:T(8,128)(2,1)S(1)}, bf16[256,384]{1,0:T(8,128)(2,1)S(1)}, u32[]{:S(2)}, u32[]{:S(2)}) collective-permute-start(bf16[256,384]{1,0:T(8,128)(2,1)S(1)} %get-tuple-element.64.z3.rest_4_), channel_id=1, source_target_pairs={{33,32},{35,34},{37,36},{39,38},{41,40},{43,42},{45,44},{47,46},{4... | collective-permute-start | bytes 589832 | tf_op jit(solution)/shard_map/ppermute | solution.py:78
  81.8 0.7 collective-permute-start.24
  82.5 19.5 %collective-permute-start.26 = (bf16[128,384]{1,0:T(8,128)(2,1)S(1)}, bf16[128,384]{1,0:T(8,128)(2,1)S(1)}, u32[]{:S(2)}, u32[]{:S(2)}) collective-permute-start(bf16[128,384]{1,0:T(8,128)(2,1)S(1)} %get-tuple-element.67), channel_id=1, source_target_pairs={{32,0},{33,1},{34,2},{35,3},{36,4},{37,5},{38,6},{39,7},{40,8},{41... | collective-permute-start | bytes 294920 | tf_op jit(solution)/shard_map/ppermute | solution.py:78
  83.8 18.2 %collective-permute-start.27 = (bf16[128,384]{1,0:T(8,128)(2,1)S(1)}, bf16[128,384]{1,0:T(8,128)(2,1)S(1)}, u32[]{:S(2)}, u32[]{:S(2)}) collective-permute-start(bf16[128,384]{1,0:T(8,128)(2,1)S(1)} %get-tuple-element.68), channel_id=1, source_target_pairs={{32,64},{33,65},{34,66},{35,67},{36,68},{37,69},{38,70},{39,71},{4... | collective-permute-start | bytes 294920 | tf_op jit(solution)/shard_map/ppermute | solution.py:78
  (5 other events, 37.8 us)

commit v6 on v5

--- a/solution.py
+++ b/solution.py
@@ -82,28 +82,32 @@
     return lax.optimization_barrier((x, value))
 
 
-def first_body(rhs, perm, interp, piv, z_out, skel_out, x, p, t, v, sems):
-    jobs = [(rhs.at[0, 0], x), (perm, p), (interp.at[0, 0], t), (piv.at[0, 0], v)]
+def pack_jobs(terms, couple, out):
+    jobs, at = [], 0
+    for (i, j), ks in terms:
+        jobs.append((couple.at[i, j, pl.ds(ks[0], len(ks))], out.at[pl.ds(at, len(ks))]))
+        at += len(ks)
+    return jobs
+
+
+def first_body(rhs, perm, interp, piv, couple, z_out, skel_out, up_out, x, p, t, v, sems):
+    jobs = [(rhs.at[0, 0], x), (perm, p), (interp.at[0, 0], t), (piv.at[0, 0], v), *pack_jobs(UP_TERMS, couple, up_out)]
     copies = [pltpu.make_async_copy(a, b, sems.at[n]) for n, (a, b) in enumerate(jobs)]
     for c in copies:
         c.start()
-    for c in copies:
+    for c in copies[:4]:
         c.wait()
     leaf = reordered(x[...], p[0, 0:1, :], P1)
     skel = leaf[:S1]
     diff = leaf[S1:] - dot(t[...], skel.astype(BF16))
     z_out[...] = dot(v[...], diff.astype(BF16)).astype(BF16)
     skel_out[...] = skel
-
-
-def pack_body(couple, tie, up_out, down_out, sems):
-    jobs = []
-    for terms, out in ((UP_TERMS, up_out), (DOWN_TERMS, down_out)):
-        at = 0
-        for (i, j), ks in terms:
-            jobs.append((couple.at[i, j, pl.ds(ks[0], len(ks))], out.at[pl.ds(at, len(ks))]))
-            at += len(ks)
-    copies = [pltpu.make_async_copy(a, b, sems.at[n]) for n, (a, b) in enumerate(jobs)]
+    for c in copies[4:]:
+        c.wait()
+
+
+def pack_body(couple, tie, down_out, sems):
+    copies = [pltpu.make_async_copy(a, b, sems.at[n]) for n, (a, b) in enumerate(pack_jobs(DOWN_TERMS, couple, down_out))]
     for c in copies:
         c.start()
     for c in copies:
@@ -213,30 +217,22 @@
         body = functools.partial(update_body, own, jobs_of(order, drop), len(order), part)
         return call(body, ins, [LEAF_S])[0]
 
-    z00, skel0 = call(
+    z00, skel0, up_pack = call(
         first_body,
-        [pltpu.with_memory_space_constraint(x, pltpu.HBM) for x in (rhs, perm1, interp1, pivinv1)],
-        [LEAF_Z, ((S1, K), F32)],
-        specs=[HBM] * 4,
+        [pltpu.with_memory_space_constraint(x, pltpu.HBM) for x in (rhs, perm1, interp1, pivinv1, couple1)],
+        [LEAF_Z, ((S1, K), F32), LEAF_W],
+        specs=[HBM] * 5,
         scratch=[
             pltpu.VMEM((P1, K), F32),
             pltpu.VMEM((2, 2, P1), jnp.int32),
             pltpu.VMEM((R1, S1), BF16),
             pltpu.VMEM((R1, R1), BF16),
-            pltpu.SemaphoreType.DMA((4,)),
+            pltpu.SemaphoreType.DMA((6,)),
         ],
     )
     have[(0, here)] = z00
     z00r = have[(0, (0, 1))] = shift(z00, (0, -1))
-    up_pack, down_pack = call(
-        pack_body,
-        [pltpu.with_memory_space_constraint(couple1, pltpu.HBM), z00],
-        [LEAF_W, LEAF_W],
-        specs=[HBM, ANY],
-        scratch=[pltpu.SemaphoreType.DMA((4,))],
-    )
     up_mats = shift(up_pack, (1, 0))
-    down_mats = shift(down_pack, (-1, 0))
     skels, reds = call(spread_body, [rhs, perm1, interp1, couple1, z00, skel0], [LEAF_S, LEAF_R])
     z01, skels = solve(1, {(0, (0, 1))}, skels, reds)
     have[(1, (1, -1))] = shift(z01, (-1, 1))
@@ -245,6 +241,14 @@
     skels = update(1, [(0, (0, 1))], skels, drop=[(1, (0, (0, 1)))])
     z10, skels = solve(2, {(1, (0, -1)), (1, (1, -1))}, skels, reds, arrived=from_below, part=0)
     z10r = have[(2, (0, 1))] = shift(z10, (0, -1))
+    (down_pack,) = call(
+        pack_body,
+        [pltpu.with_memory_space_constraint(couple1, pltpu.HBM), z01],
+        [LEAF_W],
+        specs=[HBM, ANY],
+        scratch=[pltpu.SemaphoreType.DMA((2,))],
+    )
+    down_mats = shift(down_pack, (-1, 0))
     skels = update(2, [(1, (0, -1))], skels, drop=[(2, (1, (0, -1)))], arrived=from_below, part=3)
     z11, skels = solve(3, {(2, (0, 1))}, skels, reds)
     have[(3, (-1, -1))] = shift(z11, (1, 1))

time: 103 us -> 103 us (level)
  transfers between devices with their start and end apart: 28 -> 28, of which waited for: 11 -> 10; matrix products, arithmetic and copies ran while one was open for 1% -> 1% of each run, Pallas kernels for 5% -> 6%
where the time goes in v6:
time: 103 us; the launch traced here: 102 us
  starting transfers between devices  50.8 us (49%)
  waiting for transfers between devices  38 us (37%)
  Pallas kernels  10.9 us (11%)
  between operations  1.25 us (1%)
    ppermute x28, starting transfers between devices, shift(): return lax.ppermute(x, ('bx', 'by'), pairs(*to, colours))  50.8 us
    ppermute x28, waiting for transfers between devices, shift(): return lax.ppermute(x, ('bx', 'by'), pairs(*to, colours))  38 us
    pallas_call x20, Pallas kernels, call(): pl.pallas_call(body, out_shape=[jax.ShapeDtypeStruct(s, d) for s, d in ou...  10.9 us
  transfers between devices with their start and end apart: 28, of which 10 were waited for; matrix products, arithmetic and copies ran while one was open for 1% of the time, Pallas kernels for 6%

profile of v6, /device:TPU:70, one launch (start us, length us, event | category | flops | bytes accessed | tf_op | source)
XLA Modules:
  0.0 101.9 jit_solution(8453070949833647597)
XLA Ops:
  0.7 1.9 %shard_map.112 = (bf16[160,384]{1,0:T(8,128)(2,1)S(1)}, f32[96,384]{1,0:T(8,128)S(1)}, bf16[5,160,96]{2,1,0:T(8,128)(2,1)S(1)}) custom-call(f32[2,2,256,384]{3,2,1,0:T(8,128)} %rhs.3, s32[2,2,256]{2,1,0:T(2,128)} %perm.4, bf16[2,2,160,96]{3,2,1,0:T(8,128)(2,1)} %interp.20, bf16[2,2,160,160]{3,2,1,0:T(8,128)(2,1)} %piv.11, bf16[2,2,8,160,96]{4,3,2,1,0:T(8,128)(2,1)} %bitcast.9), custom_call_target="tpu_custom_call" | custom-call | flops 300000000 | bytes 2000000 | tf_op jit(solution)/shard_map/pallas_call | solution.py:55
  2.6 3.8 %collective-permute-start.3 = (bf16[5,160,96]{2,1,0:T(8,128)(2,1)S(1)}, bf16[5,160,96]{2,1,0:T(8,128)(2,1)S(1)}, u32[]{:S(2)}, u32[]{:S(2)}) collective-permute-start(bf16[5,160,96]{2,1,0:T(8,128)(2,1)S(1)} %get-tuple-element.41), channel_id=1, source_target_pairs={{0,32},{1,33},{2,34},{3,35},{4,36},{5,37},{6,38},{7,39},{8,40},{9,... | collective-permute-start | bytes 460808 | tf_op jit(solution)/shard_map/ppermute | solution.py:78
  6.4 4.3 %collective-permute-start = (bf16[160,384]{1,0:T(8,128)(2,1)S(1)}, bf16[160,384]{1,0:T(8,128)(2,1)S(1)}, u32[]{:S(2)}, u32[]{:S(2)}) collective-permute-start(bf16[160,384]{1,0:T(8,128)(2,1)S(1)} %get-tuple-element.35.z.left), channel_id=1, source_target_pairs={{1,0},{2,1},{3,2},{4,3},{5,4},{6,5},{7,6},{8,7},{9,8},{10,9},{11,1... | collective-permute-start | bytes 368648 | tf_op jit(solution)/shard_map/ppermute | solution.py:78
  11.5 1.6 %collective-permute-done.rest_0_.refs_1_.right = bf16[160,384]{1,0:T(8,128)(2,1)S(1)} collective-permute-done((bf16[160,384]{1,0:T(8,128)(2,1)S(1)}, bf16[160,384]{1,0:T(8,128)(2,1)S(1)}, u32[]{:S(2)}, u32[]{:S(2)}) %collective-permute-start) | collective-permute-done | bytes 122912 | tf_op jit(solution)/shard_map/ppermute | solution.py:78
  14.1 2.2 %collective-permute-start.4 = (bf16[192,384]{1,0:T(8,128)(2,1)S(1)}, bf16[192,384]{1,0:T(8,128)(2,1)S(1)}, u32[]{:S(2)}, u32[]{:S(2)}) collective-permute-start(bf16[192,384]{1,0:T(8,128)(2,1)S(1)} %shard_map.116), channel_id=1, source_target_pairs={{32,0},{33,1},{34,2},{35,3},{36,4},{37,5},{38,6},{39,7},{40,8},{41... | collective-permute-start | bytes 442376 | tf_op jit(solution)/shard_map/ppermute | solution.py:78
  16.2 1.9 %collective-permute-start.2 = (bf16[160,384]{1,0:T(8,128)(2,1)S(1)}, bf16[160,384]{1,0:T(8,128)(2,1)S(1)}, u32[]{:S(2)}, u32[]{:S(2)}) collective-permute-start(bf16[160,384]{1,0:T(8,128)(2,1)S(1)} %get-tuple-element.39.refs_0_.own.tie), channel_id=1, source_target_pairs={{32,1},{33,2},{34,3},{35,4},{36,5},{37,6},{38,7},{39,8},{40,9},{41... | collective-permute-start | bytes 368648 | tf_op jit(solution)/shard_map/ppermute | solution.py:78
  18.2 1.9 %collective-permute-start.1 = (bf16[160,384]{1,0:T(8,128)(2,1)S(1)}, bf16[160,384]{1,0:T(8,128)(2,1)S(1)}, u32[]{:S(2)}, u32[]{:S(2)}) collective-permute-start(bf16[160,384]{1,0:T(8,128)(2,1)S(1)} %get-tuple-element.39.refs_0_.own.tie), channel_id=1, source_target_pairs={{0,1},{1,2},{2,3},{3,4},{4,5},{5,6},{6,7},{7,8},{8,9},{9,10},{10,1... | collective-permute-start | bytes 368648 | tf_op jit(solution)/shard_map/ppermute | solution.py:78
  21.1 2.0 %collective-permute-start.8 = (bf16[5,160,96]{2,1,0:T(8,128)(2,1)S(1)}, bf16[5,160,96]{2,1,0:T(8,128)(2,1)S(1)}, u32[]{:S(2)}, u32[]{:S(2)}) collective-permute-start(bf16[5,160,96]{2,1,0:T(8,128)(2,1)S(1)} %shard_map.121), channel_id=1, source_target_pairs={{32,0},{33,1},{34,2},{35,3},{36,4},{37,5},{38,6},{39,7},{40,8},{41... | collective-permute-start | bytes 460808 | tf_op jit(solution)/shard_map/ppermute | solution.py:78
  23.4 4.7 %collective-permute-done.2.rest_1_ = bf16[160,384]{1,0:T(8,128)(2,1)S(1)} collective-permute-done((bf16[160,384]{1,0:T(8,128)(2,1)S(1)}, bf16[160,384]{1,0:T(8,128)(2,1)S(1)}, u32[]{:S(2)}, u32[]{:S(2)}) %collective-permute-start.2) | collective-permute-done | bytes 122912 | tf_op jit(solution)/shard_map/ppermute | solution.py:78
  28.7 1.9 %collective-permute-start.5 = (bf16[160,384]{1,0:T(8,128)(2,1)S(1)}, bf16[160,384]{1,0:T(8,128)(2,1)S(1)}, u32[]{:S(2)}, u32[]{:S(2)}) collective-permute-start(bf16[160,384]{1,0:T(8,128)(2,1)S(1)} %get-tuple-element.42.refs_0_.left), channel_id=1, source_target_pairs={{1,0},{2,1},{3,2},{4,3},{5,4},{6,5},{7,6},{8,7},{9,8},{10,9},{11,1... | collective-permute-start | bytes 368648 | tf_op jit(solution)/shard_map/ppermute | solution.py:78
  31.0 2.1 %collective-permute-done.5.rest_0_.right.refs_1_ = bf16[160,384]{1,0:T(8,128)(2,1)S(1)} collective-permute-done((bf16[160,384]{1,0:T(8,128)(2,1)S(1)}, bf16[160,384]{1,0:T(8,128)(2,1)S(1)}, u32[]{:S(2)}, u32[]{:S(2)}) %collective-permute-start.5) | collective-permute-done | bytes 122912 | tf_op jit(solution)/shard_map/ppermute | solution.py:78
  33.9 5.2 %collective-permute-start.9 = (bf16[192,384]{1,0:T(8,128)(2,1)S(1)}, bf16[192,384]{1,0:T(8,128)(2,1)S(1)}, u32[]{:S(2)}, u32[]{:S(2)}) collective-permute-start(bf16[192,384]{1,0:T(8,128)(2,1)S(1)} %shard_map.122), channel_id=1, source_target_pairs={{0,32},{1,33},{2,34},{3,35},{4,36},{5,37},{6,38},{7,39},{8,40},{9,... | collective-permute-start | bytes 442376 | tf_op jit(solution)/shard_map/ppermute | solution.py:78
  39.1 2.1 %collective-permute-start.7 = (bf16[160,384]{1,0:T(8,128)(2,1)S(1)}, bf16[160,384]{1,0:T(8,128)(2,1)S(1)}, u32[]{:S(2)}, u32[]{:S(2)}) collective-permute-start(bf16[160,384]{1,0:T(8,128)(2,1)S(1)} %get-tuple-element.44.tie.own.refs_0_), channel_id=1, source_target_pairs={{0,33},{1,34},{2,35},{3,36},{4,37},{5,38},{6,39},{7,40},{8,41},{9,... | collective-permute-start | bytes 368648 | tf_op jit(solution)/shard_map/ppermute | solution.py:78
  41.2 1.9 %collective-permute-start.6 = (bf16[160,384]{1,0:T(8,128)(2,1)S(1)}, bf16[160,384]{1,0:T(8,128)(2,1)S(1)}, u32[]{:S(2)}, u32[]{:S(2)}) collective-permute-start(bf16[160,384]{1,0:T(8,128)(2,1)S(1)} %get-tuple-element.44.tie.own.refs_0_), channel_id=1, source_target_pairs={{0,1},{1,2},{2,3},{3,4},{4,5},{5,6},{6,7},{7,8},{8,9},{9,10},{10,1... | collective-permute-start | bytes 368648 | tf_op jit(solution)/shard_map/ppermute | solution.py:78
  43.2 1.0 %shard_map.120 = (bf16[384,384]{1,0:T(8,128)(2,1)S(1)}, bf16[3,128,256]{2,1,0:T(8,128)(2,1)S(1)}, bf16[3,128,256]{2,1,0:T(8,128)(2,1)S(1)}) custom-call(s32[1,1,384]{2,1,0:T(1,128)S(1)} %copy-done.9, bf16[1,1,8,128,256]{4,3,2,1,0:T(8,128)(2,1)} %couple.9, bf16[160,384]{1,0:T(8,128)(2,1)S(1)} %get-tuple-element.44.tie.own.refs_0_), custom_call_target="tpu_custom_call" | custom-call | flops 300000000 | bytes 2000000 | tf_op jit(solution)/shard_map/pallas_call | solution.py:55
  44.6 4.3 %collective-permute-done.7.zb = bf16[160,384]{1,0:T(8,128)(2,1)S(1)} collective-permute-done((bf16[160,384]{1,0:T(8,128)(2,1)S(1)}, bf16[160,384]{1,0:T(8,128)(2,1)S(1)}, u32[]{:S(2)}, u32[]{:S(2)}) %collective-permute-start.7) | collective-permute-done | bytes 122912 | tf_op jit(solution)/shard_map/ppermute | solution.py:78
  49.0 1.9 %collective-permute-done.6.za = bf16[160,384]{1,0:T(8,128)(2,1)S(1)} collective-permute-done((bf16[160,384]{1,0:T(8,128)(2,1)S(1)}, bf16[160,384]{1,0:T(8,128)(2,1)S(1)}, u32[]{:S(2)}, u32[]{:S(2)}) %collective-permute-start.6) | collective-permute-done | bytes 122912 | tf_op jit(solution)/shard_map/ppermute | solution.py:78
  50.9 1.2 %shard_map.124 = (f32[128,384]{1,0:T(8,128)S(1)}, f32[256,384]{1,0:T(8,128)S(1)}, bf16[256,384]{1,0:T(8,128)(2,1)S(1)}) custom-call(s32[1]{0:T(128)} %bitcast.6.me, bf16[384,384]{1,0:T(8,128)(2,1)S(1)} %get-tuple-element.45.pick, bf16[1,1,256,128]{3,2,1,0:T(8,128)(2,1)S(1)} %copy-done.7, bf16[1,1,256,256]{3,2,1,0:T(8,128)(2,1)S(1)} %copy-done.6, ...), custom_call_target="tpu_custom_call" | custom-call | flops 300000000 | bytes 2000000 | tf_op jit(solution)/shard_map/pallas_call | solution.py:55
  52.1 1.3 %collective-permute-start.11 = (bf16[256,384]{1,0:T(8,128)(2,1)S(1)}, bf16[256,384]{1,0:T(8,128)(2,1)S(1)}, u32[]{:S(2)}, u32[]{:S(2)}) collective-permute-start(bf16[256,384]{1,0:T(8,128)(2,1)S(1)} %get-tuple-element.53.z0), channel_id=1, source_target_pairs={{2,1},{4,3},{6,5},{8,7},{10,9},{12,11},{14,13},{16,15},{18,17},{20... | collective-permute-start | bytes 589832 | tf_op jit(solution)/shard_map/ppermute | solution.py:78
  53.4 1.3 %collective-permute-start.10 = (bf16[256,384]{1,0:T(8,128)(2,1)S(1)}, bf16[256,384]{1,0:T(8,128)(2,1)S(1)}, u32[]{:S(2)}, u32[]{:S(2)}) collective-permute-start(bf16[256,384]{1,0:T(8,128)(2,1)S(1)} %get-tuple-element.53.z0), channel_id=1, source_target_pairs={{0,1},{2,3},{4,5},{6,7},{8,9},{10,11},{12,13},{14,15},{16,17},{18,... | collective-permute-start | bytes 589832 | tf_op jit(solution)/shard_map/ppermute | solution.py:78
  54.7 1.3 %collective-permute-start.13 = (bf16[256,384]{1,0:T(8,128)(2,1)S(1)}, bf16[256,384]{1,0:T(8,128)(2,1)S(1)}, u32[]{:S(2)}, u32[]{:S(2)}) collective-permute-start(bf16[256,384]{1,0:T(8,128)(2,1)S(1)} %get-tuple-element.53.z0), channel_id=1, source_target_pairs={{64,32},{66,34},{68,36},{70,38},{72,40},{74,42},{76,44},{78,46},{8... | collective-permute-start | bytes 589832 | tf_op jit(solution)/shard_map/ppermute | solution.py:78
  56.0 2.0 %collective-permute-start.12 = (bf16[256,384]{1,0:T(8,128)(2,1)S(1)}, bf16[256,384]{1,0:T(8,128)(2,1)S(1)}, u32[]{:S(2)}, u32[]{:S(2)}) collective-permute-start(bf16[256,384]{1,0:T(8,128)(2,1)S(1)} %get-tuple-element.53.z0), channel_id=1, source_target_pairs={{0,32},{2,34},{4,36},{6,38},{8,40},{10,42},{12,44},{14,46},{16,48}... | collective-permute-start | bytes 589832 | tf_op jit(solution)/shard_map/ppermute | solution.py:78
  61.1 5.8 %collective-permute-start.20 = (bf16[3,128,256]{2,1,0:T(8,128)(2,1)S(1)}, bf16[3,128,256]{2,1,0:T(8,128)(2,1)S(1)}, u32[]{:S(2)}, u32[]{:S(2)}) collective-permute-start(bf16[3,128,256]{2,1,0:T(8,128)(2,1)S(1)} %get-tuple-element.57), channel_id=1, source_target_pairs={{0,32},{1,33},{2,34},{3,35},{4,36},{5,37},{6,38},{7,39},{8,40},{9,... | collective-permute-start | bytes 589832 | tf_op jit(solution)/shard_map/ppermute | solution.py:78
  66.9 1.3 %collective-permute-start.21 = (bf16[3,128,256]{2,1,0:T(8,128)(2,1)S(1)}, bf16[3,128,256]{2,1,0:T(8,128)(2,1)S(1)}, u32[]{:S(2)}, u32[]{:S(2)}) collective-permute-start(bf16[3,128,256]{2,1,0:T(8,128)(2,1)S(1)} %get-tuple-element.58), channel_id=1, source_target_pairs={{33,1},{35,3},{37,5},{39,7},{41,9},{43,11},{45,13},{47,15},{49,17}... | collective-permute-start | bytes 589832 | tf_op jit(solution)/shard_map/ppermute | solution.py:78
  68.3 1.3 %collective-permute-start.19 = (bf16[256,384]{1,0:T(8,128)(2,1)S(1)}, bf16[256,384]{1,0:T(8,128)(2,1)S(1)}, u32[]{:S(2)}, u32[]{:S(2)}) collective-permute-start(bf16[256,384]{1,0:T(8,128)(2,1)S(1)} %get-tuple-element.56.z2.rest_1_), channel_id=1, source_target_pairs={{1,0},{3,2},{5,4},{7,6},{9,8},{11,10},{13,12},{15,14},{17,16},{19,... | collective-permute-start | bytes 589832 | tf_op jit(solution)/shard_map/ppermute | solution.py:78
  69.6 1.3 %collective-permute-start.18 = (bf16[256,384]{1,0:T(8,128)(2,1)S(1)}, bf16[256,384]{1,0:T(8,128)(2,1)S(1)}, u32[]{:S(2)}, u32[]{:S(2)}) collective-permute-start(bf16[256,384]{1,0:T(8,128)(2,1)S(1)} %get-tuple-element.56.z2.rest_1_), channel_id=1, source_target_pairs={{1,2},{3,4},{5,6},{7,8},{9,10},{11,12},{13,14},{15,16},{17,18},{19... | collective-permute-start | bytes 589832 | tf_op jit(solution)/shard_map/ppermute | solution.py:78
  71.6 1.7 %collective-permute-done.21.below = bf16[3,128,256]{2,1,0:T(8,128)(2,1)S(1)} collective-permute-done((bf16[3,128,256]{2,1,0:T(8,128)(2,1)S(1)}, bf16[3,128,256]{2,1,0:T(8,128)(2,1)S(1)}, u32[]{:S(2)}, u32[]{:S(2)}) %collective-permute-start.21) | collective-permute-done | bytes 196640 | tf_op jit(solution)/shard_map/ppermute | solution.py:78
  74.7 5.6 %collective-permute-done.18.rest_0_.al.rest_3_ = bf16[256,384]{1,0:T(8,128)(2,1)S(1)} collective-permute-done((bf16[256,384]{1,0:T(8,128)(2,1)S(1)}, bf16[256,384]{1,0:T(8,128)(2,1)S(1)}, u32[]{:S(2)}, u32[]{:S(2)}) %collective-permute-start.18) | collective-permute-done | bytes 196640 | tf_op jit(solution)/shard_map/ppermute | solution.py:78
  81.7 1.3 %collective-permute-start.26 = (bf16[128,384]{1,0:T(8,128)(2,1)S(1)}, bf16[128,384]{1,0:T(8,128)(2,1)S(1)}, u32[]{:S(2)}, u32[]{:S(2)}) collective-permute-start(bf16[128,384]{1,0:T(8,128)(2,1)S(1)} %get-tuple-element.65), channel_id=1, source_target_pairs={{32,0},{33,1},{34,2},{35,3},{36,4},{37,5},{38,6},{39,7},{40,8},{41... | collective-permute-start | bytes 294920 | tf_op jit(solution)/shard_map/ppermute | solution.py:78
  83.0 1.3 %collective-permute-start.27 = (bf16[128,384]{1,0:T(8,128)(2,1)S(1)}, bf16[128,384]{1,0:T(8,128)(2,1)S(1)}, u32[]{:S(2)}, u32[]{:S(2)}) collective-permute-start(bf16[128,384]{1,0:T(8,128)(2,1)S(1)} %get-tuple-element.66), channel_id=1, source_target_pairs={{32,64},{33,65},{34,66},{35,67},{36,68},{37,69},{38,70},{39,71},{4... | collective-permute-start | bytes 294920 | tf_op jit(solution)/shard_map/ppermute | solution.py:78
  85.2 1.0 shard_map.129
  86.2 15.0 %collective-permute-done.26.a = bf16[128,384]{1,0:T(8,128)(2,1)S(1)} collective-permute-done((bf16[128,384]{1,0:T(8,128)(2,1)S(1)}, bf16[128,384]{1,0:T(8,128)(2,1)S(1)}, u32[]{:S(2)}, u32[]{:S(2)}) %collective-permute-start.26) | collective-permute-done | bytes 98336 | tf_op jit(solution)/shard_map/ppermute | solution.py:78
  (65 shorter events, 13.2 us)
Async XLA Ops:
  0.6 10.1 %copy-start = (bf16[2,2,8,96,160]{3,4,2,1,0:T(8,128)(2,1)S(1)}, bf16[2,2,8,96,160]{3,4,2,1,0:T(8,128)(2,1)}, u32[]{:S(2)}) copy-start(bf16[2,2,8,96,160]{3,4,2,1,0:T(8,128)(2,1)} %param.13) | copy-start | bytes 2949124
  0.6 10.1 %copy-start.2 = (bf16[2,2,160,96]{3,2,1,0:T(8,128)(2,1)S(1)}, bf16[2,2,160,96]{3,2,1,0:T(8,128)(2,1)}, u32[]{:S(2)}) copy-start(bf16[2,2,160,96]{3,2,1,0:T(8,128)(2,1)} %interp.20) | copy-start | bytes 368644
  2.6 11.2 %collective-permute-start.3 = (bf16[5,160,96]{2,1,0:T(8,128)(2,1)S(1)}, bf16[5,160,96]{2,1,0:T(8,128)(2,1)S(1)}, u32[]{:S(2)}, u32[]{:S(2)}) collective-permute-start(bf16[5,160,96]{2,1,0:T(8,128)(2,1)S(1)} %get-tuple-element.41), channel_id=1, source_target_pairs={{0,32},{1,33},{2,34},{3,35},{4,36},{5,37},{6,38},{7,39},{8,40},{9,... | collective-permute-start | bytes 460808 | tf_op jit(solution)/shard_map/ppermute | solution.py:78
  6.4 6.8 %collective-permute-start = (bf16[160,384]{1,0:T(8,128)(2,1)S(1)}, bf16[160,384]{1,0:T(8,128)(2,1)S(1)}, u32[]{:S(2)}, u32[]{:S(2)}) collective-permute-start(bf16[160,384]{1,0:T(8,128)(2,1)S(1)} %get-tuple-element.35.z.left), channel_id=1, source_target_pairs={{1,0},{2,1},{3,2},{4,3},{5,4},{6,5},{7,6},{8,7},{9,8},{10,9},{11,1... | collective-permute-start | bytes 368648 | tf_op jit(solution)/shard_map/ppermute | solution.py:78
  14.1 14.0 %collective-permute-start.4 = (bf16[192,384]{1,0:T(8,128)(2,1)S(1)}, bf16[192,384]{1,0:T(8,128)(2,1)S(1)}, u32[]{:S(2)}, u32[]{:S(2)}) collective-permute-start(bf16[192,384]{1,0:T(8,128)(2,1)S(1)} %shard_map.116), channel_id=1, source_target_pairs={{32,0},{33,1},{34,2},{35,3},{36,4},{37,5},{38,6},{39,7},{40,8},{41... | collective-permute-start | bytes 442376 | tf_op jit(solution)/shard_map/ppermute | solution.py:78
  16.2 11.9 %collective-permute-start.2 = (bf16[160,384]{1,0:T(8,128)(2,1)S(1)}, bf16[160,384]{1,0:T(8,128)(2,1)S(1)}, u32[]{:S(2)}, u32[]{:S(2)}) collective-permute-start(bf16[160,384]{1,0:T(8,128)(2,1)S(1)} %get-tuple-element.39.refs_0_.own.tie), channel_id=1, source_target_pairs={{32,1},{33,2},{34,3},{35,4},{36,5},{37,6},{38,7},{39,8},{40,9},{41... | collective-permute-start | bytes 368648 | tf_op jit(solution)/shard_map/ppermute | solution.py:78
  18.2 9.9 %collective-permute-start.1 = (bf16[160,384]{1,0:T(8,128)(2,1)S(1)}, bf16[160,384]{1,0:T(8,128)(2,1)S(1)}, u32[]{:S(2)}, u32[]{:S(2)}) collective-permute-start(bf16[160,384]{1,0:T(8,128)(2,1)S(1)} %get-tuple-element.39.refs_0_.own.tie), channel_id=1, source_target_pairs={{0,1},{1,2},{2,3},{3,4},{4,5},{5,6},{6,7},{7,8},{8,9},{9,10},{10,1... | collective-permute-start | bytes 368648 | tf_op jit(solution)/shard_map/ppermute | solution.py:78
  21.1 12.5 %collective-permute-start.8 = (bf16[5,160,96]{2,1,0:T(8,128)(2,1)S(1)}, bf16[5,160,96]{2,1,0:T(8,128)(2,1)S(1)}, u32[]{:S(2)}, u32[]{:S(2)}) collective-permute-start(bf16[5,160,96]{2,1,0:T(8,128)(2,1)S(1)} %shard_map.121), channel_id=1, source_target_pairs={{32,0},{33,1},{34,2},{35,3},{36,4},{37,5},{38,6},{39,7},{40,8},{41... | collective-permute-start | bytes 460808 | tf_op jit(solution)/shard_map/ppermute | solution.py:78
  28.7 4.4 %collective-permute-start.5 = (bf16[160,384]{1,0:T(8,128)(2,1)S(1)}, bf16[160,384]{1,0:T(8,128)(2,1)S(1)}, u32[]{:S(2)}, u32[]{:S(2)}) collective-permute-start(bf16[160,384]{1,0:T(8,128)(2,1)S(1)} %get-tuple-element.42.refs_0_.left), channel_id=1, source_target_pairs={{1,0},{2,1},{3,2},{4,3},{5,4},{6,5},{7,6},{8,7},{9,8},{10,9},{11,1... | collective-permute-start | bytes 368648 | tf_op jit(solution)/shard_map/ppermute | solution.py:78
  31.0 12.2 %copy-start.9 = (s32[1,1,384]{2,1,0:T(1,128)S(1)}, s32[1,1,384]{2,1,0:T(1,128)}, u32[]{:S(2)}) copy-start(s32[1,1,384]{2,1,0:T(1,128)} %perm.5) | copy-start | bytes 4612
  33.9 16.9 %collective-permute-start.9 = (bf16[192,384]{1,0:T(8,128)(2,1)S(1)}, bf16[192,384]{1,0:T(8,128)(2,1)S(1)}, u32[]{:S(2)}, u32[]{:S(2)}) collective-permute-start(bf16[192,384]{1,0:T(8,128)(2,1)S(1)} %shard_map.122), channel_id=1, source_target_pairs={{0,32},{1,33},{2,34},{3,35},{4,36},{5,37},{6,38},{7,39},{8,40},{9,... | collective-permute-start | bytes 442376 | tf_op jit(solution)/shard_map/ppermute | solution.py:78
  39.1 9.8 %collective-permute-start.7 = (bf16[160,384]{1,0:T(8,128)(2,1)S(1)}, bf16[160,384]{1,0:T(8,128)(2,1)S(1)}, u32[]{:S(2)}, u32[]{:S(2)}) collective-permute-start(bf16[160,384]{1,0:T(8,128)(2,1)S(1)} %get-tuple-element.44.tie.own.refs_0_), channel_id=1, source_target_pairs={{0,33},{1,34},{2,35},{3,36},{4,37},{5,38},{6,39},{7,40},{8,41},{9,... | collective-permute-start | bytes 368648 | tf_op jit(solution)/shard_map/ppermute | solution.py:78
  41.2 9.7 %collective-permute-start.6 = (bf16[160,384]{1,0:T(8,128)(2,1)S(1)}, bf16[160,384]{1,0:T(8,128)(2,1)S(1)}, u32[]{:S(2)}, u32[]{:S(2)}) collective-permute-start(bf16[160,384]{1,0:T(8,128)(2,1)S(1)} %get-tuple-element.44.tie.own.refs_0_), channel_id=1, source_target_pairs={{0,1},{1,2},{2,3},{3,4},{4,5},{5,6},{6,7},{7,8},{8,9},{9,10},{10,1... | collective-permute-start | bytes 368648 | tf_op jit(solution)/shard_map/ppermute | solution.py:78
  44.6 13.4 %copy-start.3 = (bf16[1,1,8,128,256]{4,3,2,1,0:T(8,128)(2,1)S(1)}, bf16[1,1,8,128,256]{4,3,2,1,0:T(8,128)(2,1)}, u32[]{:S(2)}) copy-start(bf16[1,1,8,128,256]{4,3,2,1,0:T(8,128)(2,1)} %couple.9) | copy-start | bytes 1572868
  52.1 5.9 %collective-permute-start.11 = (bf16[256,384]{1,0:T(8,128)(2,1)S(1)}, bf16[256,384]{1,0:T(8,128)(2,1)S(1)}, u32[]{:S(2)}, u32[]{:S(2)}) collective-permute-start(bf16[256,384]{1,0:T(8,128)(2,1)S(1)} %get-tuple-element.53.z0), channel_id=1, source_target_pairs={{2,1},{4,3},{6,5},{8,7},{10,9},{12,11},{14,13},{16,15},{18,17},{20... | collective-permute-start | bytes 589832 | tf_op jit(solution)/shard_map/ppermute | solution.py:78
  53.4 4.6 %collective-permute-start.10 = (bf16[256,384]{1,0:T(8,128)(2,1)S(1)}, bf16[256,384]{1,0:T(8,128)(2,1)S(1)}, u32[]{:S(2)}, u32[]{:S(2)}) collective-permute-start(bf16[256,384]{1,0:T(8,128)(2,1)S(1)} %get-tuple-element.53.z0), channel_id=1, source_target_pairs={{0,1},{2,3},{4,5},{6,7},{8,9},{10,11},{12,13},{14,15},{16,17},{18,... | collective-permute-start | bytes 589832 | tf_op jit(solution)/shard_map/ppermute | solution.py:78
  54.7 5.4 %collective-permute-start.13 = (bf16[256,384]{1,0:T(8,128)(2,1)S(1)}, bf16[256,384]{1,0:T(8,128)(2,1)S(1)}, u32[]{:S(2)}, u32[]{:S(2)}) collective-permute-start(bf16[256,384]{1,0:T(8,128)(2,1)S(1)} %get-tuple-element.53.z0), channel_id=1, source_target_pairs={{64,32},{66,34},{68,36},{70,38},{72,40},{74,42},{76,44},{78,46},{8... | collective-permute-start | bytes 589832 | tf_op jit(solution)/shard_map/ppermute | solution.py:78
  56.0 5.2 %collective-permute-start.12 = (bf16[256,384]{1,0:T(8,128)(2,1)S(1)}, bf16[256,384]{1,0:T(8,128)(2,1)S(1)}, u32[]{:S(2)}, u32[]{:S(2)}) collective-permute-start(bf16[256,384]{1,0:T(8,128)(2,1)S(1)} %get-tuple-element.53.z0), channel_id=1, source_target_pairs={{0,32},{2,34},{4,36},{6,38},{8,40},{10,42},{12,44},{14,46},{16,48}... | collective-permute-start | bytes 589832 | tf_op jit(solution)/shard_map/ppermute | solution.py:78
  58.0 8.9 %collective-permute-start.17 = (bf16[256,384]{1,0:T(8,128)(2,1)S(1)}, bf16[256,384]{1,0:T(8,128)(2,1)S(1)}, u32[]{:S(2)}, u32[]{:S(2)}) collective-permute-start(bf16[256,384]{1,0:T(8,128)(2,1)S(1)} %get-tuple-element.54.rest_6_.rest_1_.z1), channel_id=1, source_target_pairs={{65,32},{67,34},{69,36},{71,38},{73,40},{75,42},{77,44},{79,46},{8... | collective-permute-start | bytes 589832 | tf_op jit(solution)/shard_map/ppermute | solution.py:78
  58.7 9.5 %collective-permute-start.16 = (bf16[256,384]{1,0:T(8,128)(2,1)S(1)}, bf16[256,384]{1,0:T(8,128)(2,1)S(1)}, u32[]{:S(2)}, u32[]{:S(2)}) collective-permute-start(bf16[256,384]{1,0:T(8,128)(2,1)S(1)} %get-tuple-element.54.rest_6_.rest_1_.z1), channel_id=1, source_target_pairs={{65,34},{67,36},{69,38},{71,40},{73,42},{75,44},{77,46},{79,48},{8... | collective-permute-start | bytes 589832 | tf_op jit(solution)/shard_map/ppermute | solution.py:78
  59.4 8.9 %collective-permute-start.15 = (bf16[256,384]{1,0:T(8,128)(2,1)S(1)}, bf16[256,384]{1,0:T(8,128)(2,1)S(1)}, u32[]{:S(2)}, u32[]{:S(2)}) collective-permute-start(bf16[256,384]{1,0:T(8,128)(2,1)S(1)} %get-tuple-element.54.rest_6_.rest_1_.z1), channel_id=1, source_target_pairs={{1,32},{3,34},{5,36},{7,38},{9,40},{11,42},{13,44},{15,46},{17,48}... | collective-permute-start | bytes 589832 | tf_op jit(solution)/shard_map/ppermute | solution.py:78
  60.1 8.2 %collective-permute-start.14 = (bf16[256,384]{1,0:T(8,128)(2,1)S(1)}, bf16[256,384]{1,0:T(8,128)(2,1)S(1)}, u32[]{:S(2)}, u32[]{:S(2)}) collective-permute-start(bf16[256,384]{1,0:T(8,128)(2,1)S(1)} %get-tuple-element.54.rest_6_.rest_1_.z1), channel_id=1, source_target_pairs={{1,34},{3,36},{5,38},{7,40},{9,42},{11,44},{13,46},{15,48},{17,50}... | collective-permute-start | bytes 589832 | tf_op jit(solution)/shard_map/ppermute | solution.py:78
  61.1 10.5 %collective-permute-start.20 = (bf16[3,128,256]{2,1,0:T(8,128)(2,1)S(1)}, bf16[3,128,256]{2,1,0:T(8,128)(2,1)S(1)}, u32[]{:S(2)}, u32[]{:S(2)}) collective-permute-start(bf16[3,128,256]{2,1,0:T(8,128)(2,1)S(1)} %get-tuple-element.57), channel_id=1, source_target_pairs={{0,32},{1,33},{2,34},{3,35},{4,36},{5,37},{6,38},{7,39},{8,40},{9,... | collective-permute-start | bytes 589832 | tf_op jit(solution)/shard_map/ppermute | solution.py:78
  66.9 6.3 %collective-permute-start.21 = (bf16[3,128,256]{2,1,0:T(8,128)(2,1)S(1)}, bf16[3,128,256]{2,1,0:T(8,128)(2,1)S(1)}, u32[]{:S(2)}, u32[]{:S(2)}) collective-permute-start(bf16[3,128,256]{2,1,0:T(8,128)(2,1)S(1)} %get-tuple-element.58), channel_id=1, source_target_pairs={{33,1},{35,3},{37,5},{39,7},{41,9},{43,11},{45,13},{47,15},{49,17}... | collective-permute-start | bytes 589832 | tf_op jit(solution)/shard_map/ppermute | solution.py:78
  68.3 6.3 %collective-permute-start.19 = (bf16[256,384]{1,0:T(8,128)(2,1)S(1)}, bf16[256,384]{1,0:T(8,128)(2,1)S(1)}, u32[]{:S(2)}, u32[]{:S(2)}) collective-permute-start(bf16[256,384]{1,0:T(8,128)(2,1)S(1)} %get-tuple-element.56.z2.rest_1_), channel_id=1, source_target_pairs={{1,0},{3,2},{5,4},{7,6},{9,8},{11,10},{13,12},{15,14},{17,16},{19,... | collective-permute-start | bytes 589832 | tf_op jit(solution)/shard_map/ppermute | solution.py:78
  69.6 10.6 %collective-permute-start.18 = (bf16[256,384]{1,0:T(8,128)(2,1)S(1)}, bf16[256,384]{1,0:T(8,128)(2,1)S(1)}, u32[]{:S(2)}, u32[]{:S(2)}) collective-permute-start(bf16[256,384]{1,0:T(8,128)(2,1)S(1)} %get-tuple-element.56.z2.rest_1_), channel_id=1, source_target_pairs={{1,2},{3,4},{5,6},{7,8},{9,10},{11,12},{13,14},{15,16},{17,18},{19... | collective-permute-start | bytes 589832 | tf_op jit(solution)/shard_map/ppermute | solution.py:78
  73.3 1.3 %collective-permute-start.22 = (bf16[128,384]{1,0:T(8,128)(2,1)S(1)}, bf16[128,384]{1,0:T(8,128)(2,1)S(1)}, u32[]{:S(2)}, u32[]{:S(2)}) collective-permute-start(bf16[128,384]{1,0:T(8,128)(2,1)S(1)} %get-tuple-element.59), channel_id=1, source_target_pairs={{65,33},{67,35},{69,37},{71,39},{73,41},{75,43},{77,45},{79,47},{8... | collective-permute-start | bytes 294920 | tf_op jit(solution)/shard_map/ppermute | solution.py:78
  73.9 0.7 collective-permute-start.23
  80.3 1.4 %collective-permute-start.25 = (bf16[256,384]{1,0:T(8,128)(2,1)S(1)}, bf16[256,384]{1,0:T(8,128)(2,1)S(1)}, u32[]{:S(2)}, u32[]{:S(2)}) collective-permute-start(bf16[256,384]{1,0:T(8,128)(2,1)S(1)} %get-tuple-element.62.z3.rest_4_), channel_id=1, source_target_pairs={{33,32},{35,34},{37,36},{39,38},{41,40},{43,42},{45,44},{47,46},{4... | collective-permute-start | bytes 589832 | tf_op jit(solution)/shard_map/ppermute | solution.py:78
  81.0 0.7 collective-permute-start.24
  81.7 19.5 %collective-permute-start.26 = (bf16[128,384]{1,0:T(8,128)(2,1)S(1)}, bf16[128,384]{1,0:T(8,128)(2,1)S(1)}, u32[]{:S(2)}, u32[]{:S(2)}) collective-permute-start(bf16[128,384]{1,0:T(8,128)(2,1)S(1)} %get-tuple-element.65), channel_id=1, source_target_pairs={{32,0},{33,1},{34,2},{35,3},{36,4},{37,5},{38,6},{39,7},{40,8},{41... | collective-permute-start | bytes 294920 | tf_op jit(solution)/shard_map/ppermute | solution.py:78
  83.0 18.2 %collective-permute-start.27 = (bf16[128,384]{1,0:T(8,128)(2,1)S(1)}, bf16[128,384]{1,0:T(8,128)(2,1)S(1)}, u32[]{:S(2)}, u32[]{:S(2)}) collective-permute-start(bf16[128,384]{1,0:T(8,128)(2,1)S(1)} %get-tuple-element.66), channel_id=1, source_target_pairs={{32,64},{33,65},{34,66},{35,67},{36,68},{37,69},{38,70},{39,71},{4... | collective-permute-start | bytes 294920 | tf_op jit(solution)/shard_map/ppermute | solution.py:78
  (6 other events, 45.3 us)
